TPU v7x, 768 devices: a whole 4x8x12 slice. The times are simulated.
768 devices in a mesh: energy: 32 (over y, z_hi), col: 24 (over z_lo, x, core).
Axes of the slice: x: 4, y: 8, z: 12 (z_hi: 4, z_lo: 3; z = z_hi * 3 + z_lo), core: 2. Of those that a mesh axis runs over, the one named last changes fastest.
Arguments:
- lesser: float32 [512, 2, 72, 1152], P('energy', None, 'col'), may hold values from -6 to 6
- greater_transposed: float32 [512, 2, 72, 1152], P('energy', None, 'col'), may hold values from -6 to 6
- coulomb: bfloat16 [1152, 1152], P('energy', 'col'), may hold values from -0.1875 to 0.1875
Outputs:
- screened: float32 [512, 2, 72, 1152], P('energy', None, 'col')
All inputs are finite; a program needn't handle non-finite values.
Results may differ from a plain program's by a relative error of at most 0.0029.
Values may be sent and summed in bfloat16 or wider, within the bound.
No kernel may reach another device: no remote copies, remote signals or barrier semaphores. Data moves between devices by JAX's collectives and lax.ppermute only.
A program may use at most 64 MiB of HBM per device.

v0:
```python
import functools
import math

import jax
import jax.numpy as jnp
import numpy as np
from jax import lax
from jax.experimental import pallas as pl
from jax.experimental.layout import Layout, with_layout_constraint
from jax.experimental.pallas import tpu as pltpu
from jax.sharding import PartitionSpec as P

LANES = 128
RADIX = 8
HALF = math.sqrt(0.5)
SCALE = 4096.0


def split(x):
    high = x.astype(jnp.bfloat16)
    return high, (x - high.astype(jnp.float32)).astype(jnp.bfloat16)


def turn(re, im, eighths):
    eighths %= 8
    if eighths % 2:
        re, im = (re + im) * HALF, (im - re) * HALF
        eighths -= 1
    return ((re, im), (im, -re), (-re, -im), (-im, re))[eighths // 2]


def pack_kernel(lesser_ref, greater_ref, out_ref):
    energies = out_ref.shape[3]
    stride = lesser_ref.shape[0] // energies
    blocks = stride // 2
    for which, ref in enumerate((lesser_ref, greater_ref)):
        for block in range(blocks):
            for part in range(2):
                out_ref[block, which, part] = ref[pl.ds(block * 2 + part, energies, stride=stride), :]
    out_ref[blocks:] = jnp.zeros_like(out_ref[blocks:])


def correlate_kernel(x_ref, high_ref, low_ref, twiddle_ref, out_ref, total_ref, spread_ref):
    sources, here, lanes = x_ref.shape[0], x_ref.shape[1] // 4, x_ref.shape[2]
    points = high_ref.shape[0] // 2
    pieces = sources * here // points
    per_piece = sources // pieces
    high, low = high_ref[...], low_ref[...]

    def dft(re, im):
        x = jnp.concatenate([re, im], axis=0)
        x_high, x_low = split(x)
        y = jnp.dot(high, x_high, preferred_element_type=jnp.float32)
        y += jnp.dot(high, x_low, preferred_element_type=jnp.float32)
        return y + jnp.dot(low, x_high, preferred_element_type=jnp.float32)

    def piece(which, part, j):
        at = (which * 2 + part) * here
        return x_ref[j * per_piece:(j + 1) * per_piece, at:at + here, :].reshape(points, lanes)

    for r in range(RADIX // 2):
        for other in (r, r + RADIX // 2):
            spread_ref[2 * other] = jnp.broadcast_to(twiddle_ref[:, 2 * other:2 * other + 1], (points, lanes))
            spread_ref[2 * other + 1] = jnp.broadcast_to(twiddle_ref[:, 2 * other + 1:2 * other + 2], (points, lanes))
        sums = []
        for which in range(2):
            terms = []
            for j in range(4):
                re, im = piece(which, 0, j), piece(which, 1, j)
                if which:
                    im = -im
                terms.append(turn(re, im, r * j))
            even = [terms[0][k] + terms[2][k] for k in range(2)]
            odd = [terms[1][k] + terms[3][k] for k in range(2)]
            sums.append(([even[k] + odd[k] for k in range(2)], [even[k] - odd[k] for k in range(2)]))
        mixed = []
        for half, other in enumerate((r, r + RADIX // 2)):
            w_re, w_im = spread_ref[2 * other], spread_ref[2 * other + 1]
            turned = []
            for which in range(2):
                re, im = sums[which][half]
                turned.append((re * w_re - im * w_im, re * w_im + im * w_re))
            y = dft(
                jnp.concatenate([turned[0][0], turned[1][0]], axis=1),
                jnp.concatenate([turned[0][1], turned[1][1]], axis=1),
            )
            l_re, l_im = y[:points, :lanes], y[points:, :lanes]
            g_re, g_im = y[:points, lanes:], y[points:, lanes:]
            mixed.append((l_re * g_re + l_im * g_im, l_re * g_im - l_im * g_re))
        z = dft(
            jnp.concatenate([mixed[0][0], mixed[1][0]], axis=1),
            jnp.concatenate([mixed[0][1], mixed[1][1]], axis=1),
        )
        back = []
        for half, other in enumerate((r, r + RADIX // 2)):
            w_re, w_im = spread_ref[2 * other], spread_ref[2 * other + 1]
            re, im = z[:points, half * lanes:(half + 1) * lanes], z[points:, half * lanes:(half + 1) * lanes]
            back.append((re * w_re - im * w_im, re * w_im + im * w_re))
        both = [back[0][k] + back[1][k] for k in range(2)]
        apart = [back[0][k] - back[1][k] for k in range(2)]
        for j in range(4):
            re, im = turn(*(apart if j % 2 else both), r * j)
            if r == 0:
                total_ref[j, 0] = re
                total_ref[j, 1] = im
            else:
                total_ref[j, 0] += re
                total_ref[j, 1] += im
    energies = sources * here
    factor = -1.0 / (math.sqrt(energies) * 2 * energies * SCALE * SCALE)
    for j in range(pieces):
        for part in range(2):
            value = (total_ref[j, 1 - part] * factor).astype(jnp.bfloat16)
            out_ref[j * per_piece:(j + 1) * per_piece, part * here:(part + 1) * here, :] = value.reshape(
                per_piece, here, lanes
            )


def screen_kernel(polar_ref, coulomb_ref, out_ref):
    order = coulomb_ref.shape[0]
    groups = order // LANES
    here = polar_ref.shape[1] // 2
    stride = out_ref.shape[0] // here
    columns = stride // 2 // groups
    rows = [
        jnp.concatenate([polar_ref[c * groups + k] for k in range(groups)], axis=1) for c in range(columns)
    ]
    product = lax.dot_general(
        jnp.concatenate(rows, axis=0), coulomb_ref[...], (((1,), (1,)), ((), ())), preferred_element_type=jnp.float32
    )
    for c in range(columns):
        for part in range(2):
            at = (c * 2 + part) * here
            for k in range(groups):
                out_ref[pl.ds((c * groups + k) * 2 + part, here, stride=stride), :] = product[
                    at:at + here, k * LANES:(k + 1) * LANES
                ]


def tables(energies):
    points = energies * 2 // RADIX
    angle = np.outer(np.arange(points), np.arange(points)) % points * (2 * np.pi / points)
    cos, sin = np.cos(angle), np.sin(angle)
    whole = np.block([[cos, sin], [-sin, cos]])
    high = whole.astype(jnp.bfloat16)
    low = (whole - high.astype(np.float64)).astype(jnp.bfloat16)
    twiddle = np.zeros((points, LANES), np.float32)
    for r in range(RADIX):
        turned = np.arange(points) * r * (np.pi / energies)
        twiddle[:, 2 * r], twiddle[:, 2 * r + 1] = np.cos(turned), -np.sin(turned)
    return high, low, twiddle


def rows_view(x):
    energies, _, columns, order = x.shape
    x = x.reshape(energies, 2, columns, order // LANES, LANES).transpose(0, 2, 3, 1, 4)
    x = with_layout_constraint(x, Layout(tuple(range(x.ndim))))
    return x.reshape(-1, LANES)


def pack(lesser, greater, owners):
    here = lesser.shape[0]
    return pl.pallas_call(
        pack_kernel,
        out_shape=jax.ShapeDtypeStruct((owners, 2, 2, here, LANES), jnp.float32),
        compiler_params=pltpu.CompilerParams(vmem_limit_bytes=16 << 20),
        name="pack",
    )(rows_view(lesser), rows_view(greater))


def correlate(x):
    owners, _, _, here, lanes = x.shape
    energies = owners * here
    points = energies * 2 // RADIX
    high, low, twiddle = tables(energies)
    return pl.pallas_call(
        correlate_kernel,
        out_shape=jax.ShapeDtypeStruct((owners, 2 * here, lanes), jnp.bfloat16),
        scratch_shapes=[
            pltpu.VMEM((4, 2, points, lanes), jnp.float32),
            pltpu.VMEM((2 * RADIX, points, lanes), jnp.float32),
        ],
        compiler_params=pltpu.CompilerParams(vmem_limit_bytes=24 << 20),
        name="correlate",
    )(x.reshape(owners, 4 * here, lanes), jnp.asarray(high), jnp.asarray(low), jnp.asarray(twiddle))


def screen(polar, coulomb, shape):
    energies, _, columns, order = shape
    out = pl.pallas_call(
        screen_kernel,
        out_shape=jax.ShapeDtypeStruct((energies * columns * order * 2 // LANES, LANES), jnp.float32),
        compiler_params=pltpu.CompilerParams(vmem_limit_bytes=24 << 20),
        name="screen",
    )(polar, coulomb)
    out = out.reshape(energies, columns, order // LANES, 2, LANES).transpose(0, 1, 3, 2, 4)
    return out.reshape(energies, columns, 2, order).transpose(0, 2, 1, 3)


def per_device(lesser, greater_transposed, coulomb):
    owners = lax.axis_size("energy")
    packed = pack(lesser, greater_transposed, owners)
    sent = (packed * SCALE).astype(jnp.float16)
    got = lax.all_to_all(sent, "energy", split_axis=0, concat_axis=0, tiled=True)
    polar = correlate(got.astype(jnp.float32))
    polar = lax.all_to_all(polar, "energy", split_axis=0, concat_axis=0, tiled=True)
    mine = lax.all_gather(coulomb.T, "energy", axis=1, tiled=True)
    coulomb_t = lax.all_gather(mine, "col", axis=0, tiled=True)
    return screen(polar, coulomb_t, lesser.shape)


def solution(mesh):
    placed = (P("energy", None, "col", None), P("energy", None, "col", None), P("energy", "col"))
    return jax.shard_map(
        per_device,
        mesh=mesh,
        in_specs=placed,
        out_specs=P("energy", None, "col", None),
        check_vma=False,
    )
```

profile of v0, /device:TPU:200, one launch (start us, length us, event | category | flops | bytes accessed | tf_op | source)
XLA Modules:
  0.0 234.1 jit_solution(6277151508846655999)
XLA Ops:
  6.5 0.0 all-gather.3.cloned.1.call-start
  6.5 86.9 %all-gather = bf16[32,36,48]{2,1,0:T(8,128)(2,1)S(1)} all-gather(bf16[1,36,48]{2,1,0:T(8,128)(2,1)} %bitcast.25), channel_id=1, replica_groups=mesh['energy'=32,'col'=24] {'energy'}, dimensions={0}, use_global_device_ids=true | all-gather | bytes 114048 | tf_op jit(solution)/shard_map/all_gather | solution.py:207
  93.4 0.1 reshape.35
  93.5 0.8 copy.10
  94.4 0.0 all-gather.3.cloned.1.call-update
  94.4 0.0 copy-start.1
  94.4 1.0 copy-done.1
  95.4 0.0 copy-start.2
  95.4 1.0 copy-done.2
  96.4 0.0 copy-start.3
  96.4 0.0 copy-start.5
  96.4 0.1 pack.1
  96.5 0.1 multiply_convert_fusion
  96.6 31.4 %all_to_all.10 = f16[32,2,2,16,128]{4,3,2,1,0:T(8,128)(2,1)S(1)} all-to-all(f16[32,2,2,16,128]{4,3,2,1,0:T(8,128)(2,1)S(1)} %multiply_convert_fusion), channel_id=1, replica_groups=mesh['energy'=32,'col'=24] {'energy'}, dimensions={0} | all-to-all | bytes 1048576 | tf_op jit(solution)/shard_map/all_to_all | solution.py:204
  128.1 0.1 bitcast_convert_fusion.x_ref
  128.2 0.0 copy-done.3
  128.2 0.0 copy-done.4
  128.2 0.0 copy-done.5
  128.2 2.8 %correlate.1 = bf16[32,32,128]{2,1,0:T(8,128)(2,1)S(1)} custom-call(f32[32,64,128]{2,1,0:T(8,128)S(1)} %bitcast_convert_fusion.x_ref, bf16[256,256]{1,0:T(8,128)(2,1)S(1)} %copy-done.3, bf16[256,256]{1,0:T(8,128)(2,1)S(1)} %copy-done.4, f32[128,128]{1,0:T(8,128)S(1)} %copy-done.5), custom_call_target="tpu_custom_call" | custom-call | tf_op jit(solution)/shard_map/correlate/pallas_call | solution.py:176
  131.0 24.2 %all_to_all.11.polar_ref = bf16[32,32,128]{2,1,0:T(8,128)(2,1)S(1)} all-to-all(bf16[32,32,128]{2,1,0:T(8,128)(2,1)S(1)} %correlate.1), channel_id=1, replica_groups=mesh['energy'=32,'col'=24] {'energy'}, dimensions={0} | all-to-all | bytes 524288 | tf_op jit(solution)/shard_map/all_to_all | solution.py:206
  155.3 68.5 %all-gather.3.cloned.1.call-done.coulomb_ref = bf16[1152,1152]{1,0:T(8,128)(2,1)} async-done(((bf16[48,1152]{1,0:T(8,128)(2,1)}), bf16[1152,1152]{1,0:T(8,128)(2,1)}) %all-gather.3.cloned.1.call-update) | async-done | bytes 2654224 | tf_op jit(solution)/shard_map/all_gather | solution.py:208
  223.8 0.0 copy-start
  223.8 1.7 copy-done
  225.5 1.7 screen.1
  (1 shorter events, 0.0 us)
Async XLA Ops:
  6.5 217.3 %all-gather.3.cloned.1.call-start = ((), (), s32[]{:S(2)}) async-start(), calls=%async_computation.2 | async-start | bytes 2764800 | tf_op jit(solution)/shard_map/all_gather | solution.py:208
  94.4 1.0 copy-start.1
  95.4 1.0 copy-start.2
  96.4 31.8 %copy-start.3 = (bf16[256,256]{1,0:T(8,128)(2,1)S(1)}, bf16[256,256]{1,0:T(8,128)(2,1)}, u32[]{:S(2)}) copy-start(bf16[256,256]{1,0:T(8,128)(2,1)} %constant.8.clone.high_ref) | copy-start | bytes 393220
  96.4 31.8 %copy-start.4 = (bf16[256,256]{1,0:T(8,128)(2,1)S(1)}, bf16[256,256]{1,0:T(8,128)(2,1)}, u32[]{:S(2)}) copy-start(bf16[256,256]{1,0:T(8,128)(2,1)} %constant.9.clone.low_ref) | copy-start | bytes 393220
  96.4 31.8 %copy-start.5 = (f32[128,128]{1,0:T(8,128)S(1)}, f32[128,128]{1,0:T(8,128)}, u32[]{:S(2)}) copy-start(f32[128,128]{1,0:T(8,128)} %constant.10.clone.twiddle_ref) | copy-start | bytes 196612
  223.8 1.7 copy-start
Sparse Core Ops, SparseCore 0:
  94.5 129.2 all-gather.2
where the time goes:
time: 234 us
  blocking collectives  143 us (61%)
  waiting for transfers between devices  68.5 us (29%)
  between operations  13.5 us (6%)
  local copies, waits for them, and re-layouts  4.69 us (2%)
  Pallas kernels  4.55 us (2%)
    all_gather x1, blocking collectives, per_device(): mine = lax.all_gather(coulomb.T, 'energy', axis=1, tiled=True)  86.9 us
    all_gather x1, waiting for transfers between devices, per_device(): coulomb_t = lax.all_gather(mine, 'col', axis=0, tiled=True)  68.5 us
    all_to_all x1, blocking collectives, per_device(): lax.all_to_all(sent, 'energy', split_axis=0, concat_axis=0, tiled=True)  31.4 us
    all_to_all x1, blocking collectives, per_device(): lax.all_to_all(polar, 'energy', split_axis=0, concat_axis=0, tiled=True)  24.2 us
    unnamed x14, local copies, waits for them, and re-layouts  4.69 us
  transfers between devices with their start and end apart: 1, of which 1 were waited for; matrix products, arithmetic and copies ran while one was open for 0% of the time, Pallas kernels for 1%

commit v1 on v0

--- a/solution.py
+++ b/solution.py
@@ -12,7 +12,9 @@
 
 LANES = 128
 RADIX = 8
+RUN, ACROSS, CORES = 3, 4, 2
 HALF = math.sqrt(0.5)
+COULOMB_SCALE = float(2**18)
 SCALE = 4096.0
 
 
@@ -29,19 +31,43 @@
     return ((re, im), (im, -re), (-re, -im), (-im, re))[eighths // 2]
 
 
-def pack_kernel(lesser_ref, greater_ref, out_ref):
-    energies = out_ref.shape[3]
-    stride = lesser_ref.shape[0] // energies
+def pack_kernel(lesser_ref, greater_ref, coulomb_ref, place_ref, out_ref):
+    extra = out_ref.shape[1] // 5
+    here = extra
+    stride = lesser_ref.shape[0] // here
     blocks = stride // 2
     for which, ref in enumerate((lesser_ref, greater_ref)):
         for block in range(blocks):
             for part in range(2):
-                out_ref[block, which, part] = ref[pl.ds(block * 2 + part, energies, stride=stride), :]
-    out_ref[blocks:] = jnp.zeros_like(out_ref[blocks:])
+                at = (which * 2 + part) * here
+                out_ref[block, at:at + here, :] = ref[pl.ds(block * 2 + part, here, stride=stride), :] * SCALE
+    out_ref[blocks:, :4 * here, :] = jnp.zeros_like(out_ref[blocks:, :4 * here, :])
+    block = coulomb_ref[...]
+    total = None
+    for group in range(block.shape[1] // extra):
+        turned = lax.dot_general(
+            block, place_ref[group], (((0,), (0,)), ((), ())), preferred_element_type=jnp.float32
+        )[group * extra:(group + 1) * extra, :]
+        total = turned if total is None else total + turned
+    total = total * COULOMB_SCALE
+    for owner in range(out_ref.shape[0]):
+        out_ref[owner, 4 * here:, :] = total
+
+
+def unpack_kernel(x_ref, out_ref):
+    sources, rows, _ = x_ref.shape
+    extra = rows // 5
+    width = out_ref.shape[1] // sources
+    for group in range(out_ref.shape[0] // extra):
+        pieces = [
+            x_ref[source, 4 * extra:, group * width:(group + 1) * width] for source in range(sources)
+        ]
+        row = jnp.concatenate(pieces, axis=1) * (1.0 / COULOMB_SCALE)
+        out_ref[group * extra:(group + 1) * extra, :] = row.astype(jnp.bfloat16)
 
 
 def correlate_kernel(x_ref, high_ref, low_ref, twiddle_ref, out_ref, total_ref, spread_ref):
-    sources, here, lanes = x_ref.shape[0], x_ref.shape[1] // 4, x_ref.shape[2]
+    sources, here, lanes = x_ref.shape[0], x_ref.shape[1] // 5, x_ref.shape[2]
     points = high_ref.shape[0] // 2
     pieces = sources * here // points
     per_piece = sources // pieces
@@ -116,17 +142,34 @@
             )
 
 
-def screen_kernel(polar_ref, coulomb_ref, out_ref):
-    order = coulomb_ref.shape[0]
+def piece_hops():
+    return [(z, x, core) for core in range(CORES) for x in range(ACROSS) for z in range(RUN)]
+
+
+def source_of(at, hops):
+    z, x, core = lax.div(at, ACROSS * CORES), lax.rem(lax.div(at, CORES), ACROSS), lax.rem(at, CORES)
+    z, x, core = lax.rem(z + hops[0], RUN), lax.rem(x + hops[1], ACROSS), lax.rem(core + hops[2], CORES)
+    return (z * ACROSS + x) * CORES + core
+
+
+def screen_kernel(index_ref, polar_ref, *refs):
+    *pieces, out_ref, coulomb_ref = refs
+    wide, order = pieces[0].shape
     groups = order // LANES
     here = polar_ref.shape[1] // 2
     stride = out_ref.shape[0] // here
     columns = stride // 2 // groups
+    me = index_ref[0]
+    for hops, piece in zip(piece_hops(), pieces):
+        coulomb_ref[source_of(me, hops)] = piece[...]
     rows = [
         jnp.concatenate([polar_ref[c * groups + k] for k in range(groups)], axis=1) for c in range(columns)
     ]
     product = lax.dot_general(
-        jnp.concatenate(rows, axis=0), coulomb_ref[...], (((1,), (1,)), ((), ())), preferred_element_type=jnp.float32
+        jnp.concatenate(rows, axis=0),
+        coulomb_ref[...].reshape(order, order),
+        (((1,), (1,)), ((), ())),
+        preferred_element_type=jnp.float32,
     )
     for c in range(columns):
         for part in range(2):
@@ -158,18 +201,32 @@
     return x.reshape(-1, LANES)
 
 
-def pack(lesser, greater, owners):
+def pack(lesser, greater, coulomb, owners):
     here = lesser.shape[0]
+    rows, wide = coulomb.shape
+    groups = wide // here
+    place = np.zeros((groups, rows, LANES), np.float32)
+    for group in range(groups):
+        place[group, np.arange(rows), group * rows + np.arange(rows)] = 1
     return pl.pallas_call(
         pack_kernel,
-        out_shape=jax.ShapeDtypeStruct((owners, 2, 2, here, LANES), jnp.float32),
+        out_shape=jax.ShapeDtypeStruct((owners, 5 * here, LANES), jnp.float32),
         compiler_params=pltpu.CompilerParams(vmem_limit_bytes=16 << 20),
         name="pack",
-    )(rows_view(lesser), rows_view(greater))
+    )(rows_view(lesser), rows_view(greater), coulomb, jnp.asarray(place, jnp.bfloat16))
+
+
+def unpack(x, wide, order):
+    return pl.pallas_call(
+        unpack_kernel,
+        out_shape=jax.ShapeDtypeStruct((wide, order), jnp.bfloat16),
+        compiler_params=pltpu.CompilerParams(vmem_limit_bytes=16 << 20),
+        name="unpack",
+    )(x)
 
 
 def correlate(x):
-    owners, _, _, here, lanes = x.shape
+    owners, here, lanes = x.shape[0], x.shape[1] // 5, x.shape[2]
     energies = owners * here
     points = energies * 2 // RADIX
     high, low, twiddle = tables(energies)
@@ -182,31 +239,50 @@
         ],
         compiler_params=pltpu.CompilerParams(vmem_limit_bytes=24 << 20),
         name="correlate",
-    )(x.reshape(owners, 4 * here, lanes), jnp.asarray(high), jnp.asarray(low), jnp.asarray(twiddle))
-
-
-def screen(polar, coulomb, shape):
+    )(x, jnp.asarray(high), jnp.asarray(low), jnp.asarray(twiddle))
+
+
+def screen(polar, pieces, index, shape):
     energies, _, columns, order = shape
     out = pl.pallas_call(
         screen_kernel,
         out_shape=jax.ShapeDtypeStruct((energies * columns * order * 2 // LANES, LANES), jnp.float32),
+        in_specs=[pl.BlockSpec(memory_space=pltpu.SMEM)]
+        + [pl.BlockSpec(memory_space=pltpu.VMEM)] * (1 + len(pieces)),
+        out_specs=pl.BlockSpec(memory_space=pltpu.VMEM),
+        scratch_shapes=[pltpu.VMEM((len(pieces),) + pieces[0].shape, jnp.bfloat16)],
         compiler_params=pltpu.CompilerParams(vmem_limit_bytes=24 << 20),
         name="screen",
-    )(polar, coulomb)
+    )(index, polar, *pieces)
     out = out.reshape(energies, columns, order // LANES, 2, LANES).transpose(0, 1, 3, 2, 4)
     return out.reshape(energies, columns, 2, order).transpose(0, 2, 1, 3)
 
 
+def moved(x, sharers, hops):
+    def source(at):
+        z, x, core = at // (ACROSS * CORES), at // CORES % ACROSS, at % CORES
+        z, x, core = (z + hops[0]) % RUN, (x + hops[1]) % ACROSS, (core + hops[2]) % CORES
+        return (z * ACROSS + x) * CORES + core
+
+    return lax.ppermute(x, "col", [(source(at), at) for at in range(sharers)])
+
+
 def per_device(lesser, greater_transposed, coulomb):
     owners = lax.axis_size("energy")
-    packed = pack(lesser, greater_transposed, owners)
-    sent = (packed * SCALE).astype(jnp.float16)
-    got = lax.all_to_all(sent, "energy", split_axis=0, concat_axis=0, tiled=True)
-    polar = correlate(got.astype(jnp.float32))
+    sharers = lax.axis_size("col")
+    order = lesser.shape[3]
+    packed = pack(lesser, greater_transposed, coulomb, owners)
+    got = lax.all_to_all(packed.astype(jnp.float16), "energy", split_axis=0, concat_axis=0, tiled=True)
+    got = got.astype(jnp.float32)
+    pieces = [unpack(got, coulomb.shape[1], order)]
+    for axis, size in enumerate((RUN, ACROSS, CORES)):
+        had = list(pieces)
+        for hop in range(1, size):
+            pieces += [moved(p, sharers, [hop * (axis == k) for k in range(3)]) for p in had]
+    index = jnp.full((1,), lax.axis_index("col"), jnp.int32)
+    polar = correlate(got)
     polar = lax.all_to_all(polar, "energy", split_axis=0, concat_axis=0, tiled=True)
-    mine = lax.all_gather(coulomb.T, "energy", axis=1, tiled=True)
-    coulomb_t = lax.all_gather(mine, "col", axis=0, tiled=True)
-    return screen(polar, coulomb_t, lesser.shape)
+    return screen(polar, pieces, index, lesser.shape)
 
 
 def solution(mesh):

time: 234 us -> 133 us (0.57)
  the two profiles are of different devices: /device:TPU:200 before, /device:TPU:1 now
where the time goes in v1:
time: 133 us; the launch traced here: 132 us
  starting transfers between devices  82.7 us (62%)
  blocking collectives  38.2 us (29%)
  Pallas kernels  5.9 us (4%)
  local copies, waits for them, and re-layouts  3.5 us (3%)
    ppermute x23, starting transfers between devices, moved(): return lax.ppermute(x, 'col', [(source(at), at) for at in range(sharers)])  70.6 us
    all_to_all x1, blocking collectives, per_device(): lax.all_to_all(packed.astype(jnp.float16), 'energy', split_axis=0, concat...  38.2 us
    all_to_all x1, starting transfers between devices, per_device(): lax.all_to_all(polar, 'energy', split_axis=0, concat_axis=0, tiled=True)  12.1 us
    pallas_call x1, Pallas kernels, correlate(): pl.pallas_call(correlate_kernel, out_shape=jax.ShapeDtypeStruct((owners,...  3.52 us
    unnamed x14, local copies, waits for them, and re-layouts  3.5 us
  transfers between devices with their start and end apart: 24, of which 1 were waited for; matrix products, arithmetic and copies ran while one was open for 0% of the time, Pallas kernels for 0%

profile of v1, /device:TPU:1, one launch (start us, length us, event | category | flops | bytes accessed | tf_op | source)
XLA Modules:
  0.0 132.3 jit_solution(251585917007628942)
XLA Ops:
  3.9 38.2 %all_to_all.10 = f16[32,80,128]{2,1,0:T(8,128)(2,1)S(1)} all-to-all(f16[32,80,128]{2,1,0:T(8,128)(2,1)S(1)} %convert_element_type.6), channel_id=1, replica_groups=mesh['energy'=32,'col'=24] {'energy'}, dimensions={0} | all-to-all | bytes 1310720 | tf_op jit(solution)/shard_map/all_to_all | solution.py:275
  42.2 3.5 %correlate.1 = bf16[32,32,128]{2,1,0:T(8,128)(2,1)} custom-call(f32[32,80,128]{2,1,0:T(8,128)S(1)} %convert_element_type.7.x_ref, bf16[256,256]{1,0:T(8,128)(2,1)S(1)} %copy-done.3, bf16[256,256]{1,0:T(8,128)(2,1)S(1)} %copy-done.2, f32[128,128]{1,0:T(8,128)S(1)} %copy-done.4), custom_call_target="tpu_custom_call" | custom-call | tf_op jit(solution)/shard_map/correlate/pallas_call | solution.py:233
  45.7 12.1 %all-to-all-start.1 = ((bf16[32,32,128]{2,1,0:T(8,128)(2,1)}), bf16[32,32,128]{2,1,0:T(8,128)(2,1)S(1)}, u32[]{:S(2)}, u32[]{:S(2)}) async-start(bf16[32,32,128]{2,1,0:T(8,128)(2,1)} %correlate.1), calls=%async_computation.1 | async-start | bytes 524288 | tf_op jit(solution)/shard_map/all_to_all | solution.py:284
  58.2 8.7 %collective-permute-start.11 = (bf16[48,1152]{1,0:T(8,128)(2,1)S(1)}, bf16[48,1152]{1,0:T(8,128)(2,1)S(1)}, u32[]{:S(2)}, u32[]{:S(2)}) collective-permute-start(bf16[48,1152]{1,0:T(8,128)(2,1)S(1)} %unpack.1.refs_0_), channel_id=1, source_target_pairs={{1,0},{0,1},{3,2},{2,3},{5,4},{4,5},{7,6},{6,7},{9,8},{8,9},{11,10... | collective-permute-start | bytes 331784 | tf_op jit(solution)/shard_map/ppermute | solution.py:267
  66.9 2.1 %collective-permute-start.8 = (bf16[48,1152]{1,0:T(8,128)(2,1)S(1)}, bf16[48,1152]{1,0:T(8,128)(2,1)S(1)}, u32[]{:S(2)}, u32[]{:S(2)}) collective-permute-start(bf16[48,1152]{1,0:T(8,128)(2,1)S(1)} %unpack.1.refs_0_), channel_id=1, source_target_pairs={{6,0},{7,1},{0,2},{1,3},{2,4},{3,5},{4,6},{5,7},{14,8},{15,9},{8,1... | collective-permute-start | bytes 331784 | tf_op jit(solution)/shard_map/ppermute | solution.py:267
  69.0 5.4 %collective-permute-start.5 = (bf16[48,1152]{1,0:T(8,128)(2,1)S(1)}, bf16[48,1152]{1,0:T(8,128)(2,1)S(1)}, u32[]{:S(2)}, u32[]{:S(2)}) collective-permute-start(bf16[48,1152]{1,0:T(8,128)(2,1)S(1)} %unpack.1.refs_0_), channel_id=1, source_target_pairs={{4,0},{5,1},{6,2},{7,3},{0,4},{1,5},{2,6},{3,7},{12,8},{13,9},{14,... | collective-permute-start | bytes 331784 | tf_op jit(solution)/shard_map/ppermute | solution.py:267
  74.3 2.1 %collective-permute-start.2 = (bf16[48,1152]{1,0:T(8,128)(2,1)S(1)}, bf16[48,1152]{1,0:T(8,128)(2,1)S(1)}, u32[]{:S(2)}, u32[]{:S(2)}) collective-permute-start(bf16[48,1152]{1,0:T(8,128)(2,1)S(1)} %unpack.1.refs_0_), channel_id=1, source_target_pairs={{2,0},{3,1},{4,2},{5,3},{6,4},{7,5},{0,6},{1,7},{10,8},{11,9},{12,... | collective-permute-start | bytes 331784 | tf_op jit(solution)/shard_map/ppermute | solution.py:267
  76.4 6.0 %collective-permute-start.1 = (bf16[48,1152]{1,0:T(8,128)(2,1)S(1)}, bf16[48,1152]{1,0:T(8,128)(2,1)S(1)}, u32[]{:S(2)}, u32[]{:S(2)}) collective-permute-start(bf16[48,1152]{1,0:T(8,128)(2,1)S(1)} %unpack.1.refs_0_), channel_id=1, source_target_pairs={{16,0},{17,1},{18,2},{19,3},{20,4},{21,5},{22,6},{23,7},{0,8},{1,9... | collective-permute-start | bytes 331784 | tf_op jit(solution)/shard_map/ppermute | solution.py:267
  82.4 1.9 %collective-permute-start = (bf16[48,1152]{1,0:T(8,128)(2,1)S(1)}, bf16[48,1152]{1,0:T(8,128)(2,1)S(1)}, u32[]{:S(2)}, u32[]{:S(2)}) collective-permute-start(bf16[48,1152]{1,0:T(8,128)(2,1)S(1)} %unpack.1.refs_0_), channel_id=1, source_target_pairs={{8,0},{9,1},{10,2},{11,3},{12,4},{13,5},{14,6},{15,7},{16,8},{17,9... | collective-permute-start | bytes 331784 | tf_op jit(solution)/shard_map/ppermute | solution.py:267
  84.4 3.0 %collective-permute-start.20 = (bf16[48,1152]{1,0:T(8,128)(2,1)S(1)}, bf16[48,1152]{1,0:T(8,128)(2,1)S(1)}, u32[]{:S(2)}, u32[]{:S(2)}) collective-permute-start(bf16[48,1152]{1,0:T(8,128)(2,1)S(1)} %collective-permute-done.8.refs_9_), channel_id=1, source_target_pairs={{1,0},{0,1},{3,2},{2,3},{5,4},{4,5},{7,6},{6,7},{9,8},{8,9},{11,10... | collective-permute-start | bytes 331784 | tf_op jit(solution)/shard_map/ppermute | solution.py:267
  87.4 1.9 %collective-permute-start.17 = (bf16[48,1152]{1,0:T(8,128)(2,1)S(1)}, bf16[48,1152]{1,0:T(8,128)(2,1)S(1)}, u32[]{:S(2)}, u32[]{:S(2)}) collective-permute-start(bf16[48,1152]{1,0:T(8,128)(2,1)S(1)} %collective-permute-done.5.refs_6_), channel_id=1, source_target_pairs={{1,0},{0,1},{3,2},{2,3},{5,4},{4,5},{7,6},{6,7},{9,8},{8,9},{11,10... | collective-permute-start | bytes 331784 | tf_op jit(solution)/shard_map/ppermute | solution.py:267
  89.4 2.4 %collective-permute-start.14 = (bf16[48,1152]{1,0:T(8,128)(2,1)S(1)}, bf16[48,1152]{1,0:T(8,128)(2,1)S(1)}, u32[]{:S(2)}, u32[]{:S(2)}) collective-permute-start(bf16[48,1152]{1,0:T(8,128)(2,1)S(1)} %collective-permute-done.2.refs_3_), channel_id=1, source_target_pairs={{1,0},{0,1},{3,2},{2,3},{5,4},{4,5},{7,6},{6,7},{9,8},{8,9},{11,10... | collective-permute-start | bytes 331784 | tf_op jit(solution)/shard_map/ppermute | solution.py:267
  91.8 1.9 %collective-permute-start.13 = (bf16[48,1152]{1,0:T(8,128)(2,1)S(1)}, bf16[48,1152]{1,0:T(8,128)(2,1)S(1)}, u32[]{:S(2)}, u32[]{:S(2)}) collective-permute-start(bf16[48,1152]{1,0:T(8,128)(2,1)S(1)} %collective-permute-done.1.refs_2_), channel_id=1, source_target_pairs={{1,0},{0,1},{3,2},{2,3},{5,4},{4,5},{7,6},{6,7},{9,8},{8,9},{11,10... | collective-permute-start | bytes 331784 | tf_op jit(solution)/shard_map/ppermute | solution.py:267
  93.7 2.2 %collective-permute-start.10 = (bf16[48,1152]{1,0:T(8,128)(2,1)S(1)}, bf16[48,1152]{1,0:T(8,128)(2,1)S(1)}, u32[]{:S(2)}, u32[]{:S(2)}) collective-permute-start(bf16[48,1152]{1,0:T(8,128)(2,1)S(1)} %collective-permute-done.1.refs_2_), channel_id=1, source_target_pairs={{6,0},{7,1},{0,2},{1,3},{2,4},{3,5},{4,6},{5,7},{14,8},{15,9},{8,1... | collective-permute-start | bytes 331784 | tf_op jit(solution)/shard_map/ppermute | solution.py:267
  95.9 2.5 %collective-permute-start.7 = (bf16[48,1152]{1,0:T(8,128)(2,1)S(1)}, bf16[48,1152]{1,0:T(8,128)(2,1)S(1)}, u32[]{:S(2)}, u32[]{:S(2)}) collective-permute-start(bf16[48,1152]{1,0:T(8,128)(2,1)S(1)} %collective-permute-done.1.refs_2_), channel_id=1, source_target_pairs={{4,0},{5,1},{6,2},{7,3},{0,4},{1,5},{2,6},{3,7},{12,8},{13,9},{14,... | collective-permute-start | bytes 331784 | tf_op jit(solution)/shard_map/ppermute | solution.py:267
  98.5 3.7 %collective-permute-start.4 = (bf16[48,1152]{1,0:T(8,128)(2,1)S(1)}, bf16[48,1152]{1,0:T(8,128)(2,1)S(1)}, u32[]{:S(2)}, u32[]{:S(2)}) collective-permute-start(bf16[48,1152]{1,0:T(8,128)(2,1)S(1)} %collective-permute-done.1.refs_2_), channel_id=1, source_target_pairs={{2,0},{3,1},{4,2},{5,3},{6,4},{7,5},{0,6},{1,7},{10,8},{11,9},{12,... | collective-permute-start | bytes 331784 | tf_op jit(solution)/shard_map/ppermute | solution.py:267
  102.2 3.0 %collective-permute-start.12 = (bf16[48,1152]{1,0:T(8,128)(2,1)S(1)}, bf16[48,1152]{1,0:T(8,128)(2,1)S(1)}, u32[]{:S(2)}, u32[]{:S(2)}) collective-permute-start(bf16[48,1152]{1,0:T(8,128)(2,1)S(1)} %collective-permute-done.refs_1_), channel_id=1, source_target_pairs={{1,0},{0,1},{3,2},{2,3},{5,4},{4,5},{7,6},{6,7},{9,8},{8,9},{11,10... | collective-permute-start | bytes 331784 | tf_op jit(solution)/shard_map/ppermute | solution.py:267
  105.2 2.5 %collective-permute-start.9 = (bf16[48,1152]{1,0:T(8,128)(2,1)S(1)}, bf16[48,1152]{1,0:T(8,128)(2,1)S(1)}, u32[]{:S(2)}, u32[]{:S(2)}) collective-permute-start(bf16[48,1152]{1,0:T(8,128)(2,1)S(1)} %collective-permute-done.refs_1_), channel_id=1, source_target_pairs={{6,0},{7,1},{0,2},{1,3},{2,4},{3,5},{4,6},{5,7},{14,8},{15,9},{8,1... | collective-permute-start | bytes 331784 | tf_op jit(solution)/shard_map/ppermute | solution.py:267
  107.7 4.0 %collective-permute-start.6 = (bf16[48,1152]{1,0:T(8,128)(2,1)S(1)}, bf16[48,1152]{1,0:T(8,128)(2,1)S(1)}, u32[]{:S(2)}, u32[]{:S(2)}) collective-permute-start(bf16[48,1152]{1,0:T(8,128)(2,1)S(1)} %collective-permute-done.refs_1_), channel_id=1, source_target_pairs={{4,0},{5,1},{6,2},{7,3},{0,4},{1,5},{2,6},{3,7},{12,8},{13,9},{14,... | collective-permute-start | bytes 331784 | tf_op jit(solution)/shard_map/ppermute | solution.py:267
  111.7 4.0 %collective-permute-start.3 = (bf16[48,1152]{1,0:T(8,128)(2,1)S(1)}, bf16[48,1152]{1,0:T(8,128)(2,1)S(1)}, u32[]{:S(2)}, u32[]{:S(2)}) collective-permute-start(bf16[48,1152]{1,0:T(8,128)(2,1)S(1)} %collective-permute-done.refs_1_), channel_id=1, source_target_pairs={{2,0},{3,1},{4,2},{5,3},{6,4},{7,5},{0,6},{1,7},{10,8},{11,9},{12,... | collective-permute-start | bytes 331784 | tf_op jit(solution)/shard_map/ppermute | solution.py:267
  115.7 2.8 %collective-permute-start.22 = (bf16[48,1152]{1,0:T(8,128)(2,1)S(1)}, bf16[48,1152]{1,0:T(8,128)(2,1)S(1)}, u32[]{:S(2)}, u32[]{:S(2)}) collective-permute-start(bf16[48,1152]{1,0:T(8,128)(2,1)S(1)} %collective-permute-done.10.refs_11_), channel_id=1, source_target_pairs={{1,0},{0,1},{3,2},{2,3},{5,4},{4,5},{7,6},{6,7},{9,8},{8,9},{11,10... | collective-permute-start | bytes 331784 | tf_op jit(solution)/shard_map/ppermute | solution.py:267
  120.4 2.4 %collective-permute-start.16 = (bf16[48,1152]{1,0:T(8,128)(2,1)S(1)}, bf16[48,1152]{1,0:T(8,128)(2,1)S(1)}, u32[]{:S(2)}, u32[]{:S(2)}) collective-permute-start(bf16[48,1152]{1,0:T(8,128)(2,1)S(1)} %collective-permute-done.4.refs_5_), channel_id=1, source_target_pairs={{1,0},{0,1},{3,2},{2,3},{5,4},{4,5},{7,6},{6,7},{9,8},{8,9},{11,10... | collective-permute-start | bytes 331784 | tf_op jit(solution)/shard_map/ppermute | solution.py:267
  122.8 1.9 %collective-permute-start.21 = (bf16[48,1152]{1,0:T(8,128)(2,1)S(1)}, bf16[48,1152]{1,0:T(8,128)(2,1)S(1)}, u32[]{:S(2)}, u32[]{:S(2)}) collective-permute-start(bf16[48,1152]{1,0:T(8,128)(2,1)S(1)} %collective-permute-done.9.refs_10_), channel_id=1, source_target_pairs={{1,0},{0,1},{3,2},{2,3},{5,4},{4,5},{7,6},{6,7},{9,8},{8,9},{11,10... | collective-permute-start | bytes 331784 | tf_op jit(solution)/shard_map/ppermute | solution.py:267
  124.7 2.4 %collective-permute-start.18 = (bf16[48,1152]{1,0:T(8,128)(2,1)S(1)}, bf16[48,1152]{1,0:T(8,128)(2,1)S(1)}, u32[]{:S(2)}, u32[]{:S(2)}) collective-permute-start(bf16[48,1152]{1,0:T(8,128)(2,1)S(1)} %collective-permute-done.6.refs_7_), channel_id=1, source_target_pairs={{1,0},{0,1},{3,2},{2,3},{5,4},{4,5},{7,6},{6,7},{9,8},{8,9},{11,10... | collective-permute-start | bytes 331784 | tf_op jit(solution)/shard_map/ppermute | solution.py:267
  (45 shorter events, 11.2 us)
Async XLA Ops:
  45.7 84.6 %all-to-all-start.1 = ((bf16[32,32,128]{2,1,0:T(8,128)(2,1)}), bf16[32,32,128]{2,1,0:T(8,128)(2,1)S(1)}, u32[]{:S(2)}, u32[]{:S(2)}) async-start(bf16[32,32,128]{2,1,0:T(8,128)(2,1)} %correlate.1), calls=%async_computation.1 | async-start | bytes 524288 | tf_op jit(solution)/shard_map/all_to_all | solution.py:284
  58.2 24.3 %collective-permute-start.11 = (bf16[48,1152]{1,0:T(8,128)(2,1)S(1)}, bf16[48,1152]{1,0:T(8,128)(2,1)S(1)}, u32[]{:S(2)}, u32[]{:S(2)}) collective-permute-start(bf16[48,1152]{1,0:T(8,128)(2,1)S(1)} %unpack.1.refs_0_), channel_id=1, source_target_pairs={{1,0},{0,1},{3,2},{2,3},{5,4},{4,5},{7,6},{6,7},{9,8},{8,9},{11,10... | collective-permute-start | bytes 331784 | tf_op jit(solution)/shard_map/ppermute | solution.py:267
  66.9 17.5 %collective-permute-start.8 = (bf16[48,1152]{1,0:T(8,128)(2,1)S(1)}, bf16[48,1152]{1,0:T(8,128)(2,1)S(1)}, u32[]{:S(2)}, u32[]{:S(2)}) collective-permute-start(bf16[48,1152]{1,0:T(8,128)(2,1)S(1)} %unpack.1.refs_0_), channel_id=1, source_target_pairs={{6,0},{7,1},{0,2},{1,3},{2,4},{3,5},{4,6},{5,7},{14,8},{15,9},{8,1... | collective-permute-start | bytes 331784 | tf_op jit(solution)/shard_map/ppermute | solution.py:267
  69.0 18.4 %collective-permute-start.5 = (bf16[48,1152]{1,0:T(8,128)(2,1)S(1)}, bf16[48,1152]{1,0:T(8,128)(2,1)S(1)}, u32[]{:S(2)}, u32[]{:S(2)}) collective-permute-start(bf16[48,1152]{1,0:T(8,128)(2,1)S(1)} %unpack.1.refs_0_), channel_id=1, source_target_pairs={{4,0},{5,1},{6,2},{7,3},{0,4},{1,5},{2,6},{3,7},{12,8},{13,9},{14,... | collective-permute-start | bytes 331784 | tf_op jit(solution)/shard_map/ppermute | solution.py:267
  74.3 15.0 %collective-permute-start.2 = (bf16[48,1152]{1,0:T(8,128)(2,1)S(1)}, bf16[48,1152]{1,0:T(8,128)(2,1)S(1)}, u32[]{:S(2)}, u32[]{:S(2)}) collective-permute-start(bf16[48,1152]{1,0:T(8,128)(2,1)S(1)} %unpack.1.refs_0_), channel_id=1, source_target_pairs={{2,0},{3,1},{4,2},{5,3},{6,4},{7,5},{0,6},{1,7},{10,8},{11,9},{12,... | collective-permute-start | bytes 331784 | tf_op jit(solution)/shard_map/ppermute | solution.py:267
  76.4 15.4 %collective-permute-start.1 = (bf16[48,1152]{1,0:T(8,128)(2,1)S(1)}, bf16[48,1152]{1,0:T(8,128)(2,1)S(1)}, u32[]{:S(2)}, u32[]{:S(2)}) collective-permute-start(bf16[48,1152]{1,0:T(8,128)(2,1)S(1)} %unpack.1.refs_0_), channel_id=1, source_target_pairs={{16,0},{17,1},{18,2},{19,3},{20,4},{21,5},{22,6},{23,7},{0,8},{1,9... | collective-permute-start | bytes 331784 | tf_op jit(solution)/shard_map/ppermute | solution.py:267
  82.4 11.3 %collective-permute-start = (bf16[48,1152]{1,0:T(8,128)(2,1)S(1)}, bf16[48,1152]{1,0:T(8,128)(2,1)S(1)}, u32[]{:S(2)}, u32[]{:S(2)}) collective-permute-start(bf16[48,1152]{1,0:T(8,128)(2,1)S(1)} %unpack.1.refs_0_), channel_id=1, source_target_pairs={{8,0},{9,1},{10,2},{11,3},{12,4},{13,5},{14,6},{15,7},{16,8},{17,9... | collective-permute-start | bytes 331784 | tf_op jit(solution)/shard_map/ppermute | solution.py:267
  84.4 11.6 %collective-permute-start.20 = (bf16[48,1152]{1,0:T(8,128)(2,1)S(1)}, bf16[48,1152]{1,0:T(8,128)(2,1)S(1)}, u32[]{:S(2)}, u32[]{:S(2)}) collective-permute-start(bf16[48,1152]{1,0:T(8,128)(2,1)S(1)} %collective-permute-done.8.refs_9_), channel_id=1, source_target_pairs={{1,0},{0,1},{3,2},{2,3},{5,4},{4,5},{7,6},{6,7},{9,8},{8,9},{11,10... | collective-permute-start | bytes 331784 | tf_op jit(solution)/shard_map/ppermute | solution.py:267
  87.4 11.1 %collective-permute-start.17 = (bf16[48,1152]{1,0:T(8,128)(2,1)S(1)}, bf16[48,1152]{1,0:T(8,128)(2,1)S(1)}, u32[]{:S(2)}, u32[]{:S(2)}) collective-permute-start(bf16[48,1152]{1,0:T(8,128)(2,1)S(1)} %collective-permute-done.5.refs_6_), channel_id=1, source_target_pairs={{1,0},{0,1},{3,2},{2,3},{5,4},{4,5},{7,6},{6,7},{9,8},{8,9},{11,10... | collective-permute-start | bytes 331784 | tf_op jit(solution)/shard_map/ppermute | solution.py:267
  89.4 12.8 %collective-permute-start.14 = (bf16[48,1152]{1,0:T(8,128)(2,1)S(1)}, bf16[48,1152]{1,0:T(8,128)(2,1)S(1)}, u32[]{:S(2)}, u32[]{:S(2)}) collective-permute-start(bf16[48,1152]{1,0:T(8,128)(2,1)S(1)} %collective-permute-done.2.refs_3_), channel_id=1, source_target_pairs={{1,0},{0,1},{3,2},{2,3},{5,4},{4,5},{7,6},{6,7},{9,8},{8,9},{11,10... | collective-permute-start | bytes 331784 | tf_op jit(solution)/shard_map/ppermute | solution.py:267
  91.8 13.4 %collective-permute-start.13 = (bf16[48,1152]{1,0:T(8,128)(2,1)S(1)}, bf16[48,1152]{1,0:T(8,128)(2,1)S(1)}, u32[]{:S(2)}, u32[]{:S(2)}) collective-permute-start(bf16[48,1152]{1,0:T(8,128)(2,1)S(1)} %collective-permute-done.1.refs_2_), channel_id=1, source_target_pairs={{1,0},{0,1},{3,2},{2,3},{5,4},{4,5},{7,6},{6,7},{9,8},{8,9},{11,10... | collective-permute-start | bytes 331784 | tf_op jit(solution)/shard_map/ppermute | solution.py:267
  93.7 13.9 %collective-permute-start.10 = (bf16[48,1152]{1,0:T(8,128)(2,1)S(1)}, bf16[48,1152]{1,0:T(8,128)(2,1)S(1)}, u32[]{:S(2)}, u32[]{:S(2)}) collective-permute-start(bf16[48,1152]{1,0:T(8,128)(2,1)S(1)} %collective-permute-done.1.refs_2_), channel_id=1, source_target_pairs={{6,0},{7,1},{0,2},{1,3},{2,4},{3,5},{4,6},{5,7},{14,8},{15,9},{8,1... | collective-permute-start | bytes 331784 | tf_op jit(solution)/shard_map/ppermute | solution.py:267
  95.9 15.7 %collective-permute-start.7 = (bf16[48,1152]{1,0:T(8,128)(2,1)S(1)}, bf16[48,1152]{1,0:T(8,128)(2,1)S(1)}, u32[]{:S(2)}, u32[]{:S(2)}) collective-permute-start(bf16[48,1152]{1,0:T(8,128)(2,1)S(1)} %collective-permute-done.1.refs_2_), channel_id=1, source_target_pairs={{4,0},{5,1},{6,2},{7,3},{0,4},{1,5},{2,6},{3,7},{12,8},{13,9},{14,... | collective-permute-start | bytes 331784 | tf_op jit(solution)/shard_map/ppermute | solution.py:267
  98.5 17.2 %collective-permute-start.4 = (bf16[48,1152]{1,0:T(8,128)(2,1)S(1)}, bf16[48,1152]{1,0:T(8,128)(2,1)S(1)}, u32[]{:S(2)}, u32[]{:S(2)}) collective-permute-start(bf16[48,1152]{1,0:T(8,128)(2,1)S(1)} %collective-permute-done.1.refs_2_), channel_id=1, source_target_pairs={{2,0},{3,1},{4,2},{5,3},{6,4},{7,5},{0,6},{1,7},{10,8},{11,9},{12,... | collective-permute-start | bytes 331784 | tf_op jit(solution)/shard_map/ppermute | solution.py:267
  102.2 16.2 %collective-permute-start.12 = (bf16[48,1152]{1,0:T(8,128)(2,1)S(1)}, bf16[48,1152]{1,0:T(8,128)(2,1)S(1)}, u32[]{:S(2)}, u32[]{:S(2)}) collective-permute-start(bf16[48,1152]{1,0:T(8,128)(2,1)S(1)} %collective-permute-done.refs_1_), channel_id=1, source_target_pairs={{1,0},{0,1},{3,2},{2,3},{5,4},{4,5},{7,6},{6,7},{9,8},{8,9},{11,10... | collective-permute-start | bytes 331784 | tf_op jit(solution)/shard_map/ppermute | solution.py:267
  105.2 15.2 %collective-permute-start.9 = (bf16[48,1152]{1,0:T(8,128)(2,1)S(1)}, bf16[48,1152]{1,0:T(8,128)(2,1)S(1)}, u32[]{:S(2)}, u32[]{:S(2)}) collective-permute-start(bf16[48,1152]{1,0:T(8,128)(2,1)S(1)} %collective-permute-done.refs_1_), channel_id=1, source_target_pairs={{6,0},{7,1},{0,2},{1,3},{2,4},{3,5},{4,6},{5,7},{14,8},{15,9},{8,1... | collective-permute-start | bytes 331784 | tf_op jit(solution)/shard_map/ppermute | solution.py:267
  107.7 15.1 %collective-permute-start.6 = (bf16[48,1152]{1,0:T(8,128)(2,1)S(1)}, bf16[48,1152]{1,0:T(8,128)(2,1)S(1)}, u32[]{:S(2)}, u32[]{:S(2)}) collective-permute-start(bf16[48,1152]{1,0:T(8,128)(2,1)S(1)} %collective-permute-done.refs_1_), channel_id=1, source_target_pairs={{4,0},{5,1},{6,2},{7,3},{0,4},{1,5},{2,6},{3,7},{12,8},{13,9},{14,... | collective-permute-start | bytes 331784 | tf_op jit(solution)/shard_map/ppermute | solution.py:267
  111.7 13.1 %collective-permute-start.3 = (bf16[48,1152]{1,0:T(8,128)(2,1)S(1)}, bf16[48,1152]{1,0:T(8,128)(2,1)S(1)}, u32[]{:S(2)}, u32[]{:S(2)}) collective-permute-start(bf16[48,1152]{1,0:T(8,128)(2,1)S(1)} %collective-permute-done.refs_1_), channel_id=1, source_target_pairs={{2,0},{3,1},{4,2},{5,3},{6,4},{7,5},{0,6},{1,7},{10,8},{11,9},{12,... | collective-permute-start | bytes 331784 | tf_op jit(solution)/shard_map/ppermute | solution.py:267
  115.7 11.5 %collective-permute-start.22 = (bf16[48,1152]{1,0:T(8,128)(2,1)S(1)}, bf16[48,1152]{1,0:T(8,128)(2,1)S(1)}, u32[]{:S(2)}, u32[]{:S(2)}) collective-permute-start(bf16[48,1152]{1,0:T(8,128)(2,1)S(1)} %collective-permute-done.10.refs_11_), channel_id=1, source_target_pairs={{1,0},{0,1},{3,2},{2,3},{5,4},{4,5},{7,6},{6,7},{9,8},{8,9},{11,10... | collective-permute-start | bytes 331784 | tf_op jit(solution)/shard_map/ppermute | solution.py:267
  118.4 10.7 %collective-permute-start.19 = (bf16[48,1152]{1,0:T(8,128)(2,1)S(1)}, bf16[48,1152]{1,0:T(8,128)(2,1)S(1)}, u32[]{:S(2)}, u32[]{:S(2)}) collective-permute-start(bf16[48,1152]{1,0:T(8,128)(2,1)S(1)} %collective-permute-done.7.refs_8_), channel_id=1, source_target_pairs={{1,0},{0,1},{3,2},{2,3},{5,4},{4,5},{7,6},{6,7},{9,8},{8,9},{11,10... | collective-permute-start | bytes 331784 | tf_op jit(solution)/shard_map/ppermute | solution.py:267
  120.4 8.7 %collective-permute-start.16 = (bf16[48,1152]{1,0:T(8,128)(2,1)S(1)}, bf16[48,1152]{1,0:T(8,128)(2,1)S(1)}, u32[]{:S(2)}, u32[]{:S(2)}) collective-permute-start(bf16[48,1152]{1,0:T(8,128)(2,1)S(1)} %collective-permute-done.4.refs_5_), channel_id=1, source_target_pairs={{1,0},{0,1},{3,2},{2,3},{5,4},{4,5},{7,6},{6,7},{9,8},{8,9},{11,10... | collective-permute-start | bytes 331784 | tf_op jit(solution)/shard_map/ppermute | solution.py:267
  122.8 6.3 %collective-permute-start.21 = (bf16[48,1152]{1,0:T(8,128)(2,1)S(1)}, bf16[48,1152]{1,0:T(8,128)(2,1)S(1)}, u32[]{:S(2)}, u32[]{:S(2)}) collective-permute-start(bf16[48,1152]{1,0:T(8,128)(2,1)S(1)} %collective-permute-done.9.refs_10_), channel_id=1, source_target_pairs={{1,0},{0,1},{3,2},{2,3},{5,4},{4,5},{7,6},{6,7},{9,8},{8,9},{11,10... | collective-permute-start | bytes 331784 | tf_op jit(solution)/shard_map/ppermute | solution.py:267
  124.7 4.4 %collective-permute-start.18 = (bf16[48,1152]{1,0:T(8,128)(2,1)S(1)}, bf16[48,1152]{1,0:T(8,128)(2,1)S(1)}, u32[]{:S(2)}, u32[]{:S(2)}) collective-permute-start(bf16[48,1152]{1,0:T(8,128)(2,1)S(1)} %collective-permute-done.6.refs_7_), channel_id=1, source_target_pairs={{1,0},{0,1},{3,2},{2,3},{5,4},{4,5},{7,6},{6,7},{9,8},{8,9},{11,10... | collective-permute-start | bytes 331784 | tf_op jit(solution)/shard_map/ppermute | solution.py:267
  127.2 3.2 %collective-permute-start.15 = (bf16[48,1152]{1,0:T(8,128)(2,1)S(1)}, bf16[48,1152]{1,0:T(8,128)(2,1)S(1)}, u32[]{:S(2)}, u32[]{:S(2)}) collective-permute-start(bf16[48,1152]{1,0:T(8,128)(2,1)S(1)} %collective-permute-done.3.refs_4_), channel_id=1, source_target_pairs={{1,0},{0,1},{3,2},{2,3},{5,4},{4,5},{7,6},{6,7},{9,8},{8,9},{11,10... | collective-permute-start | bytes 331784 | tf_op jit(solution)/shard_map/ppermute | solution.py:267
  (7 other events, 118.6 us)

commit v2 on v1

--- a/solution.py
+++ b/solution.py
@@ -13,6 +13,7 @@
 LANES = 128
 RADIX = 8
 RUN, ACROSS, CORES = 3, 4, 2
+HOPS = (0, 2, 1, 3)
 HALF = math.sqrt(0.5)
 COULOMB_SCALE = float(2**18)
 SCALE = 4096.0
@@ -31,25 +32,36 @@
     return ((re, im), (im, -re), (-re, -im), (-im, re))[eighths // 2]
 
 
-def pack_kernel(lesser_ref, greater_ref, coulomb_ref, place_ref, out_ref):
-    extra = out_ref.shape[1] // 5
-    here = extra
+def pack_kernel(lesser_hbm, greater_hbm, coulomb_hbm, out_ref, lesser_ref, greater_ref, coulomb_ref, sems):
+    copies = [
+        pltpu.make_async_copy(source, target, sems.at[i])
+        for i, (source, target) in enumerate(
+            ((lesser_hbm, lesser_ref), (greater_hbm, greater_ref), (coulomb_hbm, coulomb_ref))
+        )
+    ]
+    for copy in copies:
+        copy.start()
+    here = out_ref.shape[1] // 5
     stride = lesser_ref.shape[0] // here
     blocks = stride // 2
+    out_ref[blocks:, :4 * here, :] = jnp.zeros_like(out_ref[blocks:, :4 * here, :])
     for which, ref in enumerate((lesser_ref, greater_ref)):
+        copies[which].wait()
         for block in range(blocks):
             for part in range(2):
                 at = (which * 2 + part) * here
                 out_ref[block, at:at + here, :] = ref[pl.ds(block * 2 + part, here, stride=stride), :] * SCALE
-    out_ref[blocks:, :4 * here, :] = jnp.zeros_like(out_ref[blocks:, :4 * here, :])
+    copies[2].wait()
     block = coulomb_ref[...]
+    rows, wide = block.shape
+    row = lax.broadcasted_iota(jnp.int32, (rows, LANES), 0)
+    lane = lax.broadcasted_iota(jnp.int32, (rows, LANES), 1)
     total = None
-    for group in range(block.shape[1] // extra):
-        turned = lax.dot_general(
-            block, place_ref[group], (((0,), (0,)), ((), ())), preferred_element_type=jnp.float32
-        )[group * extra:(group + 1) * extra, :]
+    for group in range(wide // here):
+        place = jnp.where(lane == row + group * rows, COULOMB_SCALE, 0.0).astype(jnp.bfloat16)
+        turned = lax.dot_general(block, place, (((0,), (0,)), ((), ())), preferred_element_type=jnp.float32)
+        turned = turned[group * here:(group + 1) * here, :]
         total = turned if total is None else total + turned
-    total = total * COULOMB_SCALE
     for owner in range(out_ref.shape[0]):
         out_ref[owner, 4 * here:, :] = total
 
@@ -142,26 +154,20 @@
             )
 
 
-def piece_hops():
-    return [(z, x, core) for core in range(CORES) for x in range(ACROSS) for z in range(RUN)]
-
-
-def source_of(at, hops):
-    z, x, core = lax.div(at, ACROSS * CORES), lax.rem(lax.div(at, CORES), ACROSS), lax.rem(at, CORES)
-    z, x, core = lax.rem(z + hops[0], RUN), lax.rem(x + hops[1], ACROSS), lax.rem(core + hops[2], CORES)
-    return (z * ACROSS + x) * CORES + core
-
-
-def screen_kernel(index_ref, polar_ref, *refs):
-    *pieces, out_ref, coulomb_ref = refs
-    wide, order = pieces[0].shape
+def screen_kernel(place_ref, polar_ref, *refs):
+    *run_refs, out_ref, coulomb_ref = refs
+    run, wide, order = run_refs[0].shape
+    across = len(run_refs) // CORES
     groups = order // LANES
     here = polar_ref.shape[1] // 2
     stride = out_ref.shape[0] // here
     columns = stride // 2 // groups
-    me = index_ref[0]
-    for hops, piece in zip(piece_hops(), pieces):
-        coulomb_ref[source_of(me, hops)] = piece[...]
+    z, x, core = place_ref[0], place_ref[1], place_ref[2]
+    for at, hop_x in enumerate(HOPS):
+        for hop in range(run):
+            chip = lax.rem(z + hop, run) * across + lax.rem(x + hop_x, across)
+            coulomb_ref[chip * CORES + core] = run_refs[at][hop]
+            coulomb_ref[chip * CORES + 1 - core] = run_refs[across + at][hop]
     rows = [
         jnp.concatenate([polar_ref[c * groups + k] for k in range(groups)], axis=1) for c in range(columns)
     ]
@@ -203,17 +209,17 @@
 
 def pack(lesser, greater, coulomb, owners):
     here = lesser.shape[0]
-    rows, wide = coulomb.shape
-    groups = wide // here
-    place = np.zeros((groups, rows, LANES), np.float32)
-    for group in range(groups):
-        place[group, np.arange(rows), group * rows + np.arange(rows)] = 1
+    lesser, greater = rows_view(lesser), rows_view(greater)
     return pl.pallas_call(
         pack_kernel,
         out_shape=jax.ShapeDtypeStruct((owners, 5 * here, LANES), jnp.float32),
+        in_specs=[pl.BlockSpec(memory_space=pltpu.HBM)] * 3,
+        out_specs=pl.BlockSpec(memory_space=pltpu.VMEM),
+        scratch_shapes=[pltpu.VMEM(x.shape, x.dtype) for x in (lesser, greater, coulomb)]
+        + [pltpu.SemaphoreType.DMA((3,))],
         compiler_params=pltpu.CompilerParams(vmem_limit_bytes=16 << 20),
         name="pack",
-    )(rows_view(lesser), rows_view(greater), coulomb, jnp.asarray(place, jnp.bfloat16))
+    )(*(pltpu.with_memory_space_constraint(x, pltpu.HBM) for x in (lesser, greater, coulomb)))
 
 
 def unpack(x, wide, order):
@@ -238,22 +244,26 @@
             pltpu.VMEM((2 * RADIX, points, lanes), jnp.float32),
         ],
         compiler_params=pltpu.CompilerParams(vmem_limit_bytes=24 << 20),
+        cost_estimate=pl.CostEstimate(
+            flops=RADIX * 3 * 2 * (2 * points) ** 2 * 3 * lanes, bytes_accessed=x.size * 4 + x.size, transcendentals=0
+        ),
         name="correlate",
     )(x, jnp.asarray(high), jnp.asarray(low), jnp.asarray(twiddle))
 
 
-def screen(polar, pieces, index, shape):
+def screen(polar, runs, place, shape):
     energies, _, columns, order = shape
+    run, wide, _ = runs[0].shape
     out = pl.pallas_call(
         screen_kernel,
         out_shape=jax.ShapeDtypeStruct((energies * columns * order * 2 // LANES, LANES), jnp.float32),
         in_specs=[pl.BlockSpec(memory_space=pltpu.SMEM)]
-        + [pl.BlockSpec(memory_space=pltpu.VMEM)] * (1 + len(pieces)),
+        + [pl.BlockSpec(memory_space=pltpu.VMEM)] * (1 + len(runs)),
         out_specs=pl.BlockSpec(memory_space=pltpu.VMEM),
-        scratch_shapes=[pltpu.VMEM((len(pieces),) + pieces[0].shape, jnp.bfloat16)],
+        scratch_shapes=[pltpu.VMEM((len(runs) * run, wide, order), jnp.bfloat16)],
         compiler_params=pltpu.CompilerParams(vmem_limit_bytes=24 << 20),
         name="screen",
-    )(index, polar, *pieces)
+    )(place, polar, *runs)
     out = out.reshape(energies, columns, order // LANES, 2, LANES).transpose(0, 1, 3, 2, 4)
     return out.reshape(energies, columns, 2, order).transpose(0, 2, 1, 3)
 
@@ -274,15 +284,17 @@
     packed = pack(lesser, greater_transposed, coulomb, owners)
     got = lax.all_to_all(packed.astype(jnp.float16), "energy", split_axis=0, concat_axis=0, tiled=True)
     got = got.astype(jnp.float32)
-    pieces = [unpack(got, coulomb.shape[1], order)]
-    for axis, size in enumerate((RUN, ACROSS, CORES)):
-        had = list(pieces)
-        for hop in range(1, size):
-            pieces += [moved(p, sharers, [hop * (axis == k) for k in range(3)]) for p in had]
-    index = jnp.full((1,), lax.axis_index("col"), jnp.int32)
+    wide = coulomb.shape[1]
+    mine = unpack(got, wide, order)
+    run = jnp.stack([mine] + [moved(mine, sharers, (hop, 0, 0)) for hop in range(1, RUN)])
     polar = correlate(got)
+    run, polar = lax.optimization_barrier((run, polar))
+    runs = [run] + [moved(run, sharers, (0, hop, 0)) for hop in HOPS[1:]]
+    runs += [moved(run, sharers, (0, 0, 1)) for run in runs]
     polar = lax.all_to_all(polar, "energy", split_axis=0, concat_axis=0, tiled=True)
-    return screen(polar, pieces, index, lesser.shape)
+    at = lax.axis_index("col")
+    place = [lax.div(at, ACROSS * CORES), lax.rem(lax.div(at, CORES), ACROSS), lax.rem(at, CORES)]
+    return screen(polar, runs, jnp.stack(place).astype(jnp.int32), lesser.shape)
 
 
 def solution(mesh):

time: 133 us -> 98.6 us (0.74)
  the two profiles are of different devices: /device:TPU:1 before, /device:TPU:7 now
where the time goes in v2:
time: 98.6 us; the launch traced here: 98.1 us
  starting transfers between devices  50.8 us (52%)
  blocking collectives  37.3 us (38%)
  Pallas kernels  7.67 us (8%)
  waiting for transfers between devices  1.87 us (2%)
    ppermute x9, starting transfers between devices, moved(): return lax.ppermute(x, 'col', [(source(at), at) for at in range(sharers)])  43.3 us
    all_to_all x1, blocking collectives, per_device(): lax.all_to_all(packed.astype(jnp.float16), 'energy', split_axis=0, concat...  37.3 us
    all_to_all x1, starting transfers between devices, per_device(): lax.all_to_all(polar, 'energy', split_axis=0, concat_axis=0, tiled=True)  7.5 us
    pallas_call x1, Pallas kernels, correlate(): pl.pallas_call(correlate_kernel, out_shape=jax.ShapeDtypeStruct((owners,...  3.55 us
    pallas_call x1, Pallas kernels, screen(): pl.pallas_call(screen_kernel, out_shape=jax.ShapeDtypeStruct((energies *...  2.43 us
  transfers between devices with their start and end apart: 10, of which 2 were waited for; matrix products, arithmetic and copies ran while one was open for 0% of the time, Pallas kernels for 4%

profile of v2, /device:TPU:7, one launch (start us, length us, event | category | flops | bytes accessed | tf_op | source)
XLA Modules:
  0.0 98.1 jit_solution(8089438140240114907)
XLA Ops:
  0.0 1.4 %pack.1 = f32[32,80,128]{2,1,0:T(8,128)S(1)} custom-call(f32[864,128]{1,0:T(8,128)} %bitcast.24, f32[864,128]{1,0:T(8,128)} %bitcast.25, bf16[36,48]{1,0:T(8,128)(2,1)} %coulomb_hbm.1), custom_call_target="tpu_custom_call" | custom-call | tf_op jit(solution)/shard_map/pack/pallas_call | solution.py:213
  1.4 0.1 convert_element_type.6
  1.5 37.3 %all_to_all.10 = f16[32,80,128]{2,1,0:T(8,128)(2,1)S(1)} all-to-all(f16[32,80,128]{2,1,0:T(8,128)(2,1)S(1)} %convert_element_type.6), channel_id=1, replica_groups=mesh['energy'=32,'col'=24] {'energy'}, dimensions={0} | all-to-all | bytes 1310720 | tf_op jit(solution)/shard_map/all_to_all | solution.py:285
  38.8 0.1 convert_element_type.7.x_ref
  38.9 0.3 unpack.1
  39.2 15.0 %collective-permute-start.1 = (bf16[48,1152]{1,0:T(8,128)(2,1)S(1)}, bf16[48,1152]{1,0:T(8,128)(2,1)S(1)}, u32[]{:S(2)}, u32[]{:S(2)}) collective-permute-start(bf16[48,1152]{1,0:T(8,128)(2,1)S(1)} %unpack.1), channel_id=1, source_target_pairs={{16,0},{17,1},{18,2},{19,3},{20,4},{21,5},{22,6},{23,7},{0,8},{1,9... | collective-permute-start | bytes 331784 | tf_op jit(solution)/shard_map/ppermute | solution.py:277
  54.2 1.9 %collective-permute-start = (bf16[48,1152]{1,0:T(8,128)(2,1)S(1)}, bf16[48,1152]{1,0:T(8,128)(2,1)S(1)}, u32[]{:S(2)}, u32[]{:S(2)}) collective-permute-start(bf16[48,1152]{1,0:T(8,128)(2,1)S(1)} %unpack.1), channel_id=1, source_target_pairs={{8,0},{9,1},{10,2},{11,3},{12,4},{13,5},{14,6},{15,7},{16,8},{17,9... | collective-permute-start | bytes 331784 | tf_op jit(solution)/shard_map/ppermute | solution.py:277
  56.2 3.6 %correlate.1 = bf16[32,32,128]{2,1,0:T(8,128)(2,1)} custom-call(f32[32,80,128]{2,1,0:T(8,128)S(1)} %convert_element_type.7.x_ref, bf16[256,256]{1,0:T(8,128)(2,1)S(1)} %copy-done.1, bf16[256,256]{1,0:T(8,128)(2,1)S(1)} %copy-done, f32[128,128]{1,0:T(8,128)S(1)} %copy-done.2), custom_call_target="tpu_custom_call" | custom-call | flops 1207959552 | bytes 1638400 | tf_op jit(solution)/shard_map/correlate/pallas_call | solution.py:239
  59.7 0.0 collective-permute-done.1
  59.7 0.4 collective-permute-done
  60.1 7.5 %all-to-all-start.1 = ((bf16[32,32,128]{2,1,0:T(8,128)(2,1)}), bf16[32,32,128]{2,1,0:T(8,128)(2,1)S(1)}, u32[]{:S(2)}, u32[]{:S(2)}) async-start(bf16[32,32,128]{2,1,0:T(8,128)(2,1)} %correlate.1), calls=%async_computation.1 | async-start | bytes 524288 | tf_op jit(solution)/shard_map/all_to_all | solution.py:294
  67.6 2.1 %collective-permute-start.4 = (bf16[3,48,1152]{2,1,0:T(8,128)(2,1)S(1)}, bf16[3,48,1152]{2,1,0:T(8,128)(2,1)S(1)}, u32[]{:S(2)}, u32[]{:S(2)}) collective-permute-start(bf16[3,48,1152]{2,1,0:T(8,128)(2,1)S(1)} %pad_maximum_fusion.refs_0_), channel_id=1, source_target_pairs={{6,0},{7,1},{0,2},{1,3},{2,4},{3,5},{4,6},{5,7},{14,8},{15,9},{8,1... | collective-permute-start | bytes 995336 | tf_op jit(solution)/shard_map/ppermute | solution.py:277
  69.8 3.2 %collective-permute-start.3 = (bf16[3,48,1152]{2,1,0:T(8,128)(2,1)S(1)}, bf16[3,48,1152]{2,1,0:T(8,128)(2,1)S(1)}, u32[]{:S(2)}, u32[]{:S(2)}) collective-permute-start(bf16[3,48,1152]{2,1,0:T(8,128)(2,1)S(1)} %pad_maximum_fusion.refs_0_), channel_id=1, source_target_pairs={{2,0},{3,1},{4,2},{5,3},{6,4},{7,5},{0,6},{1,7},{10,8},{11,9},{12,... | collective-permute-start | bytes 995336 | tf_op jit(solution)/shard_map/ppermute | solution.py:277
  72.9 3.0 %collective-permute-start.2 = (bf16[3,48,1152]{2,1,0:T(8,128)(2,1)S(1)}, bf16[3,48,1152]{2,1,0:T(8,128)(2,1)S(1)}, u32[]{:S(2)}, u32[]{:S(2)}) collective-permute-start(bf16[3,48,1152]{2,1,0:T(8,128)(2,1)S(1)} %pad_maximum_fusion.refs_0_), channel_id=1, source_target_pairs={{4,0},{5,1},{6,2},{7,3},{0,4},{1,5},{2,6},{3,7},{12,8},{13,9},{14,... | collective-permute-start | bytes 995336 | tf_op jit(solution)/shard_map/ppermute | solution.py:277
  76.0 5.8 %collective-permute-start.5 = (bf16[3,48,1152]{2,1,0:T(8,128)(2,1)S(1)}, bf16[3,48,1152]{2,1,0:T(8,128)(2,1)S(1)}, u32[]{:S(2)}, u32[]{:S(2)}) collective-permute-start(bf16[3,48,1152]{2,1,0:T(8,128)(2,1)S(1)} %pad_maximum_fusion.refs_0_), channel_id=1, source_target_pairs={{1,0},{0,1},{3,2},{2,3},{5,4},{4,5},{7,6},{6,7},{9,8},{8,9},{11,10... | collective-permute-start | bytes 995336 | tf_op jit(solution)/shard_map/ppermute | solution.py:277
  81.8 0.0 collective-permute-done.4.refs_3_
  81.8 1.9 %collective-permute-start.8 = (bf16[3,48,1152]{2,1,0:T(8,128)(2,1)S(1)}, bf16[3,48,1152]{2,1,0:T(8,128)(2,1)S(1)}, u32[]{:S(2)}, u32[]{:S(2)}) collective-permute-start(bf16[3,48,1152]{2,1,0:T(8,128)(2,1)S(1)} %collective-permute-done.4.refs_3_), channel_id=1, source_target_pairs={{1,0},{0,1},{3,2},{2,3},{5,4},{4,5},{7,6},{6,7},{9,8},{8,9},{11,10... | collective-permute-start | bytes 995336 | tf_op jit(solution)/shard_map/ppermute | solution.py:277
  83.7 0.0 collective-permute-done.3.refs_2_
  83.7 8.4 %collective-permute-start.7 = (bf16[3,48,1152]{2,1,0:T(8,128)(2,1)S(1)}, bf16[3,48,1152]{2,1,0:T(8,128)(2,1)S(1)}, u32[]{:S(2)}, u32[]{:S(2)}) collective-permute-start(bf16[3,48,1152]{2,1,0:T(8,128)(2,1)S(1)} %collective-permute-done.3.refs_2_), channel_id=1, source_target_pairs={{1,0},{0,1},{3,2},{2,3},{5,4},{4,5},{7,6},{6,7},{9,8},{8,9},{11,10... | collective-permute-start | bytes 995336 | tf_op jit(solution)/shard_map/ppermute | solution.py:277
  92.2 1.9 %collective-permute-start.6 = (bf16[3,48,1152]{2,1,0:T(8,128)(2,1)S(1)}, bf16[3,48,1152]{2,1,0:T(8,128)(2,1)S(1)}, u32[]{:S(2)}, u32[]{:S(2)}) collective-permute-start(bf16[3,48,1152]{2,1,0:T(8,128)(2,1)S(1)} %collective-permute-done.2.refs_1_), channel_id=1, source_target_pairs={{1,0},{0,1},{3,2},{2,3},{5,4},{4,5},{7,6},{6,7},{9,8},{8,9},{11,10... | collective-permute-start | bytes 995336 | tf_op jit(solution)/shard_map/ppermute | solution.py:277
  94.1 0.1 pad_add_fusion.place_ref
  94.2 0.0 collective-permute-done.5.refs_4_
  94.2 1.5 %collective-permute-done.6.refs_5_ = bf16[3,48,1152]{2,1,0:T(8,128)(2,1)S(1)} collective-permute-done((bf16[3,48,1152]{2,1,0:T(8,128)(2,1)S(1)}, bf16[3,48,1152]{2,1,0:T(8,128)(2,1)S(1)}, u32[]{:S(2)}, u32[]{:S(2)}) %collective-permute-start.6) | collective-permute-done | bytes 331808 | tf_op jit(solution)/shard_map/ppermute | solution.py:277
  95.7 2.4 %screen.1 = f32[864,128]{1,0:T(8,128)} custom-call(s32[3]{0:T(128)S(1)} %pad_add_fusion.place_ref, bf16[32,32,128]{2,1,0:T(8,128)(2,1)S(1)} %all-to-all-done.1.polar_ref, bf16[3,48,1152]{2,1,0:T(8,128)(2,1)S(1)} %pad_maximum_fusion.refs_0_, bf16[3,48,1152]{2,1,0:T(8,128)(2,1)S(1)} %collective-permute-done.2.refs_1_, ...), custom_call_target="tpu_custom_call" | custom-call | tf_op jit(solution)/shard_map/screen/pallas_call | solution.py:257
  (11 shorter events, 0.1 us)
Async XLA Ops:
  38.8 17.3 %copy-start = (bf16[256,256]{1,0:T(8,128)(2,1)S(1)}, bf16[256,256]{1,0:T(8,128)(2,1)}, u32[]{:S(2)}) copy-start(bf16[256,256]{1,0:T(8,128)(2,1)} %constant.24.clone.low_ref) | copy-start | bytes 393220
  38.8 17.3 %copy-start.1 = (bf16[256,256]{1,0:T(8,128)(2,1)S(1)}, bf16[256,256]{1,0:T(8,128)(2,1)}, u32[]{:S(2)}) copy-start(bf16[256,256]{1,0:T(8,128)(2,1)} %constant.23.clone.high_ref) | copy-start | bytes 393220
  38.8 17.3 %copy-start.2 = (f32[128,128]{1,0:T(8,128)S(1)}, f32[128,128]{1,0:T(8,128)}, u32[]{:S(2)}) copy-start(f32[128,128]{1,0:T(8,128)} %constant.25.clone.twiddle_ref) | copy-start | bytes 196612
  39.2 20.5 %collective-permute-start.1 = (bf16[48,1152]{1,0:T(8,128)(2,1)S(1)}, bf16[48,1152]{1,0:T(8,128)(2,1)S(1)}, u32[]{:S(2)}, u32[]{:S(2)}) collective-permute-start(bf16[48,1152]{1,0:T(8,128)(2,1)S(1)} %unpack.1), channel_id=1, source_target_pairs={{16,0},{17,1},{18,2},{19,3},{20,4},{21,5},{22,6},{23,7},{0,8},{1,9... | collective-permute-start | bytes 331784 | tf_op jit(solution)/shard_map/ppermute | solution.py:277
  54.2 5.9 %collective-permute-start = (bf16[48,1152]{1,0:T(8,128)(2,1)S(1)}, bf16[48,1152]{1,0:T(8,128)(2,1)S(1)}, u32[]{:S(2)}, u32[]{:S(2)}) collective-permute-start(bf16[48,1152]{1,0:T(8,128)(2,1)S(1)} %unpack.1), channel_id=1, source_target_pairs={{8,0},{9,1},{10,2},{11,3},{12,4},{13,5},{14,6},{15,7},{16,8},{17,9... | collective-permute-start | bytes 331784 | tf_op jit(solution)/shard_map/ppermute | solution.py:277
  60.1 35.6 %all-to-all-start.1 = ((bf16[32,32,128]{2,1,0:T(8,128)(2,1)}), bf16[32,32,128]{2,1,0:T(8,128)(2,1)S(1)}, u32[]{:S(2)}, u32[]{:S(2)}) async-start(bf16[32,32,128]{2,1,0:T(8,128)(2,1)} %correlate.1), calls=%async_computation.1 | async-start | bytes 524288 | tf_op jit(solution)/shard_map/all_to_all | solution.py:294
  67.6 14.1 %collective-permute-start.4 = (bf16[3,48,1152]{2,1,0:T(8,128)(2,1)S(1)}, bf16[3,48,1152]{2,1,0:T(8,128)(2,1)S(1)}, u32[]{:S(2)}, u32[]{:S(2)}) collective-permute-start(bf16[3,48,1152]{2,1,0:T(8,128)(2,1)S(1)} %pad_maximum_fusion.refs_0_), channel_id=1, source_target_pairs={{6,0},{7,1},{0,2},{1,3},{2,4},{3,5},{4,6},{5,7},{14,8},{15,9},{8,1... | collective-permute-start | bytes 995336 | tf_op jit(solution)/shard_map/ppermute | solution.py:277
  69.8 14.0 %collective-permute-start.3 = (bf16[3,48,1152]{2,1,0:T(8,128)(2,1)S(1)}, bf16[3,48,1152]{2,1,0:T(8,128)(2,1)S(1)}, u32[]{:S(2)}, u32[]{:S(2)}) collective-permute-start(bf16[3,48,1152]{2,1,0:T(8,128)(2,1)S(1)} %pad_maximum_fusion.refs_0_), channel_id=1, source_target_pairs={{2,0},{3,1},{4,2},{5,3},{6,4},{7,5},{0,6},{1,7},{10,8},{11,9},{12,... | collective-permute-start | bytes 995336 | tf_op jit(solution)/shard_map/ppermute | solution.py:277
  72.9 19.2 %collective-permute-start.2 = (bf16[3,48,1152]{2,1,0:T(8,128)(2,1)S(1)}, bf16[3,48,1152]{2,1,0:T(8,128)(2,1)S(1)}, u32[]{:S(2)}, u32[]{:S(2)}) collective-permute-start(bf16[3,48,1152]{2,1,0:T(8,128)(2,1)S(1)} %pad_maximum_fusion.refs_0_), channel_id=1, source_target_pairs={{4,0},{5,1},{6,2},{7,3},{0,4},{1,5},{2,6},{3,7},{12,8},{13,9},{14,... | collective-permute-start | bytes 995336 | tf_op jit(solution)/shard_map/ppermute | solution.py:277
  76.0 18.2 %collective-permute-start.5 = (bf16[3,48,1152]{2,1,0:T(8,128)(2,1)S(1)}, bf16[3,48,1152]{2,1,0:T(8,128)(2,1)S(1)}, u32[]{:S(2)}, u32[]{:S(2)}) collective-permute-start(bf16[3,48,1152]{2,1,0:T(8,128)(2,1)S(1)} %pad_maximum_fusion.refs_0_), channel_id=1, source_target_pairs={{1,0},{0,1},{3,2},{2,3},{5,4},{4,5},{7,6},{6,7},{9,8},{8,9},{11,10... | collective-permute-start | bytes 995336 | tf_op jit(solution)/shard_map/ppermute | solution.py:277
  81.8 12.4 %collective-permute-start.8 = (bf16[3,48,1152]{2,1,0:T(8,128)(2,1)S(1)}, bf16[3,48,1152]{2,1,0:T(8,128)(2,1)S(1)}, u32[]{:S(2)}, u32[]{:S(2)}) collective-permute-start(bf16[3,48,1152]{2,1,0:T(8,128)(2,1)S(1)} %collective-permute-done.4.refs_3_), channel_id=1, source_target_pairs={{1,0},{0,1},{3,2},{2,3},{5,4},{4,5},{7,6},{6,7},{9,8},{8,9},{11,10... | collective-permute-start | bytes 995336 | tf_op jit(solution)/shard_map/ppermute | solution.py:277
  83.7 10.5 %collective-permute-start.7 = (bf16[3,48,1152]{2,1,0:T(8,128)(2,1)S(1)}, bf16[3,48,1152]{2,1,0:T(8,128)(2,1)S(1)}, u32[]{:S(2)}, u32[]{:S(2)}) collective-permute-start(bf16[3,48,1152]{2,1,0:T(8,128)(2,1)S(1)} %collective-permute-done.3.refs_2_), channel_id=1, source_target_pairs={{1,0},{0,1},{3,2},{2,3},{5,4},{4,5},{7,6},{6,7},{9,8},{8,9},{11,10... | collective-permute-start | bytes 995336 | tf_op jit(solution)/shard_map/ppermute | solution.py:277
  92.2 3.5 %collective-permute-start.6 = (bf16[3,48,1152]{2,1,0:T(8,128)(2,1)S(1)}, bf16[3,48,1152]{2,1,0:T(8,128)(2,1)S(1)}, u32[]{:S(2)}, u32[]{:S(2)}) collective-permute-start(bf16[3,48,1152]{2,1,0:T(8,128)(2,1)S(1)} %collective-permute-done.2.refs_1_), channel_id=1, source_target_pairs={{1,0},{0,1},{3,2},{2,3},{5,4},{4,5},{7,6},{6,7},{9,8},{8,9},{11,10... | collective-permute-start | bytes 995336 | tf_op jit(solution)/shard_map/ppermute | solution.py:277

commit v3 on v2

--- a/solution.py
+++ b/solution.py
@@ -12,8 +12,9 @@
 
 LANES = 128
 RADIX = 8
+PARTS = 4
 RUN, ACROSS, CORES = 3, 4, 2
-HOPS = (0, 2, 1, 3)
+HOPS = (0, 1, 3, 2)
 HALF = math.sqrt(0.5)
 COULOMB_SCALE = float(2**18)
 SCALE = 4096.0
@@ -33,12 +34,13 @@
 
 
 def pack_kernel(lesser_hbm, greater_hbm, coulomb_hbm, out_ref, lesser_ref, greater_ref, coulomb_ref, sems):
-    copies = [
-        pltpu.make_async_copy(source, target, sems.at[i])
-        for i, (source, target) in enumerate(
-            ((lesser_hbm, lesser_ref), (greater_hbm, greater_ref), (coulomb_hbm, coulomb_ref))
-        )
-    ]
+    copies = []
+    for which, (source, target) in enumerate(((lesser_hbm, lesser_ref), (greater_hbm, greater_ref))):
+        rows = source.shape[0] // PARTS
+        for part in range(PARTS):
+            at = pl.ds(part * rows, rows)
+            copies.append(pltpu.make_async_copy(source.at[at, :], target.at[at, :], sems.at[which * PARTS + part]))
+    copies.append(pltpu.make_async_copy(coulomb_hbm, coulomb_ref, sems.at[2 * PARTS]))
     for copy in copies:
         copy.start()
     here = out_ref.shape[1] // 5
@@ -46,12 +48,13 @@
     blocks = stride // 2
     out_ref[blocks:, :4 * here, :] = jnp.zeros_like(out_ref[blocks:, :4 * here, :])
     for which, ref in enumerate((lesser_ref, greater_ref)):
-        copies[which].wait()
+        for copy in copies[which * PARTS:(which + 1) * PARTS]:
+            copy.wait()
         for block in range(blocks):
             for part in range(2):
                 at = (which * 2 + part) * here
                 out_ref[block, at:at + here, :] = ref[pl.ds(block * 2 + part, here, stride=stride), :] * SCALE
-    copies[2].wait()
+    copies[2 * PARTS].wait()
     block = coulomb_ref[...]
     rows, wide = block.shape
     row = lax.broadcasted_iota(jnp.int32, (rows, LANES), 0)
@@ -78,19 +81,19 @@
         out_ref[group * extra:(group + 1) * extra, :] = row.astype(jnp.bfloat16)
 
 
-def correlate_kernel(x_ref, high_ref, low_ref, twiddle_ref, out_ref, total_ref, spread_ref):
+def correlate_kernel(x_ref, matrices_ref, twiddle_ref, out_ref, total_ref, spread_ref):
     sources, here, lanes = x_ref.shape[0], x_ref.shape[1] // 5, x_ref.shape[2]
-    points = high_ref.shape[0] // 2
+    rows = matrices_ref.shape[1]
+    points = rows // 2
     pieces = sources * here // points
     per_piece = sources // pieces
-    high, low = high_ref[...], low_ref[...]
+    matrices = matrices_ref[...]
 
     def dft(re, im):
         x = jnp.concatenate([re, im], axis=0)
         x_high, x_low = split(x)
-        y = jnp.dot(high, x_high, preferred_element_type=jnp.float32)
-        y += jnp.dot(high, x_low, preferred_element_type=jnp.float32)
-        return y + jnp.dot(low, x_high, preferred_element_type=jnp.float32)
+        both = jnp.dot(matrices, x_high, preferred_element_type=jnp.float32)
+        return both[:rows] + both[rows:] + jnp.dot(matrices[:rows], x_low, preferred_element_type=jnp.float32)
 
     def piece(which, part, j):
         at = (which * 2 + part) * here
@@ -154,36 +157,44 @@
             )
 
 
-def screen_kernel(place_ref, polar_ref, *refs):
+def product_kernel(place_ref, polar_ref, *refs):
     *run_refs, out_ref, coulomb_ref = refs
     run, wide, order = run_refs[0].shape
-    across = len(run_refs) // CORES
+    across = len(run_refs)
     groups = order // LANES
-    here = polar_ref.shape[1] // 2
-    stride = out_ref.shape[0] // here
-    columns = stride // 2 // groups
-    z, x, core = place_ref[0], place_ref[1], place_ref[2]
+    z, x = place_ref[0], place_ref[1]
     for at, hop_x in enumerate(HOPS):
         for hop in range(run):
-            chip = lax.rem(z + hop, run) * across + lax.rem(x + hop_x, across)
-            coulomb_ref[chip * CORES + core] = run_refs[at][hop]
-            coulomb_ref[chip * CORES + 1 - core] = run_refs[across + at][hop]
+            coulomb_ref[lax.rem(z + hop, run) * across + lax.rem(x + hop_x, across)] = run_refs[at][hop]
+    columns = out_ref.shape[0] // polar_ref.shape[1]
     rows = [
         jnp.concatenate([polar_ref[c * groups + k] for k in range(groups)], axis=1) for c in range(columns)
     ]
-    product = lax.dot_general(
+    out_ref[...] = lax.dot_general(
         jnp.concatenate(rows, axis=0),
-        coulomb_ref[...].reshape(order, order),
+        coulomb_ref[...].reshape(across * run * wide, order),
         (((1,), (1,)), ((), ())),
         preferred_element_type=jnp.float32,
     )
-    for c in range(columns):
-        for part in range(2):
-            at = (c * 2 + part) * here
-            for k in range(groups):
-                out_ref[pl.ds((c * groups + k) * 2 + part, here, stride=stride), :] = product[
-                    at:at + here, k * LANES:(k + 1) * LANES
-                ]
+
+
+def merge_kernel(place_ref, mine_ref, other_ref, out_ref, *, wide, here):
+    first = place_ref[2] == 0
+    stride = out_ref.shape[0] // here
+    columns = mine_ref.shape[0] // (2 * here)
+    for at in range(columns * 2):
+        rows = slice(at * here, (at + 1) * here)
+        mine, other = mine_ref[rows, :], other_ref[rows, :]
+        cores = jnp.where(first, mine, other), jnp.where(first, other, mine)
+        pieces = []
+        for chip in range(mine.shape[1] // wide):
+            pieces += [part[:, chip * wide:(chip + 1) * wide] for part in cores]
+        row = jnp.concatenate(pieces, axis=1)
+        groups = row.shape[1] // LANES
+        for k in range(groups):
+            out_ref[pl.ds((at // 2 * groups + k) * 2 + at % 2, here, stride=stride), :] = row[
+                :, k * LANES:(k + 1) * LANES
+            ]
 
 
 def tables(energies):
@@ -197,7 +208,7 @@
     for r in range(RADIX):
         turned = np.arange(points) * r * (np.pi / energies)
         twiddle[:, 2 * r], twiddle[:, 2 * r + 1] = np.cos(turned), -np.sin(turned)
-    return high, low, twiddle
+    return np.concatenate([high, low]), twiddle
 
 
 def rows_view(x):
@@ -216,7 +227,7 @@
         in_specs=[pl.BlockSpec(memory_space=pltpu.HBM)] * 3,
         out_specs=pl.BlockSpec(memory_space=pltpu.VMEM),
         scratch_shapes=[pltpu.VMEM(x.shape, x.dtype) for x in (lesser, greater, coulomb)]
-        + [pltpu.SemaphoreType.DMA((3,))],
+        + [pltpu.SemaphoreType.DMA((2 * PARTS + 1,))],
         compiler_params=pltpu.CompilerParams(vmem_limit_bytes=16 << 20),
         name="pack",
     )(*(pltpu.with_memory_space_constraint(x, pltpu.HBM) for x in (lesser, greater, coulomb)))
@@ -235,7 +246,7 @@
     owners, here, lanes = x.shape[0], x.shape[1] // 5, x.shape[2]
     energies = owners * here
     points = energies * 2 // RADIX
-    high, low, twiddle = tables(energies)
+    matrices, twiddle = tables(energies)
     return pl.pallas_call(
         correlate_kernel,
         out_shape=jax.ShapeDtypeStruct((owners, 2 * here, lanes), jnp.bfloat16),
@@ -248,22 +259,34 @@
             flops=RADIX * 3 * 2 * (2 * points) ** 2 * 3 * lanes, bytes_accessed=x.size * 4 + x.size, transcendentals=0
         ),
         name="correlate",
-    )(x, jnp.asarray(high), jnp.asarray(low), jnp.asarray(twiddle))
-
-
-def screen(polar, runs, place, shape):
-    energies, _, columns, order = shape
-    run, wide, _ = runs[0].shape
-    out = pl.pallas_call(
-        screen_kernel,
-        out_shape=jax.ShapeDtypeStruct((energies * columns * order * 2 // LANES, LANES), jnp.float32),
+    )(x, jnp.asarray(matrices), jnp.asarray(twiddle))
+
+
+def product(polar, runs, place, columns):
+    run, wide, order = runs[0].shape
+    chips = len(runs) * run
+    return pl.pallas_call(
+        product_kernel,
+        out_shape=jax.ShapeDtypeStruct((columns * polar.shape[1], chips * wide), jnp.float32),
         in_specs=[pl.BlockSpec(memory_space=pltpu.SMEM)]
         + [pl.BlockSpec(memory_space=pltpu.VMEM)] * (1 + len(runs)),
         out_specs=pl.BlockSpec(memory_space=pltpu.VMEM),
-        scratch_shapes=[pltpu.VMEM((len(runs) * run, wide, order), jnp.bfloat16)],
+        scratch_shapes=[pltpu.VMEM((chips, wide, order), jnp.bfloat16)],
         compiler_params=pltpu.CompilerParams(vmem_limit_bytes=24 << 20),
-        name="screen",
+        name="product",
     )(place, polar, *runs)
+
+
+def merge(mine, other, place, wide, shape):
+    energies, _, columns, order = shape
+    out = pl.pallas_call(
+        functools.partial(merge_kernel, wide=wide, here=energies),
+        out_shape=jax.ShapeDtypeStruct((energies * columns * order * 2 // LANES, LANES), jnp.float32),
+        in_specs=[pl.BlockSpec(memory_space=pltpu.SMEM)] + [pl.BlockSpec(memory_space=pltpu.VMEM)] * 2,
+        out_specs=pl.BlockSpec(memory_space=pltpu.VMEM),
+        compiler_params=pltpu.CompilerParams(vmem_limit_bytes=16 << 20),
+        name="merge",
+    )(place, mine, other)
     out = out.reshape(energies, columns, order // LANES, 2, LANES).transpose(0, 1, 3, 2, 4)
     return out.reshape(energies, columns, 2, order).transpose(0, 2, 1, 3)
 
@@ -290,11 +313,13 @@
     polar = correlate(got)
     run, polar = lax.optimization_barrier((run, polar))
     runs = [run] + [moved(run, sharers, (0, hop, 0)) for hop in HOPS[1:]]
-    runs += [moved(run, sharers, (0, 0, 1)) for run in runs]
     polar = lax.all_to_all(polar, "energy", split_axis=0, concat_axis=0, tiled=True)
     at = lax.axis_index("col")
     place = [lax.div(at, ACROSS * CORES), lax.rem(lax.div(at, CORES), ACROSS), lax.rem(at, CORES)]
-    return screen(polar, runs, jnp.stack(place).astype(jnp.int32), lesser.shape)
+    place = jnp.stack(place).astype(jnp.int32)
+    given = product(moved(polar, sharers, (0, 0, 1)), runs, place, lesser.shape[2])
+    other = moved(given, sharers, (0, 0, 1))
+    return merge(product(polar, runs, place, lesser.shape[2]), other, place, coulomb.shape[1], lesser.shape)
 
 
 def solution(mesh):

time: 98.6 us -> 98.6 us (level)
  the two profiles are of different devices: /device:TPU:7 before, /device:TPU:1 now
where the time goes in v3:
time: 98.6 us; the launch traced here: 98.2 us
  starting transfers between devices  45.7 us (46%)
  blocking collectives  38.1 us (39%)
  Pallas kernels  9.27 us (9%)
  waiting for transfers between devices  4.58 us (5%)
    ppermute x7, starting transfers between devices, moved(): return lax.ppermute(x, 'col', [(source(at), at) for at in range(sharers)])  38.3 us
    all_to_all x1, blocking collectives, per_device(): lax.all_to_all(packed.astype(jnp.float16), 'energy', split_axis=0, concat...  38.1 us
    all_to_all x1, starting transfers between devices, per_device(): lax.all_to_all(polar, 'energy', split_axis=0, concat_axis=0, tiled=True)  7.46 us
    pallas_call x1, Pallas kernels, correlate(): pl.pallas_call(correlate_kernel, out_shape=jax.ShapeDtypeStruct((owners,...  3.41 us
    all_to_all x1, waiting for transfers between devices, per_device(): lax.all_to_all(polar, 'energy', split_axis=0, concat_axis=0, tiled=True)  3.02 us
    pallas_call x2, Pallas kernels, product(): pl.pallas_call(product_kernel, out_shape=jax.ShapeDtypeStruct((columns *...  2.31 us
  transfers between devices with their start and end apart: 8, of which 3 were waited for; matrix products, arithmetic and copies ran while one was open for 0% of the time, Pallas kernels for 5%

profile of v3, /device:TPU:1, one launch (start us, length us, event | category | flops | bytes accessed | tf_op | source)
XLA Modules:
  0.0 98.2 jit_solution(6603641232005929649)
XLA Ops:
  0.0 1.6 %pack.1 = f32[32,80,128]{2,1,0:T(8,128)S(1)} custom-call(f32[864,128]{1,0:T(8,128)} %bitcast.24, f32[864,128]{1,0:T(8,128)} %bitcast.25, bf16[36,48]{1,0:T(8,128)(2,1)} %coulomb_hbm.1), custom_call_target="tpu_custom_call" | custom-call | tf_op jit(solution)/shard_map/pack/pallas_call | solution.py:224
  1.6 0.1 convert_element_type.6
  1.7 38.1 %all_to_all.10 = f16[32,80,128]{2,1,0:T(8,128)(2,1)S(1)} all-to-all(f16[32,80,128]{2,1,0:T(8,128)(2,1)S(1)} %convert_element_type.6), channel_id=1, replica_groups=mesh['energy'=32,'col'=24] {'energy'}, dimensions={0} | all-to-all | bytes 1310720 | tf_op jit(solution)/shard_map/all_to_all | solution.py:308
  39.8 0.1 convert_element_type.7.x_ref
  39.9 0.3 unpack.1
  40.2 15.0 %collective-permute-start.1 = (bf16[48,1152]{1,0:T(8,128)(2,1)S(1)}, bf16[48,1152]{1,0:T(8,128)(2,1)S(1)}, u32[]{:S(2)}, u32[]{:S(2)}) collective-permute-start(bf16[48,1152]{1,0:T(8,128)(2,1)S(1)} %unpack.1), channel_id=1, source_target_pairs={{16,0},{17,1},{18,2},{19,3},{20,4},{21,5},{22,6},{23,7},{0,8},{1,9... | collective-permute-start | bytes 331784 | tf_op jit(solution)/shard_map/ppermute | solution.py:300
  55.2 1.9 %collective-permute-start = (bf16[48,1152]{1,0:T(8,128)(2,1)S(1)}, bf16[48,1152]{1,0:T(8,128)(2,1)S(1)}, u32[]{:S(2)}, u32[]{:S(2)}) collective-permute-start(bf16[48,1152]{1,0:T(8,128)(2,1)S(1)} %unpack.1), channel_id=1, source_target_pairs={{8,0},{9,1},{10,2},{11,3},{12,4},{13,5},{14,6},{15,7},{16,8},{17,9... | collective-permute-start | bytes 331784 | tf_op jit(solution)/shard_map/ppermute | solution.py:300
  57.1 3.4 %correlate.1 = bf16[32,32,128]{2,1,0:T(8,128)(2,1)} custom-call(f32[32,80,128]{2,1,0:T(8,128)S(1)} %convert_element_type.7.x_ref, bf16[512,256]{1,0:T(8,128)(2,1)S(1)} %copy-done, f32[128,128]{1,0:T(8,128)S(1)} %copy-done.1), custom_call_target="tpu_custom_call" | custom-call | flops 1207959552 | bytes 1638400 | tf_op jit(solution)/shard_map/correlate/pallas_call | solution.py:250
  60.5 0.0 collective-permute-done.1
  60.5 0.5 collective-permute-done
  61.1 7.5 %all-to-all-start.1 = ((bf16[32,32,128]{2,1,0:T(8,128)(2,1)}), bf16[32,32,128]{2,1,0:T(8,128)(2,1)S(1)}, u32[]{:S(2)}, u32[]{:S(2)}) async-start(bf16[32,32,128]{2,1,0:T(8,128)(2,1)} %correlate.1), calls=%async_computation.1 | async-start | bytes 524288 | tf_op jit(solution)/shard_map/all_to_all | solution.py:316
  68.6 4.7 %collective-permute-start.4 = (bf16[3,48,1152]{2,1,0:T(8,128)(2,1)S(1)}, bf16[3,48,1152]{2,1,0:T(8,128)(2,1)S(1)}, u32[]{:S(2)}, u32[]{:S(2)}) collective-permute-start(bf16[3,48,1152]{2,1,0:T(8,128)(2,1)S(1)} %pad_maximum_fusion.refs_0_), channel_id=1, source_target_pairs={{4,0},{5,1},{6,2},{7,3},{0,4},{1,5},{2,6},{3,7},{12,8},{13,9},{14,... | collective-permute-start | bytes 995336 | tf_op jit(solution)/shard_map/ppermute | solution.py:300
  73.2 2.2 %collective-permute-start.3 = (bf16[3,48,1152]{2,1,0:T(8,128)(2,1)S(1)}, bf16[3,48,1152]{2,1,0:T(8,128)(2,1)S(1)}, u32[]{:S(2)}, u32[]{:S(2)}) collective-permute-start(bf16[3,48,1152]{2,1,0:T(8,128)(2,1)S(1)} %pad_maximum_fusion.refs_0_), channel_id=1, source_target_pairs={{6,0},{7,1},{0,2},{1,3},{2,4},{3,5},{4,6},{5,7},{14,8},{15,9},{8,1... | collective-permute-start | bytes 995336 | tf_op jit(solution)/shard_map/ppermute | solution.py:300
  75.5 4.3 %collective-permute-start.2 = (bf16[3,48,1152]{2,1,0:T(8,128)(2,1)S(1)}, bf16[3,48,1152]{2,1,0:T(8,128)(2,1)S(1)}, u32[]{:S(2)}, u32[]{:S(2)}) collective-permute-start(bf16[3,48,1152]{2,1,0:T(8,128)(2,1)S(1)} %pad_maximum_fusion.refs_0_), channel_id=1, source_target_pairs={{2,0},{3,1},{4,2},{5,3},{6,4},{7,5},{0,6},{1,7},{10,8},{11,9},{12,... | collective-permute-start | bytes 995336 | tf_op jit(solution)/shard_map/ppermute | solution.py:300
  79.8 3.0 %all-to-all-done.1.polar_ref = bf16[32,32,128]{2,1,0:T(8,128)(2,1)S(1)} async-done(((bf16[32,32,128]{2,1,0:T(8,128)(2,1)}), bf16[32,32,128]{2,1,0:T(8,128)(2,1)S(1)}, u32[]{:S(2)}, u32[]{:S(2)}) %all-to-all-start.1) | async-done | bytes 262176 | tf_op jit(solution)/shard_map/all_to_all | solution.py:316
  82.8 7.9 %collective-permute-start.5 = (bf16[32,32,128]{2,1,0:T(8,128)(2,1)S(1)}, bf16[32,32,128]{2,1,0:T(8,128)(2,1)S(1)}, u32[]{:S(2)}, u32[]{:S(2)}) collective-permute-start(bf16[32,32,128]{2,1,0:T(8,128)(2,1)S(1)} %all-to-all-done.1.polar_ref), channel_id=1, source_target_pairs={{1,0},{0,1},{3,2},{2,3},{5,4},{4,5},{7,6},{6,7},{9,8},{8,9},{11,10... | collective-permute-start | bytes 786440 | tf_op jit(solution)/shard_map/ppermute | solution.py:300
  90.7 0.1 pad_add_fusion.place_ref
  90.8 0.0 collective-permute-done.2.refs_1_
  90.8 1.0 %collective-permute-done.5.polar_ref = bf16[32,32,128]{2,1,0:T(8,128)(2,1)S(1)} collective-permute-done((bf16[32,32,128]{2,1,0:T(8,128)(2,1)S(1)}, bf16[32,32,128]{2,1,0:T(8,128)(2,1)S(1)}, u32[]{:S(2)}, u32[]{:S(2)}) %collective-permute-start.5) | collective-permute-done | bytes 262176 | tf_op jit(solution)/shard_map/ppermute | solution.py:300
  91.8 1.2 %product.3 = f32[96,576]{1,0:T(8,128)S(1)} custom-call(s32[3]{0:T(128)S(1)} %pad_add_fusion.place_ref, bf16[32,32,128]{2,1,0:T(8,128)(2,1)S(1)} %collective-permute-done.5.polar_ref, bf16[3,48,1152]{2,1,0:T(8,128)(2,1)S(1)} %pad_maximum_fusion.refs_0_, bf16[3,48,1152]{2,1,0:T(8,128)(2,1)S(1)} %collective-permute-done.2.refs_1_, ...), custom_call_target="tpu_custom_call" | custom-call | tf_op jit(solution)/shard_map/product/pallas_call | solution.py:268
  93.0 2.3 %collective-permute-start.6 = (f32[96,576]{1,0:T(8,128)S(1)}, f32[96,576]{1,0:T(8,128)S(1)}, u32[]{:S(2)}, u32[]{:S(2)}) collective-permute-start(f32[96,576]{1,0:T(8,128)S(1)} %product.3), channel_id=1, source_target_pairs={{1,0},{0,1},{3,2},{2,3},{5,4},{4,5},{7,6},{6,7},{9,8},{8,9},{11,10... | collective-permute-start | bytes 663560 | tf_op jit(solution)/shard_map/ppermute | solution.py:300
  95.3 1.2 %product.2.mine_ref = f32[96,576]{1,0:T(8,128)S(1)} custom-call(s32[3]{0:T(128)S(1)} %pad_add_fusion.place_ref, bf16[32,32,128]{2,1,0:T(8,128)(2,1)S(1)} %all-to-all-done.1.polar_ref, bf16[3,48,1152]{2,1,0:T(8,128)(2,1)S(1)} %pad_maximum_fusion.refs_0_, bf16[3,48,1152]{2,1,0:T(8,128)(2,1)S(1)} %collective-permute-done.2.refs_1_, ...), custom_call_target="tpu_custom_call" | custom-call | tf_op jit(solution)/shard_map/product/pallas_call | solution.py:268
  96.5 0.0 collective-permute-done.6.other_ref
  96.5 1.7 %merge.1 = f32[864,128]{1,0:T(8,128)} custom-call(s32[3]{0:T(128)S(1)} %pad_add_fusion.place_ref, f32[96,576]{1,0:T(8,128)S(1)} %product.2.mine_ref, f32[96,576]{1,0:T(8,128)S(1)} %collective-permute-done.6.other_ref), custom_call_target="tpu_custom_call" | custom-call | tf_op jit(solution)/shard_map/merge/pallas_call | solution.py:282
  (7 shorter events, 0.1 us)
Async XLA Ops:
  39.8 17.3 %copy-start = (bf16[512,256]{1,0:T(8,128)(2,1)S(1)}, bf16[512,256]{1,0:T(8,128)(2,1)}, u32[]{:S(2)}) copy-start(bf16[512,256]{1,0:T(8,128)(2,1)} %constant.21.clone.matrices_ref) | copy-start | bytes 786436
  39.8 17.3 %copy-start.1 = (f32[128,128]{1,0:T(8,128)S(1)}, f32[128,128]{1,0:T(8,128)}, u32[]{:S(2)}) copy-start(f32[128,128]{1,0:T(8,128)} %constant.22.clone.twiddle_ref) | copy-start | bytes 196612
  40.2 20.4 %collective-permute-start.1 = (bf16[48,1152]{1,0:T(8,128)(2,1)S(1)}, bf16[48,1152]{1,0:T(8,128)(2,1)S(1)}, u32[]{:S(2)}, u32[]{:S(2)}) collective-permute-start(bf16[48,1152]{1,0:T(8,128)(2,1)S(1)} %unpack.1), channel_id=1, source_target_pairs={{16,0},{17,1},{18,2},{19,3},{20,4},{21,5},{22,6},{23,7},{0,8},{1,9... | collective-permute-start | bytes 331784 | tf_op jit(solution)/shard_map/ppermute | solution.py:300
  55.2 5.9 %collective-permute-start = (bf16[48,1152]{1,0:T(8,128)(2,1)S(1)}, bf16[48,1152]{1,0:T(8,128)(2,1)S(1)}, u32[]{:S(2)}, u32[]{:S(2)}) collective-permute-start(bf16[48,1152]{1,0:T(8,128)(2,1)S(1)} %unpack.1), channel_id=1, source_target_pairs={{8,0},{9,1},{10,2},{11,3},{12,4},{13,5},{14,6},{15,7},{16,8},{17,9... | collective-permute-start | bytes 331784 | tf_op jit(solution)/shard_map/ppermute | solution.py:300
  61.1 21.7 %all-to-all-start.1 = ((bf16[32,32,128]{2,1,0:T(8,128)(2,1)}), bf16[32,32,128]{2,1,0:T(8,128)(2,1)S(1)}, u32[]{:S(2)}, u32[]{:S(2)}) async-start(bf16[32,32,128]{2,1,0:T(8,128)(2,1)} %correlate.1), calls=%async_computation.1 | async-start | bytes 524288 | tf_op jit(solution)/shard_map/all_to_all | solution.py:316
  68.6 22.2 %collective-permute-start.4 = (bf16[3,48,1152]{2,1,0:T(8,128)(2,1)S(1)}, bf16[3,48,1152]{2,1,0:T(8,128)(2,1)S(1)}, u32[]{:S(2)}, u32[]{:S(2)}) collective-permute-start(bf16[3,48,1152]{2,1,0:T(8,128)(2,1)S(1)} %pad_maximum_fusion.refs_0_), channel_id=1, source_target_pairs={{4,0},{5,1},{6,2},{7,3},{0,4},{1,5},{2,6},{3,7},{12,8},{13,9},{14,... | collective-permute-start | bytes 995336 | tf_op jit(solution)/shard_map/ppermute | solution.py:300
  73.2 17.6 %collective-permute-start.3 = (bf16[3,48,1152]{2,1,0:T(8,128)(2,1)S(1)}, bf16[3,48,1152]{2,1,0:T(8,128)(2,1)S(1)}, u32[]{:S(2)}, u32[]{:S(2)}) collective-permute-start(bf16[3,48,1152]{2,1,0:T(8,128)(2,1)S(1)} %pad_maximum_fusion.refs_0_), channel_id=1, source_target_pairs={{6,0},{7,1},{0,2},{1,3},{2,4},{3,5},{4,6},{5,7},{14,8},{15,9},{8,1... | collective-permute-start | bytes 995336 | tf_op jit(solution)/shard_map/ppermute | solution.py:300
  75.5 15.3 %collective-permute-start.2 = (bf16[3,48,1152]{2,1,0:T(8,128)(2,1)S(1)}, bf16[3,48,1152]{2,1,0:T(8,128)(2,1)S(1)}, u32[]{:S(2)}, u32[]{:S(2)}) collective-permute-start(bf16[3,48,1152]{2,1,0:T(8,128)(2,1)S(1)} %pad_maximum_fusion.refs_0_), channel_id=1, source_target_pairs={{2,0},{3,1},{4,2},{5,3},{6,4},{7,5},{0,6},{1,7},{10,8},{11,9},{12,... | collective-permute-start | bytes 995336 | tf_op jit(solution)/shard_map/ppermute | solution.py:300
  82.8 9.1 %collective-permute-start.5 = (bf16[32,32,128]{2,1,0:T(8,128)(2,1)S(1)}, bf16[32,32,128]{2,1,0:T(8,128)(2,1)S(1)}, u32[]{:S(2)}, u32[]{:S(2)}) collective-permute-start(bf16[32,32,128]{2,1,0:T(8,128)(2,1)S(1)} %all-to-all-done.1.polar_ref), channel_id=1, source_target_pairs={{1,0},{0,1},{3,2},{2,3},{5,4},{4,5},{7,6},{6,7},{9,8},{8,9},{11,10... | collective-permute-start | bytes 786440 | tf_op jit(solution)/shard_map/ppermute | solution.py:300
  93.0 3.5 %collective-permute-start.6 = (f32[96,576]{1,0:T(8,128)S(1)}, f32[96,576]{1,0:T(8,128)S(1)}, u32[]{:S(2)}, u32[]{:S(2)}) collective-permute-start(f32[96,576]{1,0:T(8,128)S(1)} %product.3), channel_id=1, source_target_pairs={{1,0},{0,1},{3,2},{2,3},{5,4},{4,5},{7,6},{6,7},{9,8},{8,9},{11,10... | collective-permute-start | bytes 663560 | tf_op jit(solution)/shard_map/ppermute | solution.py:300

commit v4 on v2

--- a/solution.py
+++ b/solution.py
@@ -13,7 +13,7 @@
 LANES = 128
 RADIX = 8
 RUN, ACROSS, CORES = 3, 4, 2
-HOPS = (0, 2, 1, 3)
+HOPS = (0, 1, 3, 2)
 HALF = math.sqrt(0.5)
 COULOMB_SCALE = float(2**18)
 SCALE = 4096.0
@@ -78,19 +78,19 @@
         out_ref[group * extra:(group + 1) * extra, :] = row.astype(jnp.bfloat16)
 
 
-def correlate_kernel(x_ref, high_ref, low_ref, twiddle_ref, out_ref, total_ref, spread_ref):
+def correlate_kernel(x_ref, matrices_ref, twiddle_ref, out_ref, total_ref, spread_ref):
     sources, here, lanes = x_ref.shape[0], x_ref.shape[1] // 5, x_ref.shape[2]
-    points = high_ref.shape[0] // 2
+    rows = matrices_ref.shape[1]
+    points = rows // 2
     pieces = sources * here // points
     per_piece = sources // pieces
-    high, low = high_ref[...], low_ref[...]
+    matrices = matrices_ref[...]
 
     def dft(re, im):
         x = jnp.concatenate([re, im], axis=0)
         x_high, x_low = split(x)
-        y = jnp.dot(high, x_high, preferred_element_type=jnp.float32)
-        y += jnp.dot(high, x_low, preferred_element_type=jnp.float32)
-        return y + jnp.dot(low, x_high, preferred_element_type=jnp.float32)
+        both = jnp.dot(matrices, x_high, preferred_element_type=jnp.float32)
+        return both[:rows] + both[rows:] + jnp.dot(matrices[:rows], x_low, preferred_element_type=jnp.float32)
 
     def piece(which, part, j):
         at = (which * 2 + part) * here
@@ -197,7 +197,7 @@
     for r in range(RADIX):
         turned = np.arange(points) * r * (np.pi / energies)
         twiddle[:, 2 * r], twiddle[:, 2 * r + 1] = np.cos(turned), -np.sin(turned)
-    return high, low, twiddle
+    return np.concatenate([high, low]), twiddle
 
 
 def rows_view(x):
@@ -235,7 +235,7 @@
     owners, here, lanes = x.shape[0], x.shape[1] // 5, x.shape[2]
     energies = owners * here
     points = energies * 2 // RADIX
-    high, low, twiddle = tables(energies)
+    matrices, twiddle = tables(energies)
     return pl.pallas_call(
         correlate_kernel,
         out_shape=jax.ShapeDtypeStruct((owners, 2 * here, lanes), jnp.bfloat16),
@@ -248,7 +248,7 @@
             flops=RADIX * 3 * 2 * (2 * points) ** 2 * 3 * lanes, bytes_accessed=x.size * 4 + x.size, transcendentals=0
         ),
         name="correlate",
-    )(x, jnp.asarray(high), jnp.asarray(low), jnp.asarray(twiddle))
+    )(x, jnp.asarray(matrices), jnp.asarray(twiddle))
 
 
 def screen(polar, runs, place, shape):

time: 98.6 us -> 97.8 us (level)
  the two profiles are of different devices: /device:TPU:7 before, /device:TPU:1 now
where the time goes in v4:
time: 97.8 us; the launch traced here: 97.4 us
  starting transfers between devices  49.2 us (50%)
  blocking collectives  38.1 us (39%)
  Pallas kernels  7.53 us (8%)
  waiting for transfers between devices  2.04 us (2%)
    ppermute x9, starting transfers between devices, moved(): return lax.ppermute(x, 'col', [(source(at), at) for at in range(sharers)])  41.7 us
    all_to_all x1, blocking collectives, per_device(): lax.all_to_all(packed.astype(jnp.float16), 'energy', split_axis=0, concat...  38.1 us
    all_to_all x1, starting transfers between devices, per_device(): lax.all_to_all(polar, 'energy', split_axis=0, concat_axis=0, tiled=True)  7.45 us
    pallas_call x1, Pallas kernels, correlate(): pl.pallas_call(correlate_kernel, out_shape=jax.ShapeDtypeStruct((owners,...  3.42 us
    pallas_call x1, Pallas kernels, screen(): pl.pallas_call(screen_kernel, out_shape=jax.ShapeDtypeStruct((energies *...  2.43 us
    ppermute x9, waiting for transfers between devices, moved(): return lax.ppermute(x, 'col', [(source(at), at) for at in range(sharers)])  2.04 us
  transfers between devices with their start and end apart: 10, of which 2 were waited for; matrix products, arithmetic and copies ran while one was open for 0% of the time, Pallas kernels for 4%

profile of v4, /device:TPU:1, one launch (start us, length us, event | category | flops | bytes accessed | tf_op | source)
XLA Modules:
  0.0 97.4 jit_solution(13893978691097121577)
XLA Ops:
  0.0 1.4 %pack.1 = f32[32,80,128]{2,1,0:T(8,128)S(1)} custom-call(f32[864,128]{1,0:T(8,128)} %bitcast.24, f32[864,128]{1,0:T(8,128)} %bitcast.25, bf16[36,48]{1,0:T(8,128)(2,1)} %coulomb_hbm.1), custom_call_target="tpu_custom_call" | custom-call | tf_op jit(solution)/shard_map/pack/pallas_call | solution.py:213
  1.4 0.1 convert_element_type.6
  1.5 38.1 %all_to_all.10 = f16[32,80,128]{2,1,0:T(8,128)(2,1)S(1)} all-to-all(f16[32,80,128]{2,1,0:T(8,128)(2,1)S(1)} %convert_element_type.6), channel_id=1, replica_groups=mesh['energy'=32,'col'=24] {'energy'}, dimensions={0} | all-to-all | bytes 1310720 | tf_op jit(solution)/shard_map/all_to_all | solution.py:285
  39.6 0.1 convert_element_type.7.x_ref
  39.7 0.3 unpack.1
  40.0 15.0 %collective-permute-start.1 = (bf16[48,1152]{1,0:T(8,128)(2,1)S(1)}, bf16[48,1152]{1,0:T(8,128)(2,1)S(1)}, u32[]{:S(2)}, u32[]{:S(2)}) collective-permute-start(bf16[48,1152]{1,0:T(8,128)(2,1)S(1)} %unpack.1), channel_id=1, source_target_pairs={{16,0},{17,1},{18,2},{19,3},{20,4},{21,5},{22,6},{23,7},{0,8},{1,9... | collective-permute-start | bytes 331784 | tf_op jit(solution)/shard_map/ppermute | solution.py:277
  55.0 1.9 %collective-permute-start = (bf16[48,1152]{1,0:T(8,128)(2,1)S(1)}, bf16[48,1152]{1,0:T(8,128)(2,1)S(1)}, u32[]{:S(2)}, u32[]{:S(2)}) collective-permute-start(bf16[48,1152]{1,0:T(8,128)(2,1)S(1)} %unpack.1), channel_id=1, source_target_pairs={{8,0},{9,1},{10,2},{11,3},{12,4},{13,5},{14,6},{15,7},{16,8},{17,9... | collective-permute-start | bytes 331784 | tf_op jit(solution)/shard_map/ppermute | solution.py:277
  57.0 3.4 %correlate.1 = bf16[32,32,128]{2,1,0:T(8,128)(2,1)} custom-call(f32[32,80,128]{2,1,0:T(8,128)S(1)} %convert_element_type.7.x_ref, bf16[512,256]{1,0:T(8,128)(2,1)S(1)} %copy-done, f32[128,128]{1,0:T(8,128)S(1)} %copy-done.1), custom_call_target="tpu_custom_call" | custom-call | flops 1207959552 | bytes 1638400 | tf_op jit(solution)/shard_map/correlate/pallas_call | solution.py:239
  60.4 0.0 collective-permute-done.1
  60.4 0.5 collective-permute-done
  61.0 7.5 %all-to-all-start.1 = ((bf16[32,32,128]{2,1,0:T(8,128)(2,1)}), bf16[32,32,128]{2,1,0:T(8,128)(2,1)S(1)}, u32[]{:S(2)}, u32[]{:S(2)}) async-start(bf16[32,32,128]{2,1,0:T(8,128)(2,1)} %correlate.1), calls=%async_computation.1 | async-start | bytes 524288 | tf_op jit(solution)/shard_map/all_to_all | solution.py:294
  68.4 4.6 %collective-permute-start.4 = (bf16[3,48,1152]{2,1,0:T(8,128)(2,1)S(1)}, bf16[3,48,1152]{2,1,0:T(8,128)(2,1)S(1)}, u32[]{:S(2)}, u32[]{:S(2)}) collective-permute-start(bf16[3,48,1152]{2,1,0:T(8,128)(2,1)S(1)} %pad_maximum_fusion.refs_0_), channel_id=1, source_target_pairs={{4,0},{5,1},{6,2},{7,3},{0,4},{1,5},{2,6},{3,7},{12,8},{13,9},{14,... | collective-permute-start | bytes 995336 | tf_op jit(solution)/shard_map/ppermute | solution.py:277
  73.1 2.2 %collective-permute-start.3 = (bf16[3,48,1152]{2,1,0:T(8,128)(2,1)S(1)}, bf16[3,48,1152]{2,1,0:T(8,128)(2,1)S(1)}, u32[]{:S(2)}, u32[]{:S(2)}) collective-permute-start(bf16[3,48,1152]{2,1,0:T(8,128)(2,1)S(1)} %pad_maximum_fusion.refs_0_), channel_id=1, source_target_pairs={{6,0},{7,1},{0,2},{1,3},{2,4},{3,5},{4,6},{5,7},{14,8},{15,9},{8,1... | collective-permute-start | bytes 995336 | tf_op jit(solution)/shard_map/ppermute | solution.py:277
  75.3 4.3 %collective-permute-start.2 = (bf16[3,48,1152]{2,1,0:T(8,128)(2,1)S(1)}, bf16[3,48,1152]{2,1,0:T(8,128)(2,1)S(1)}, u32[]{:S(2)}, u32[]{:S(2)}) collective-permute-start(bf16[3,48,1152]{2,1,0:T(8,128)(2,1)S(1)} %pad_maximum_fusion.refs_0_), channel_id=1, source_target_pairs={{2,0},{3,1},{4,2},{5,3},{6,4},{7,5},{0,6},{1,7},{10,8},{11,9},{12,... | collective-permute-start | bytes 995336 | tf_op jit(solution)/shard_map/ppermute | solution.py:277
  79.6 5.8 %collective-permute-start.5 = (bf16[3,48,1152]{2,1,0:T(8,128)(2,1)S(1)}, bf16[3,48,1152]{2,1,0:T(8,128)(2,1)S(1)}, u32[]{:S(2)}, u32[]{:S(2)}) collective-permute-start(bf16[3,48,1152]{2,1,0:T(8,128)(2,1)S(1)} %pad_maximum_fusion.refs_0_), channel_id=1, source_target_pairs={{1,0},{0,1},{3,2},{2,3},{5,4},{4,5},{7,6},{6,7},{9,8},{8,9},{11,10... | collective-permute-start | bytes 995336 | tf_op jit(solution)/shard_map/ppermute | solution.py:277
  85.4 0.0 collective-permute-done.4.refs_3_
  85.4 1.9 %collective-permute-start.8 = (bf16[3,48,1152]{2,1,0:T(8,128)(2,1)S(1)}, bf16[3,48,1152]{2,1,0:T(8,128)(2,1)S(1)}, u32[]{:S(2)}, u32[]{:S(2)}) collective-permute-start(bf16[3,48,1152]{2,1,0:T(8,128)(2,1)S(1)} %collective-permute-done.4.refs_3_), channel_id=1, source_target_pairs={{1,0},{0,1},{3,2},{2,3},{5,4},{4,5},{7,6},{6,7},{9,8},{8,9},{11,10... | collective-permute-start | bytes 995336 | tf_op jit(solution)/shard_map/ppermute | solution.py:277
  87.4 4.0 %collective-permute-start.7 = (bf16[3,48,1152]{2,1,0:T(8,128)(2,1)S(1)}, bf16[3,48,1152]{2,1,0:T(8,128)(2,1)S(1)}, u32[]{:S(2)}, u32[]{:S(2)}) collective-permute-start(bf16[3,48,1152]{2,1,0:T(8,128)(2,1)S(1)} %collective-permute-done.3.refs_2_), channel_id=1, source_target_pairs={{1,0},{0,1},{3,2},{2,3},{5,4},{4,5},{7,6},{6,7},{9,8},{8,9},{11,10... | collective-permute-start | bytes 995336 | tf_op jit(solution)/shard_map/ppermute | solution.py:277
  91.4 0.0 collective-permute-done.2.refs_1_
  91.4 1.9 %collective-permute-start.6 = (bf16[3,48,1152]{2,1,0:T(8,128)(2,1)S(1)}, bf16[3,48,1152]{2,1,0:T(8,128)(2,1)S(1)}, u32[]{:S(2)}, u32[]{:S(2)}) collective-permute-start(bf16[3,48,1152]{2,1,0:T(8,128)(2,1)S(1)} %collective-permute-done.2.refs_1_), channel_id=1, source_target_pairs={{1,0},{0,1},{3,2},{2,3},{5,4},{4,5},{7,6},{6,7},{9,8},{8,9},{11,10... | collective-permute-start | bytes 995336 | tf_op jit(solution)/shard_map/ppermute | solution.py:277
  93.4 0.1 pad_add_fusion.place_ref
  93.4 0.0 collective-permute-done.5.refs_4_
  93.4 1.5 %collective-permute-done.6.refs_5_ = bf16[3,48,1152]{2,1,0:T(8,128)(2,1)S(1)} collective-permute-done((bf16[3,48,1152]{2,1,0:T(8,128)(2,1)S(1)}, bf16[3,48,1152]{2,1,0:T(8,128)(2,1)S(1)}, u32[]{:S(2)}, u32[]{:S(2)}) %collective-permute-start.6) | collective-permute-done | bytes 331808 | tf_op jit(solution)/shard_map/ppermute | solution.py:277
  94.9 2.4 %screen.1 = f32[864,128]{1,0:T(8,128)} custom-call(s32[3]{0:T(128)S(1)} %pad_add_fusion.place_ref, bf16[32,32,128]{2,1,0:T(8,128)(2,1)S(1)} %all-to-all-done.1.polar_ref, bf16[3,48,1152]{2,1,0:T(8,128)(2,1)S(1)} %pad_maximum_fusion.refs_0_, bf16[3,48,1152]{2,1,0:T(8,128)(2,1)S(1)} %collective-permute-done.2.refs_1_, ...), custom_call_target="tpu_custom_call" | custom-call | tf_op jit(solution)/shard_map/screen/pallas_call | solution.py:257
  (9 shorter events, 0.1 us)
Async XLA Ops:
  39.6 17.3 %copy-start = (bf16[512,256]{1,0:T(8,128)(2,1)S(1)}, bf16[512,256]{1,0:T(8,128)(2,1)}, u32[]{:S(2)}) copy-start(bf16[512,256]{1,0:T(8,128)(2,1)} %constant.21.clone.matrices_ref) | copy-start | bytes 786436
  39.6 17.3 %copy-start.1 = (f32[128,128]{1,0:T(8,128)S(1)}, f32[128,128]{1,0:T(8,128)}, u32[]{:S(2)}) copy-start(f32[128,128]{1,0:T(8,128)} %constant.22.clone.twiddle_ref) | copy-start | bytes 196612
  40.0 20.4 %collective-permute-start.1 = (bf16[48,1152]{1,0:T(8,128)(2,1)S(1)}, bf16[48,1152]{1,0:T(8,128)(2,1)S(1)}, u32[]{:S(2)}, u32[]{:S(2)}) collective-permute-start(bf16[48,1152]{1,0:T(8,128)(2,1)S(1)} %unpack.1), channel_id=1, source_target_pairs={{16,0},{17,1},{18,2},{19,3},{20,4},{21,5},{22,6},{23,7},{0,8},{1,9... | collective-permute-start | bytes 331784 | tf_op jit(solution)/shard_map/ppermute | solution.py:277
  55.0 5.9 %collective-permute-start = (bf16[48,1152]{1,0:T(8,128)(2,1)S(1)}, bf16[48,1152]{1,0:T(8,128)(2,1)S(1)}, u32[]{:S(2)}, u32[]{:S(2)}) collective-permute-start(bf16[48,1152]{1,0:T(8,128)(2,1)S(1)} %unpack.1), channel_id=1, source_target_pairs={{8,0},{9,1},{10,2},{11,3},{12,4},{13,5},{14,6},{15,7},{16,8},{17,9... | collective-permute-start | bytes 331784 | tf_op jit(solution)/shard_map/ppermute | solution.py:277
  61.0 33.9 %all-to-all-start.1 = ((bf16[32,32,128]{2,1,0:T(8,128)(2,1)}), bf16[32,32,128]{2,1,0:T(8,128)(2,1)S(1)}, u32[]{:S(2)}, u32[]{:S(2)}) async-start(bf16[32,32,128]{2,1,0:T(8,128)(2,1)} %correlate.1), calls=%async_computation.1 | async-start | bytes 524288 | tf_op jit(solution)/shard_map/all_to_all | solution.py:294
  68.4 17.0 %collective-permute-start.4 = (bf16[3,48,1152]{2,1,0:T(8,128)(2,1)S(1)}, bf16[3,48,1152]{2,1,0:T(8,128)(2,1)S(1)}, u32[]{:S(2)}, u32[]{:S(2)}) collective-permute-start(bf16[3,48,1152]{2,1,0:T(8,128)(2,1)S(1)} %pad_maximum_fusion.refs_0_), channel_id=1, source_target_pairs={{4,0},{5,1},{6,2},{7,3},{0,4},{1,5},{2,6},{3,7},{12,8},{13,9},{14,... | collective-permute-start | bytes 995336 | tf_op jit(solution)/shard_map/ppermute | solution.py:277
  73.1 14.3 %collective-permute-start.3 = (bf16[3,48,1152]{2,1,0:T(8,128)(2,1)S(1)}, bf16[3,48,1152]{2,1,0:T(8,128)(2,1)S(1)}, u32[]{:S(2)}, u32[]{:S(2)}) collective-permute-start(bf16[3,48,1152]{2,1,0:T(8,128)(2,1)S(1)} %pad_maximum_fusion.refs_0_), channel_id=1, source_target_pairs={{6,0},{7,1},{0,2},{1,3},{2,4},{3,5},{4,6},{5,7},{14,8},{15,9},{8,1... | collective-permute-start | bytes 995336 | tf_op jit(solution)/shard_map/ppermute | solution.py:277
  75.3 16.1 %collective-permute-start.2 = (bf16[3,48,1152]{2,1,0:T(8,128)(2,1)S(1)}, bf16[3,48,1152]{2,1,0:T(8,128)(2,1)S(1)}, u32[]{:S(2)}, u32[]{:S(2)}) collective-permute-start(bf16[3,48,1152]{2,1,0:T(8,128)(2,1)S(1)} %pad_maximum_fusion.refs_0_), channel_id=1, source_target_pairs={{2,0},{3,1},{4,2},{5,3},{6,4},{7,5},{0,6},{1,7},{10,8},{11,9},{12,... | collective-permute-start | bytes 995336 | tf_op jit(solution)/shard_map/ppermute | solution.py:277
  79.6 13.8 %collective-permute-start.5 = (bf16[3,48,1152]{2,1,0:T(8,128)(2,1)S(1)}, bf16[3,48,1152]{2,1,0:T(8,128)(2,1)S(1)}, u32[]{:S(2)}, u32[]{:S(2)}) collective-permute-start(bf16[3,48,1152]{2,1,0:T(8,128)(2,1)S(1)} %pad_maximum_fusion.refs_0_), channel_id=1, source_target_pairs={{1,0},{0,1},{3,2},{2,3},{5,4},{4,5},{7,6},{6,7},{9,8},{8,9},{11,10... | collective-permute-start | bytes 995336 | tf_op jit(solution)/shard_map/ppermute | solution.py:277
  85.4 8.0 %collective-permute-start.8 = (bf16[3,48,1152]{2,1,0:T(8,128)(2,1)S(1)}, bf16[3,48,1152]{2,1,0:T(8,128)(2,1)S(1)}, u32[]{:S(2)}, u32[]{:S(2)}) collective-permute-start(bf16[3,48,1152]{2,1,0:T(8,128)(2,1)S(1)} %collective-permute-done.4.refs_3_), channel_id=1, source_target_pairs={{1,0},{0,1},{3,2},{2,3},{5,4},{4,5},{7,6},{6,7},{9,8},{8,9},{11,10... | collective-permute-start | bytes 995336 | tf_op jit(solution)/shard_map/ppermute | solution.py:277
  87.4 6.1 %collective-permute-start.7 = (bf16[3,48,1152]{2,1,0:T(8,128)(2,1)S(1)}, bf16[3,48,1152]{2,1,0:T(8,128)(2,1)S(1)}, u32[]{:S(2)}, u32[]{:S(2)}) collective-permute-start(bf16[3,48,1152]{2,1,0:T(8,128)(2,1)S(1)} %collective-permute-done.3.refs_2_), channel_id=1, source_target_pairs={{1,0},{0,1},{3,2},{2,3},{5,4},{4,5},{7,6},{6,7},{9,8},{8,9},{11,10... | collective-permute-start | bytes 995336 | tf_op jit(solution)/shard_map/ppermute | solution.py:277
  91.4 3.5 %collective-permute-start.6 = (bf16[3,48,1152]{2,1,0:T(8,128)(2,1)S(1)}, bf16[3,48,1152]{2,1,0:T(8,128)(2,1)S(1)}, u32[]{:S(2)}, u32[]{:S(2)}) collective-permute-start(bf16[3,48,1152]{2,1,0:T(8,128)(2,1)S(1)} %collective-permute-done.2.refs_1_), channel_id=1, source_target_pairs={{1,0},{0,1},{3,2},{2,3},{5,4},{4,5},{7,6},{6,7},{9,8},{8,9},{11,10... | collective-permute-start | bytes 995336 | tf_op jit(solution)/shard_map/ppermute | solution.py:277

commit v5 on v4

--- a/solution.py
+++ b/solution.py
@@ -12,6 +12,7 @@
 
 LANES = 128
 RADIX = 8
+APART = 4
 RUN, ACROSS, CORES = 3, 4, 2
 HOPS = (0, 1, 3, 2)
 HALF = math.sqrt(0.5)
@@ -154,6 +155,10 @@
             )
 
 
+def lies(owner, owners):
+    return owner % APART * (owners // APART) + owner // APART
+
+
 def screen_kernel(place_ref, polar_ref, *refs):
     *run_refs, out_ref, coulomb_ref = refs
     run, wide, order = run_refs[0].shape
@@ -169,7 +174,8 @@
             coulomb_ref[chip * CORES + core] = run_refs[at][hop]
             coulomb_ref[chip * CORES + 1 - core] = run_refs[across + at][hop]
     rows = [
-        jnp.concatenate([polar_ref[c * groups + k] for k in range(groups)], axis=1) for c in range(columns)
+        jnp.concatenate([polar_ref[lies(c * groups + k, polar_ref.shape[0])] for k in range(groups)], axis=1)
+        for c in range(columns)
     ]
     product = lax.dot_general(
         jnp.concatenate(rows, axis=0),
@@ -277,6 +283,14 @@
     return lax.ppermute(x, "col", [(source(at), at) for at in range(sharers)])
 
 
+def same_z(owners):
+    return [[y * APART + z for y in range(owners // APART)] for z in range(APART)]
+
+
+def same_y(owners):
+    return [[y * APART + z for z in range(APART)] for y in range(owners // APART)]
+
+
 def per_device(lesser, greater_transposed, coulomb):
     owners = lax.axis_size("energy")
     sharers = lax.axis_size("col")
@@ -291,7 +305,9 @@
     run, polar = lax.optimization_barrier((run, polar))
     runs = [run] + [moved(run, sharers, (0, hop, 0)) for hop in HOPS[1:]]
     runs += [moved(run, sharers, (0, 0, 1)) for run in runs]
-    polar = lax.all_to_all(polar, "energy", split_axis=0, concat_axis=0, tiled=True)
+    polar = lax.all_to_all(polar, "energy", split_axis=0, concat_axis=0, axis_index_groups=same_z(owners), tiled=True)
+    polar = polar.reshape((owners // APART, APART) + polar.shape[1:]).swapaxes(0, 1).reshape(polar.shape)
+    polar = lax.all_to_all(polar, "energy", split_axis=0, concat_axis=0, axis_index_groups=same_y(owners), tiled=True)
     at = lax.axis_index("col")
     place = [lax.div(at, ACROSS * CORES), lax.rem(lax.div(at, CORES), ACROSS), lax.rem(at, CORES)]
     return screen(polar, runs, jnp.stack(place).astype(jnp.int32), lesser.shape)

time: 97.8 us -> 102 us (1.043)
  the two profiles are of different devices: /device:TPU:1 before, /device:TPU:8 now
where the time goes in v5:
time: 102 us; the launch traced here: 101 us
  starting transfers between devices  46.7 us (46%)
  blocking collectives  40.4 us (40%)
  Pallas kernels  7.52 us (7%)
  waiting for transfers between devices  5.24 us (5%)
    all_to_all x1, blocking collectives, per_device(): lax.all_to_all(packed.astype(jnp.float16), 'energy', split_axis=0, concat...  40.4 us
    ppermute x9, starting transfers between devices, moved(): return lax.ppermute(x, 'col', [(source(at), at) for at in range(sharers)])  37.5 us
    all_to_all x2, starting transfers between devices, per_device(): lax.all_to_all(polar, 'energy', split_axis=0, concat_axis=0, axis_index_g...  9.15 us
    pallas_call x1, Pallas kernels, correlate(): pl.pallas_call(correlate_kernel, out_shape=jax.ShapeDtypeStruct((owners,...  3.41 us
    all_to_all x2, waiting for transfers between devices, per_device(): lax.all_to_all(polar, 'energy', split_axis=0, concat_axis=0, axis_index_g...  3.25 us
    pallas_call x1, Pallas kernels, screen(): pl.pallas_call(screen_kernel, out_shape=jax.ShapeDtypeStruct((energies *...  2.43 us
  transfers between devices with their start and end apart: 11, of which 3 were waited for; matrix products, arithmetic and copies ran while one was open for 1% of the time, Pallas kernels for 3%

profile of v5, /device:TPU:8, one launch (start us, length us, event | category | flops | bytes accessed | tf_op | source)
XLA Modules:
  0.0 101.0 jit_solution(6409163405764570447)
XLA Ops:
  0.0 1.4 %pack.1 = f32[32,80,128]{2,1,0:T(8,128)S(1)} custom-call(f32[864,128]{1,0:T(8,128)} %bitcast.29, f32[864,128]{1,0:T(8,128)} %bitcast.30, bf16[36,48]{1,0:T(8,128)(2,1)} %coulomb_hbm.1), custom_call_target="tpu_custom_call" | custom-call | tf_op jit(solution)/shard_map/pack/pallas_call | solution.py:219
  1.4 0.1 convert_element_type.6
  1.5 40.4 %all_to_all.15 = f16[32,80,128]{2,1,0:T(8,128)(2,1)S(1)} all-to-all(f16[32,80,128]{2,1,0:T(8,128)(2,1)S(1)} %convert_element_type.6), channel_id=1, replica_groups=mesh['energy'=32,'col'=24] {'energy'}, dimensions={0} | all-to-all | bytes 1310720 | tf_op jit(solution)/shard_map/all_to_all | solution.py:299
  41.9 0.1 convert_element_type.7.x_ref
  42.0 0.3 unpack.1
  42.3 14.5 %collective-permute-start.1 = (bf16[48,1152]{1,0:T(8,128)(2,1)S(1)}, bf16[48,1152]{1,0:T(8,128)(2,1)S(1)}, u32[]{:S(2)}, u32[]{:S(2)}) collective-permute-start(bf16[48,1152]{1,0:T(8,128)(2,1)S(1)} %unpack.1), channel_id=1, source_target_pairs={{16,0},{17,1},{18,2},{19,3},{20,4},{21,5},{22,6},{23,7},{0,8},{1,9... | collective-permute-start | bytes 331784 | tf_op jit(solution)/shard_map/ppermute | solution.py:283
  56.8 2.3 %collective-permute-start = (bf16[48,1152]{1,0:T(8,128)(2,1)S(1)}, bf16[48,1152]{1,0:T(8,128)(2,1)S(1)}, u32[]{:S(2)}, u32[]{:S(2)}) collective-permute-start(bf16[48,1152]{1,0:T(8,128)(2,1)S(1)} %unpack.1), channel_id=1, source_target_pairs={{8,0},{9,1},{10,2},{11,3},{12,4},{13,5},{14,6},{15,7},{16,8},{17,9... | collective-permute-start | bytes 331784 | tf_op jit(solution)/shard_map/ppermute | solution.py:283
  59.2 3.4 %correlate.1 = bf16[32,32,128]{2,1,0:T(8,128)(2,1)} custom-call(f32[32,80,128]{2,1,0:T(8,128)S(1)} %convert_element_type.7.x_ref, bf16[512,256]{1,0:T(8,128)(2,1)S(1)} %copy-done, f32[128,128]{1,0:T(8,128)S(1)} %copy-done.1), custom_call_target="tpu_custom_call" | custom-call | flops 1207959552 | bytes 1638400 | tf_op jit(solution)/shard_map/correlate/pallas_call | solution.py:245
  62.6 0.9 collective-permute-done
  63.5 3.8 %all-to-all-start.1 = ((bf16[32,32,128]{2,1,0:T(8,128)(2,1)}), bf16[32,32,128]{2,1,0:T(8,128)(2,1)S(1)}, u32[]{:S(2)}, u32[]{:S(2)}) async-start(bf16[32,32,128]{2,1,0:T(8,128)(2,1)} %correlate.1), calls=%async_computation.1 | async-start | bytes 524288 | tf_op jit(solution)/shard_map/all_to_all | solution.py:308
  67.3 4.9 %collective-permute-start.4 = (bf16[3,48,1152]{2,1,0:T(8,128)(2,1)S(1)}, bf16[3,48,1152]{2,1,0:T(8,128)(2,1)S(1)}, u32[]{:S(2)}, u32[]{:S(2)}) collective-permute-start(bf16[3,48,1152]{2,1,0:T(8,128)(2,1)S(1)} %pad_maximum_fusion.refs_0_), channel_id=1, source_target_pairs={{4,0},{5,1},{6,2},{7,3},{0,4},{1,5},{2,6},{3,7},{12,8},{13,9},{14,... | collective-permute-start | bytes 995336 | tf_op jit(solution)/shard_map/ppermute | solution.py:283
  72.2 2.5 %collective-permute-start.3 = (bf16[3,48,1152]{2,1,0:T(8,128)(2,1)S(1)}, bf16[3,48,1152]{2,1,0:T(8,128)(2,1)S(1)}, u32[]{:S(2)}, u32[]{:S(2)}) collective-permute-start(bf16[3,48,1152]{2,1,0:T(8,128)(2,1)S(1)} %pad_maximum_fusion.refs_0_), channel_id=1, source_target_pairs={{6,0},{7,1},{0,2},{1,3},{2,4},{3,5},{4,6},{5,7},{14,8},{15,9},{8,1... | collective-permute-start | bytes 995336 | tf_op jit(solution)/shard_map/ppermute | solution.py:283
  74.7 4.6 %collective-permute-start.2 = (bf16[3,48,1152]{2,1,0:T(8,128)(2,1)S(1)}, bf16[3,48,1152]{2,1,0:T(8,128)(2,1)S(1)}, u32[]{:S(2)}, u32[]{:S(2)}) collective-permute-start(bf16[3,48,1152]{2,1,0:T(8,128)(2,1)S(1)} %pad_maximum_fusion.refs_0_), channel_id=1, source_target_pairs={{2,0},{3,1},{4,2},{5,3},{6,4},{7,5},{0,6},{1,7},{10,8},{11,9},{12,... | collective-permute-start | bytes 995336 | tf_op jit(solution)/shard_map/ppermute | solution.py:283
  79.3 0.0 all-to-all-done.1
  79.3 0.7 copy.6
  80.0 5.3 %all-to-all-start.2 = ((bf16[32,32,128]{2,1,0:T(8,128)(2,1)}), bf16[32,32,128]{2,1,0:T(8,128)(2,1)S(1)}, u32[]{:S(2)}, u32[]{:S(2)}) async-start(bf16[32,32,128]{2,1,0:T(8,128)(2,1)} %bitcast.14), calls=%async_computation.2 | async-start | bytes 524288 | tf_op jit(solution)/shard_map/all_to_all | solution.py:310
  85.4 1.9 %collective-permute-start.5 = (bf16[3,48,1152]{2,1,0:T(8,128)(2,1)S(1)}, bf16[3,48,1152]{2,1,0:T(8,128)(2,1)S(1)}, u32[]{:S(2)}, u32[]{:S(2)}) collective-permute-start(bf16[3,48,1152]{2,1,0:T(8,128)(2,1)S(1)} %pad_maximum_fusion.refs_0_), channel_id=1, source_target_pairs={{1,0},{0,1},{3,2},{2,3},{5,4},{4,5},{7,6},{6,7},{9,8},{8,9},{11,10... | collective-permute-start | bytes 995336 | tf_op jit(solution)/shard_map/ppermute | solution.py:283
  87.3 2.4 %collective-permute-start.8 = (bf16[3,48,1152]{2,1,0:T(8,128)(2,1)S(1)}, bf16[3,48,1152]{2,1,0:T(8,128)(2,1)S(1)}, u32[]{:S(2)}, u32[]{:S(2)}) collective-permute-start(bf16[3,48,1152]{2,1,0:T(8,128)(2,1)S(1)} %collective-permute-done.4.refs_3_), channel_id=1, source_target_pairs={{1,0},{0,1},{3,2},{2,3},{5,4},{4,5},{7,6},{6,7},{9,8},{8,9},{11,10... | collective-permute-start | bytes 995336 | tf_op jit(solution)/shard_map/ppermute | solution.py:283
  89.7 1.9 %collective-permute-start.7 = (bf16[3,48,1152]{2,1,0:T(8,128)(2,1)S(1)}, bf16[3,48,1152]{2,1,0:T(8,128)(2,1)S(1)}, u32[]{:S(2)}, u32[]{:S(2)}) collective-permute-start(bf16[3,48,1152]{2,1,0:T(8,128)(2,1)S(1)} %collective-permute-done.3.refs_2_), channel_id=1, source_target_pairs={{1,0},{0,1},{3,2},{2,3},{5,4},{4,5},{7,6},{6,7},{9,8},{8,9},{11,10... | collective-permute-start | bytes 995336 | tf_op jit(solution)/shard_map/ppermute | solution.py:283
  91.7 2.4 %collective-permute-start.6 = (bf16[3,48,1152]{2,1,0:T(8,128)(2,1)S(1)}, bf16[3,48,1152]{2,1,0:T(8,128)(2,1)S(1)}, u32[]{:S(2)}, u32[]{:S(2)}) collective-permute-start(bf16[3,48,1152]{2,1,0:T(8,128)(2,1)S(1)} %collective-permute-done.2.refs_1_), channel_id=1, source_target_pairs={{1,0},{0,1},{3,2},{2,3},{5,4},{4,5},{7,6},{6,7},{9,8},{8,9},{11,10... | collective-permute-start | bytes 995336 | tf_op jit(solution)/shard_map/ppermute | solution.py:283
  94.1 0.1 pad_add_fusion.place_ref
  94.2 1.1 %collective-permute-done.6.refs_5_ = bf16[3,48,1152]{2,1,0:T(8,128)(2,1)S(1)} collective-permute-done((bf16[3,48,1152]{2,1,0:T(8,128)(2,1)S(1)}, bf16[3,48,1152]{2,1,0:T(8,128)(2,1)S(1)}, u32[]{:S(2)}, u32[]{:S(2)}) %collective-permute-start.6) | collective-permute-done | bytes 331808 | tf_op jit(solution)/shard_map/ppermute | solution.py:283
  95.3 3.2 %all-to-all-done.2.polar_ref = bf16[32,32,128]{2,1,0:T(8,128)(2,1)S(1)} async-done(((bf16[32,32,128]{2,1,0:T(8,128)(2,1)}), bf16[32,32,128]{2,1,0:T(8,128)(2,1)S(1)}, u32[]{:S(2)}, u32[]{:S(2)}) %all-to-all-start.2) | async-done | bytes 262176 | tf_op jit(solution)/shard_map/all_to_all | solution.py:310
  98.6 2.4 %screen.1 = f32[864,128]{1,0:T(8,128)} custom-call(s32[3]{0:T(128)S(1)} %pad_add_fusion.place_ref, bf16[32,32,128]{2,1,0:T(8,128)(2,1)S(1)} %all-to-all-done.2.polar_ref, bf16[3,48,1152]{2,1,0:T(8,128)(2,1)S(1)} %pad_maximum_fusion.refs_0_, bf16[3,48,1152]{2,1,0:T(8,128)(2,1)S(1)} %collective-permute-done.2.refs_1_, ...), custom_call_target="tpu_custom_call" | custom-call | tf_op jit(solution)/shard_map/screen/pallas_call | solution.py:263
  (12 shorter events, 0.1 us)
Async XLA Ops:
  41.9 17.3 %copy-start = (bf16[512,256]{1,0:T(8,128)(2,1)S(1)}, bf16[512,256]{1,0:T(8,128)(2,1)}, u32[]{:S(2)}) copy-start(bf16[512,256]{1,0:T(8,128)(2,1)} %constant.21.clone.matrices_ref) | copy-start | bytes 786436
  41.9 17.3 %copy-start.1 = (f32[128,128]{1,0:T(8,128)S(1)}, f32[128,128]{1,0:T(8,128)}, u32[]{:S(2)}) copy-start(f32[128,128]{1,0:T(8,128)} %constant.22.clone.twiddle_ref) | copy-start | bytes 196612
  42.3 20.3 %collective-permute-start.1 = (bf16[48,1152]{1,0:T(8,128)(2,1)S(1)}, bf16[48,1152]{1,0:T(8,128)(2,1)S(1)}, u32[]{:S(2)}, u32[]{:S(2)}) collective-permute-start(bf16[48,1152]{1,0:T(8,128)(2,1)S(1)} %unpack.1), channel_id=1, source_target_pairs={{16,0},{17,1},{18,2},{19,3},{20,4},{21,5},{22,6},{23,7},{0,8},{1,9... | collective-permute-start | bytes 331784 | tf_op jit(solution)/shard_map/ppermute | solution.py:283
  56.8 6.6 %collective-permute-start = (bf16[48,1152]{1,0:T(8,128)(2,1)S(1)}, bf16[48,1152]{1,0:T(8,128)(2,1)S(1)}, u32[]{:S(2)}, u32[]{:S(2)}) collective-permute-start(bf16[48,1152]{1,0:T(8,128)(2,1)S(1)} %unpack.1), channel_id=1, source_target_pairs={{8,0},{9,1},{10,2},{11,3},{12,4},{13,5},{14,6},{15,7},{16,8},{17,9... | collective-permute-start | bytes 331784 | tf_op jit(solution)/shard_map/ppermute | solution.py:283
  63.5 15.8 %all-to-all-start.1 = ((bf16[32,32,128]{2,1,0:T(8,128)(2,1)}), bf16[32,32,128]{2,1,0:T(8,128)(2,1)S(1)}, u32[]{:S(2)}, u32[]{:S(2)}) async-start(bf16[32,32,128]{2,1,0:T(8,128)(2,1)} %correlate.1), calls=%async_computation.1 | async-start | bytes 524288 | tf_op jit(solution)/shard_map/all_to_all | solution.py:308
  67.3 20.0 %collective-permute-start.4 = (bf16[3,48,1152]{2,1,0:T(8,128)(2,1)S(1)}, bf16[3,48,1152]{2,1,0:T(8,128)(2,1)S(1)}, u32[]{:S(2)}, u32[]{:S(2)}) collective-permute-start(bf16[3,48,1152]{2,1,0:T(8,128)(2,1)S(1)} %pad_maximum_fusion.refs_0_), channel_id=1, source_target_pairs={{4,0},{5,1},{6,2},{7,3},{0,4},{1,5},{2,6},{3,7},{12,8},{13,9},{14,... | collective-permute-start | bytes 995336 | tf_op jit(solution)/shard_map/ppermute | solution.py:283
  72.2 17.5 %collective-permute-start.3 = (bf16[3,48,1152]{2,1,0:T(8,128)(2,1)S(1)}, bf16[3,48,1152]{2,1,0:T(8,128)(2,1)S(1)}, u32[]{:S(2)}, u32[]{:S(2)}) collective-permute-start(bf16[3,48,1152]{2,1,0:T(8,128)(2,1)S(1)} %pad_maximum_fusion.refs_0_), channel_id=1, source_target_pairs={{6,0},{7,1},{0,2},{1,3},{2,4},{3,5},{4,6},{5,7},{14,8},{15,9},{8,1... | collective-permute-start | bytes 995336 | tf_op jit(solution)/shard_map/ppermute | solution.py:283
  74.7 16.9 %collective-permute-start.2 = (bf16[3,48,1152]{2,1,0:T(8,128)(2,1)S(1)}, bf16[3,48,1152]{2,1,0:T(8,128)(2,1)S(1)}, u32[]{:S(2)}, u32[]{:S(2)}) collective-permute-start(bf16[3,48,1152]{2,1,0:T(8,128)(2,1)S(1)} %pad_maximum_fusion.refs_0_), channel_id=1, source_target_pairs={{2,0},{3,1},{4,2},{5,3},{6,4},{7,5},{0,6},{1,7},{10,8},{11,9},{12,... | collective-permute-start | bytes 995336 | tf_op jit(solution)/shard_map/ppermute | solution.py:283
  80.0 18.5 %all-to-all-start.2 = ((bf16[32,32,128]{2,1,0:T(8,128)(2,1)}), bf16[32,32,128]{2,1,0:T(8,128)(2,1)S(1)}, u32[]{:S(2)}, u32[]{:S(2)}) async-start(bf16[32,32,128]{2,1,0:T(8,128)(2,1)} %bitcast.14), calls=%async_computation.2 | async-start | bytes 524288 | tf_op jit(solution)/shard_map/all_to_all | solution.py:310
  85.4 8.8 %collective-permute-start.5 = (bf16[3,48,1152]{2,1,0:T(8,128)(2,1)S(1)}, bf16[3,48,1152]{2,1,0:T(8,128)(2,1)S(1)}, u32[]{:S(2)}, u32[]{:S(2)}) collective-permute-start(bf16[3,48,1152]{2,1,0:T(8,128)(2,1)S(1)} %pad_maximum_fusion.refs_0_), channel_id=1, source_target_pairs={{1,0},{0,1},{3,2},{2,3},{5,4},{4,5},{7,6},{6,7},{9,8},{8,9},{11,10... | collective-permute-start | bytes 995336 | tf_op jit(solution)/shard_map/ppermute | solution.py:283
  87.3 6.9 %collective-permute-start.8 = (bf16[3,48,1152]{2,1,0:T(8,128)(2,1)S(1)}, bf16[3,48,1152]{2,1,0:T(8,128)(2,1)S(1)}, u32[]{:S(2)}, u32[]{:S(2)}) collective-permute-start(bf16[3,48,1152]{2,1,0:T(8,128)(2,1)S(1)} %collective-permute-done.4.refs_3_), channel_id=1, source_target_pairs={{1,0},{0,1},{3,2},{2,3},{5,4},{4,5},{7,6},{6,7},{9,8},{8,9},{11,10... | collective-permute-start | bytes 995336 | tf_op jit(solution)/shard_map/ppermute | solution.py:283
  89.7 4.5 %collective-permute-start.7 = (bf16[3,48,1152]{2,1,0:T(8,128)(2,1)S(1)}, bf16[3,48,1152]{2,1,0:T(8,128)(2,1)S(1)}, u32[]{:S(2)}, u32[]{:S(2)}) collective-permute-start(bf16[3,48,1152]{2,1,0:T(8,128)(2,1)S(1)} %collective-permute-done.3.refs_2_), channel_id=1, source_target_pairs={{1,0},{0,1},{3,2},{2,3},{5,4},{4,5},{7,6},{6,7},{9,8},{8,9},{11,10... | collective-permute-start | bytes 995336 | tf_op jit(solution)/shard_map/ppermute | solution.py:283
  91.7 3.7 %collective-permute-start.6 = (bf16[3,48,1152]{2,1,0:T(8,128)(2,1)S(1)}, bf16[3,48,1152]{2,1,0:T(8,128)(2,1)S(1)}, u32[]{:S(2)}, u32[]{:S(2)}) collective-permute-start(bf16[3,48,1152]{2,1,0:T(8,128)(2,1)S(1)} %collective-permute-done.2.refs_1_), channel_id=1, source_target_pairs={{1,0},{0,1},{3,2},{2,3},{5,4},{4,5},{7,6},{6,7},{9,8},{8,9},{11,10... | collective-permute-start | bytes 995336 | tf_op jit(solution)/shard_map/ppermute | solution.py:283

commit v6 on v4

--- a/solution.py
+++ b/solution.py
@@ -289,7 +289,8 @@
     run = jnp.stack([mine] + [moved(mine, sharers, (hop, 0, 0)) for hop in range(1, RUN)])
     polar = correlate(got)
     run, polar = lax.optimization_barrier((run, polar))
-    runs = [run] + [moved(run, sharers, (0, hop, 0)) for hop in HOPS[1:]]
+    ahead, behind = moved(run, sharers, (0, 1, 0)), moved(run, sharers, (0, ACROSS - 1, 0))
+    runs = [run, ahead, behind, moved(ahead, sharers, (0, 1, 0))]
     runs += [moved(run, sharers, (0, 0, 1)) for run in runs]
     polar = lax.all_to_all(polar, "energy", split_axis=0, concat_axis=0, tiled=True)
     at = lax.axis_index("col")

time: 97.8 us -> 96.8 us (0.990)
  no operation moved by 1% of the time
where the time goes in v6:
time: 96.8 us; the launch traced here: 96.3 us
  starting transfers between devices  48.5 us (50%)
  blocking collectives  38.1 us (39%)
  Pallas kernels  7.52 us (8%)
  waiting for transfers between devices  1.67 us (2%)
    ppermute x9, starting transfers between devices, moved(): return lax.ppermute(x, 'col', [(source(at), at) for at in range(sharers)])  41 us
    all_to_all x1, blocking collectives, per_device(): lax.all_to_all(packed.astype(jnp.float16), 'energy', split_axis=0, concat...  38.1 us
    all_to_all x1, starting transfers between devices, per_device(): lax.all_to_all(polar, 'energy', split_axis=0, concat_axis=0, tiled=True)  7.47 us
    pallas_call x1, Pallas kernels, correlate(): pl.pallas_call(correlate_kernel, out_shape=jax.ShapeDtypeStruct((owners,...  3.42 us
    pallas_call x1, Pallas kernels, screen(): pl.pallas_call(screen_kernel, out_shape=jax.ShapeDtypeStruct((energies *...  2.42 us
  transfers between devices with their start and end apart: 10, of which 2 were waited for; matrix products, arithmetic and copies ran while one was open for 0% of the time, Pallas kernels for 4%

profile of v6, /device:TPU:1, one launch (start us, length us, event | category | flops | bytes accessed | tf_op | source)
XLA Modules:
  0.0 96.3 jit_solution(18292102361030334905)
XLA Ops:
  0.0 1.4 %pack.1 = f32[32,80,128]{2,1,0:T(8,128)S(1)} custom-call(f32[864,128]{1,0:T(8,128)} %bitcast.24, f32[864,128]{1,0:T(8,128)} %bitcast.25, bf16[36,48]{1,0:T(8,128)(2,1)} %coulomb_hbm.1), custom_call_target="tpu_custom_call" | custom-call | tf_op jit(solution)/shard_map/pack/pallas_call | solution.py:213
  1.4 0.1 convert_element_type.6
  1.5 38.1 %all_to_all.10 = f16[32,80,128]{2,1,0:T(8,128)(2,1)S(1)} all-to-all(f16[32,80,128]{2,1,0:T(8,128)(2,1)S(1)} %convert_element_type.6), channel_id=1, replica_groups=mesh['energy'=32,'col'=24] {'energy'}, dimensions={0} | all-to-all | bytes 1310720 | tf_op jit(solution)/shard_map/all_to_all | solution.py:285
  39.6 0.1 convert_element_type.7.x_ref
  39.7 0.3 unpack.1
  40.0 15.0 %collective-permute-start.1 = (bf16[48,1152]{1,0:T(8,128)(2,1)S(1)}, bf16[48,1152]{1,0:T(8,128)(2,1)S(1)}, u32[]{:S(2)}, u32[]{:S(2)}) collective-permute-start(bf16[48,1152]{1,0:T(8,128)(2,1)S(1)} %unpack.1), channel_id=1, source_target_pairs={{16,0},{17,1},{18,2},{19,3},{20,4},{21,5},{22,6},{23,7},{0,8},{1,9... | collective-permute-start | bytes 331784 | tf_op jit(solution)/shard_map/ppermute | solution.py:277
  55.0 1.9 %collective-permute-start = (bf16[48,1152]{1,0:T(8,128)(2,1)S(1)}, bf16[48,1152]{1,0:T(8,128)(2,1)S(1)}, u32[]{:S(2)}, u32[]{:S(2)}) collective-permute-start(bf16[48,1152]{1,0:T(8,128)(2,1)S(1)} %unpack.1), channel_id=1, source_target_pairs={{8,0},{9,1},{10,2},{11,3},{12,4},{13,5},{14,6},{15,7},{16,8},{17,9... | collective-permute-start | bytes 331784 | tf_op jit(solution)/shard_map/ppermute | solution.py:277
  57.0 3.4 %correlate.1 = bf16[32,32,128]{2,1,0:T(8,128)(2,1)} custom-call(f32[32,80,128]{2,1,0:T(8,128)S(1)} %convert_element_type.7.x_ref, bf16[512,256]{1,0:T(8,128)(2,1)S(1)} %copy-done, f32[128,128]{1,0:T(8,128)S(1)} %copy-done.1), custom_call_target="tpu_custom_call" | custom-call | flops 1207959552 | bytes 1638400 | tf_op jit(solution)/shard_map/correlate/pallas_call | solution.py:239
  60.4 0.0 collective-permute-done.1
  60.4 0.5 collective-permute-done
  61.0 4.4 %collective-permute-start.2 = (bf16[3,48,1152]{2,1,0:T(8,128)(2,1)S(1)}, bf16[3,48,1152]{2,1,0:T(8,128)(2,1)S(1)}, u32[]{:S(2)}, u32[]{:S(2)}) collective-permute-start(bf16[3,48,1152]{2,1,0:T(8,128)(2,1)S(1)} %pad_maximum_fusion.refs_0_), channel_id=1, source_target_pairs={{2,0},{3,1},{4,2},{5,3},{6,4},{7,5},{0,6},{1,7},{10,8},{11,9},{12,... | collective-permute-start | bytes 995336 | tf_op jit(solution)/shard_map/ppermute | solution.py:277
  65.4 7.5 %all-to-all-start.1 = ((bf16[32,32,128]{2,1,0:T(8,128)(2,1)}), bf16[32,32,128]{2,1,0:T(8,128)(2,1)S(1)}, u32[]{:S(2)}, u32[]{:S(2)}) async-start(bf16[32,32,128]{2,1,0:T(8,128)(2,1)} %correlate.1), calls=%async_computation.1 | async-start | bytes 524288 | tf_op jit(solution)/shard_map/all_to_all | solution.py:295
  72.8 1.9 %collective-permute-start.3 = (bf16[3,48,1152]{2,1,0:T(8,128)(2,1)S(1)}, bf16[3,48,1152]{2,1,0:T(8,128)(2,1)S(1)}, u32[]{:S(2)}, u32[]{:S(2)}) collective-permute-start(bf16[3,48,1152]{2,1,0:T(8,128)(2,1)S(1)} %pad_maximum_fusion.refs_0_), channel_id=1, source_target_pairs={{6,0},{7,1},{0,2},{1,3},{2,4},{3,5},{4,6},{5,7},{14,8},{15,9},{8,1... | collective-permute-start | bytes 995336 | tf_op jit(solution)/shard_map/ppermute | solution.py:277
  74.8 4.6 %collective-permute-start.4 = (bf16[3,48,1152]{2,1,0:T(8,128)(2,1)S(1)}, bf16[3,48,1152]{2,1,0:T(8,128)(2,1)S(1)}, u32[]{:S(2)}, u32[]{:S(2)}) collective-permute-start(bf16[3,48,1152]{2,1,0:T(8,128)(2,1)S(1)} %collective-permute-done.2.refs_1_), channel_id=1, source_target_pairs={{2,0},{3,1},{4,2},{5,3},{6,4},{7,5},{0,6},{1,7},{10,8},{11,9},{12,... | collective-permute-start | bytes 995336 | tf_op jit(solution)/shard_map/ppermute | solution.py:277
  79.4 5.8 %collective-permute-start.5 = (bf16[3,48,1152]{2,1,0:T(8,128)(2,1)S(1)}, bf16[3,48,1152]{2,1,0:T(8,128)(2,1)S(1)}, u32[]{:S(2)}, u32[]{:S(2)}) collective-permute-start(bf16[3,48,1152]{2,1,0:T(8,128)(2,1)S(1)} %pad_maximum_fusion.refs_0_), channel_id=1, source_target_pairs={{1,0},{0,1},{3,2},{2,3},{5,4},{4,5},{7,6},{6,7},{9,8},{8,9},{11,10... | collective-permute-start | bytes 995336 | tf_op jit(solution)/shard_map/ppermute | solution.py:277
  85.2 3.1 %collective-permute-start.7 = (bf16[3,48,1152]{2,1,0:T(8,128)(2,1)S(1)}, bf16[3,48,1152]{2,1,0:T(8,128)(2,1)S(1)}, u32[]{:S(2)}, u32[]{:S(2)}) collective-permute-start(bf16[3,48,1152]{2,1,0:T(8,128)(2,1)S(1)} %collective-permute-done.3.refs_2_), channel_id=1, source_target_pairs={{1,0},{0,1},{3,2},{2,3},{5,4},{4,5},{7,6},{6,7},{9,8},{8,9},{11,10... | collective-permute-start | bytes 995336 | tf_op jit(solution)/shard_map/ppermute | solution.py:277
  88.3 1.9 %collective-permute-start.6 = (bf16[3,48,1152]{2,1,0:T(8,128)(2,1)S(1)}, bf16[3,48,1152]{2,1,0:T(8,128)(2,1)S(1)}, u32[]{:S(2)}, u32[]{:S(2)}) collective-permute-start(bf16[3,48,1152]{2,1,0:T(8,128)(2,1)S(1)} %collective-permute-done.2.refs_1_), channel_id=1, source_target_pairs={{1,0},{0,1},{3,2},{2,3},{5,4},{4,5},{7,6},{6,7},{9,8},{8,9},{11,10... | collective-permute-start | bytes 995336 | tf_op jit(solution)/shard_map/ppermute | solution.py:277
  90.2 0.0 collective-permute-done.4.refs_3_
  90.3 2.4 %collective-permute-start.8 = (bf16[3,48,1152]{2,1,0:T(8,128)(2,1)S(1)}, bf16[3,48,1152]{2,1,0:T(8,128)(2,1)S(1)}, u32[]{:S(2)}, u32[]{:S(2)}) collective-permute-start(bf16[3,48,1152]{2,1,0:T(8,128)(2,1)S(1)} %collective-permute-done.4.refs_3_), channel_id=1, source_target_pairs={{1,0},{0,1},{3,2},{2,3},{5,4},{4,5},{7,6},{6,7},{9,8},{8,9},{11,10... | collective-permute-start | bytes 995336 | tf_op jit(solution)/shard_map/ppermute | solution.py:277
  92.7 0.1 pad_add_fusion.place_ref
  92.8 0.0 collective-permute-done.7.refs_6_
  92.8 0.0 collective-permute-done.6.refs_5_
  92.8 1.1 %collective-permute-done.8.refs_7_ = bf16[3,48,1152]{2,1,0:T(8,128)(2,1)S(1)} collective-permute-done((bf16[3,48,1152]{2,1,0:T(8,128)(2,1)S(1)}, bf16[3,48,1152]{2,1,0:T(8,128)(2,1)S(1)}, u32[]{:S(2)}, u32[]{:S(2)}) %collective-permute-start.8) | collective-permute-done | bytes 331808 | tf_op jit(solution)/shard_map/ppermute | solution.py:277
  93.9 2.4 %screen.1 = f32[864,128]{1,0:T(8,128)} custom-call(s32[3]{0:T(128)S(1)} %pad_add_fusion.place_ref, bf16[32,32,128]{2,1,0:T(8,128)(2,1)S(1)} %all-to-all-done.1.polar_ref, bf16[3,48,1152]{2,1,0:T(8,128)(2,1)S(1)} %pad_maximum_fusion.refs_0_, bf16[3,48,1152]{2,1,0:T(8,128)(2,1)S(1)} %collective-permute-done.2.refs_1_, ...), custom_call_target="tpu_custom_call" | custom-call | tf_op jit(solution)/shard_map/screen/pallas_call | solution.py:257
  (9 shorter events, 0.1 us)
Async XLA Ops:
  39.6 17.3 %copy-start = (bf16[512,256]{1,0:T(8,128)(2,1)S(1)}, bf16[512,256]{1,0:T(8,128)(2,1)}, u32[]{:S(2)}) copy-start(bf16[512,256]{1,0:T(8,128)(2,1)} %constant.21.clone.matrices_ref) | copy-start | bytes 786436
  39.6 17.3 %copy-start.1 = (f32[128,128]{1,0:T(8,128)S(1)}, f32[128,128]{1,0:T(8,128)}, u32[]{:S(2)}) copy-start(f32[128,128]{1,0:T(8,128)} %constant.22.clone.twiddle_ref) | copy-start | bytes 196612
  40.0 20.4 %collective-permute-start.1 = (bf16[48,1152]{1,0:T(8,128)(2,1)S(1)}, bf16[48,1152]{1,0:T(8,128)(2,1)S(1)}, u32[]{:S(2)}, u32[]{:S(2)}) collective-permute-start(bf16[48,1152]{1,0:T(8,128)(2,1)S(1)} %unpack.1), channel_id=1, source_target_pairs={{16,0},{17,1},{18,2},{19,3},{20,4},{21,5},{22,6},{23,7},{0,8},{1,9... | collective-permute-start | bytes 331784 | tf_op jit(solution)/shard_map/ppermute | solution.py:277
  55.0 5.9 %collective-permute-start = (bf16[48,1152]{1,0:T(8,128)(2,1)S(1)}, bf16[48,1152]{1,0:T(8,128)(2,1)S(1)}, u32[]{:S(2)}, u32[]{:S(2)}) collective-permute-start(bf16[48,1152]{1,0:T(8,128)(2,1)S(1)} %unpack.1), channel_id=1, source_target_pairs={{8,0},{9,1},{10,2},{11,3},{12,4},{13,5},{14,6},{15,7},{16,8},{17,9... | collective-permute-start | bytes 331784 | tf_op jit(solution)/shard_map/ppermute | solution.py:277
  61.0 13.8 %collective-permute-start.2 = (bf16[3,48,1152]{2,1,0:T(8,128)(2,1)S(1)}, bf16[3,48,1152]{2,1,0:T(8,128)(2,1)S(1)}, u32[]{:S(2)}, u32[]{:S(2)}) collective-permute-start(bf16[3,48,1152]{2,1,0:T(8,128)(2,1)S(1)} %pad_maximum_fusion.refs_0_), channel_id=1, source_target_pairs={{2,0},{3,1},{4,2},{5,3},{6,4},{7,5},{0,6},{1,7},{10,8},{11,9},{12,... | collective-permute-start | bytes 995336 | tf_op jit(solution)/shard_map/ppermute | solution.py:277
  65.4 27.4 %all-to-all-start.1 = ((bf16[32,32,128]{2,1,0:T(8,128)(2,1)}), bf16[32,32,128]{2,1,0:T(8,128)(2,1)S(1)}, u32[]{:S(2)}, u32[]{:S(2)}) async-start(bf16[32,32,128]{2,1,0:T(8,128)(2,1)} %correlate.1), calls=%async_computation.1 | async-start | bytes 524288 | tf_op jit(solution)/shard_map/all_to_all | solution.py:295
  72.8 12.3 %collective-permute-start.3 = (bf16[3,48,1152]{2,1,0:T(8,128)(2,1)S(1)}, bf16[3,48,1152]{2,1,0:T(8,128)(2,1)S(1)}, u32[]{:S(2)}, u32[]{:S(2)}) collective-permute-start(bf16[3,48,1152]{2,1,0:T(8,128)(2,1)S(1)} %pad_maximum_fusion.refs_0_), channel_id=1, source_target_pairs={{6,0},{7,1},{0,2},{1,3},{2,4},{3,5},{4,6},{5,7},{14,8},{15,9},{8,1... | collective-permute-start | bytes 995336 | tf_op jit(solution)/shard_map/ppermute | solution.py:277
  74.8 15.5 %collective-permute-start.4 = (bf16[3,48,1152]{2,1,0:T(8,128)(2,1)S(1)}, bf16[3,48,1152]{2,1,0:T(8,128)(2,1)S(1)}, u32[]{:S(2)}, u32[]{:S(2)}) collective-permute-start(bf16[3,48,1152]{2,1,0:T(8,128)(2,1)S(1)} %collective-permute-done.2.refs_1_), channel_id=1, source_target_pairs={{2,0},{3,1},{4,2},{5,3},{6,4},{7,5},{0,6},{1,7},{10,8},{11,9},{12,... | collective-permute-start | bytes 995336 | tf_op jit(solution)/shard_map/ppermute | solution.py:277
  79.4 13.4 %collective-permute-start.5 = (bf16[3,48,1152]{2,1,0:T(8,128)(2,1)S(1)}, bf16[3,48,1152]{2,1,0:T(8,128)(2,1)S(1)}, u32[]{:S(2)}, u32[]{:S(2)}) collective-permute-start(bf16[3,48,1152]{2,1,0:T(8,128)(2,1)S(1)} %pad_maximum_fusion.refs_0_), channel_id=1, source_target_pairs={{1,0},{0,1},{3,2},{2,3},{5,4},{4,5},{7,6},{6,7},{9,8},{8,9},{11,10... | collective-permute-start | bytes 995336 | tf_op jit(solution)/shard_map/ppermute | solution.py:277
  85.2 7.6 %collective-permute-start.7 = (bf16[3,48,1152]{2,1,0:T(8,128)(2,1)S(1)}, bf16[3,48,1152]{2,1,0:T(8,128)(2,1)S(1)}, u32[]{:S(2)}, u32[]{:S(2)}) collective-permute-start(bf16[3,48,1152]{2,1,0:T(8,128)(2,1)S(1)} %collective-permute-done.3.refs_2_), channel_id=1, source_target_pairs={{1,0},{0,1},{3,2},{2,3},{5,4},{4,5},{7,6},{6,7},{9,8},{8,9},{11,10... | collective-permute-start | bytes 995336 | tf_op jit(solution)/shard_map/ppermute | solution.py:277
  88.3 4.5 %collective-permute-start.6 = (bf16[3,48,1152]{2,1,0:T(8,128)(2,1)S(1)}, bf16[3,48,1152]{2,1,0:T(8,128)(2,1)S(1)}, u32[]{:S(2)}, u32[]{:S(2)}) collective-permute-start(bf16[3,48,1152]{2,1,0:T(8,128)(2,1)S(1)} %collective-permute-done.2.refs_1_), channel_id=1, source_target_pairs={{1,0},{0,1},{3,2},{2,3},{5,4},{4,5},{7,6},{6,7},{9,8},{8,9},{11,10... | collective-permute-start | bytes 995336 | tf_op jit(solution)/shard_map/ppermute | solution.py:277
  90.3 3.7 %collective-permute-start.8 = (bf16[3,48,1152]{2,1,0:T(8,128)(2,1)S(1)}, bf16[3,48,1152]{2,1,0:T(8,128)(2,1)S(1)}, u32[]{:S(2)}, u32[]{:S(2)}) collective-permute-start(bf16[3,48,1152]{2,1,0:T(8,128)(2,1)S(1)} %collective-permute-done.4.refs_3_), channel_id=1, source_target_pairs={{1,0},{0,1},{3,2},{2,3},{5,4},{4,5},{7,6},{6,7},{9,8},{8,9},{11,10... | collective-permute-start | bytes 995336 | tf_op jit(solution)/shard_map/ppermute | solution.py:277

commit v7 on v6

--- a/solution.py
+++ b/solution.py
@@ -288,7 +288,6 @@
     mine = unpack(got, wide, order)
     run = jnp.stack([mine] + [moved(mine, sharers, (hop, 0, 0)) for hop in range(1, RUN)])
     polar = correlate(got)
-    run, polar = lax.optimization_barrier((run, polar))
     ahead, behind = moved(run, sharers, (0, 1, 0)), moved(run, sharers, (0, ACROSS - 1, 0))
     runs = [run, ahead, behind, moved(ahead, sharers, (0, 1, 0))]
     runs += [moved(run, sharers, (0, 0, 1)) for run in runs]

time: 96.8 us -> 99.4 us (1.027)
  waiting for transfers between devices: 1.67 us -> 5.46 us
  starting transfers between devices: 48.5 us -> 47.3 us
    ppermute x9, waiting for transfers between devices: 1.67 us -> 5.46 us  [moved(): return lax.ppermute(x, 'col', [(source(at), at) for at in range(sharers)])]
    ppermute x9, starting transfers between devices: 41 us -> 39.9 us  [moved(): return lax.ppermute(x, 'col', [(source(at), at) for at in range(sharers)])]
  transfers between devices with their start and end apart: 10 -> 10, of which waited for: 2 -> 2; matrix products, arithmetic and copies ran while one was open for 0% -> 0% of each run, Pallas kernels for 4% -> 3%
where the time goes in v7:
time: 99.4 us; the launch traced here: 98.9 us
  starting transfers between devices  47.3 us (48%)
  blocking collectives  38.1 us (38%)
  Pallas kernels  7.51 us (8%)
  waiting for transfers between devices  5.46 us (5%)
    ppermute x9, starting transfers between devices, moved(): return lax.ppermute(x, 'col', [(source(at), at) for at in range(sharers)])  39.9 us
    all_to_all x1, blocking collectives, per_device(): lax.all_to_all(packed.astype(jnp.float16), 'energy', split_axis=0, concat...  38.1 us
    all_to_all x1, starting transfers between devices, per_device(): lax.all_to_all(polar, 'energy', split_axis=0, concat_axis=0, tiled=True)  7.47 us
    ppermute x9, waiting for transfers between devices, moved(): return lax.ppermute(x, 'col', [(source(at), at) for at in range(sharers)])  5.46 us
    pallas_call x1, Pallas kernels, correlate(): pl.pallas_call(correlate_kernel, out_shape=jax.ShapeDtypeStruct((owners,...  3.41 us
    pallas_call x1, Pallas kernels, screen(): pl.pallas_call(screen_kernel, out_shape=jax.ShapeDtypeStruct((energies *...  2.42 us
  transfers between devices with their start and end apart: 10, of which 2 were waited for; matrix products, arithmetic and copies ran while one was open for 0% of the time, Pallas kernels for 3%

profile of v7, /device:TPU:1, one launch (start us, length us, event | category | flops | bytes accessed | tf_op | source)
XLA Modules:
  0.0 98.9 jit_solution(3821116903182552160)
XLA Ops:
  0.0 1.4 %pack.1 = f32[32,80,128]{2,1,0:T(8,128)S(1)} custom-call(f32[864,128]{1,0:T(8,128)} %bitcast.24, f32[864,128]{1,0:T(8,128)} %bitcast.25, bf16[36,48]{1,0:T(8,128)(2,1)} %coulomb_hbm.1), custom_call_target="tpu_custom_call" | custom-call | tf_op jit(solution)/shard_map/pack/pallas_call | solution.py:213
  1.4 0.1 convert_element_type.6
  1.5 38.1 %all_to_all.10 = f16[32,80,128]{2,1,0:T(8,128)(2,1)S(1)} all-to-all(f16[32,80,128]{2,1,0:T(8,128)(2,1)S(1)} %convert_element_type.6), channel_id=1, replica_groups=mesh['energy'=32,'col'=24] {'energy'}, dimensions={0} | all-to-all | bytes 1310720 | tf_op jit(solution)/shard_map/all_to_all | solution.py:285
  39.6 0.1 convert_element_type.7.x_ref
  39.7 0.0 copy-start
  39.7 0.0 copy-start.1
  39.8 0.3 unpack.1
  40.0 15.0 %collective-permute-start.1 = (bf16[48,1152]{1,0:T(8,128)(2,1)S(1)}, bf16[48,1152]{1,0:T(8,128)(2,1)S(1)}, u32[]{:S(2)}, u32[]{:S(2)}) collective-permute-start(bf16[48,1152]{1,0:T(8,128)(2,1)S(1)} %unpack.1), channel_id=1, source_target_pairs={{16,0},{17,1},{18,2},{19,3},{20,4},{21,5},{22,6},{23,7},{0,8},{1,9... | collective-permute-start | bytes 331784 | tf_op jit(solution)/shard_map/ppermute | solution.py:277
  55.0 1.9 %collective-permute-start = (bf16[48,1152]{1,0:T(8,128)(2,1)S(1)}, bf16[48,1152]{1,0:T(8,128)(2,1)S(1)}, u32[]{:S(2)}, u32[]{:S(2)}) collective-permute-start(bf16[48,1152]{1,0:T(8,128)(2,1)S(1)} %unpack.1), channel_id=1, source_target_pairs={{8,0},{9,1},{10,2},{11,3},{12,4},{13,5},{14,6},{15,7},{16,8},{17,9... | collective-permute-start | bytes 331784 | tf_op jit(solution)/shard_map/ppermute | solution.py:277
  57.0 4.0 %collective-permute-done = bf16[48,1152]{1,0:T(8,128)(2,1)S(1)} collective-permute-done((bf16[48,1152]{1,0:T(8,128)(2,1)S(1)}, bf16[48,1152]{1,0:T(8,128)(2,1)S(1)}, u32[]{:S(2)}, u32[]{:S(2)}) %collective-permute-start) | collective-permute-done | bytes 110624 | tf_op jit(solution)/shard_map/ppermute | solution.py:277
  61.0 4.4 %collective-permute-start.2 = (bf16[3,48,1152]{2,1,0:T(8,128)(2,1)S(1)}, bf16[3,48,1152]{2,1,0:T(8,128)(2,1)S(1)}, u32[]{:S(2)}, u32[]{:S(2)}) collective-permute-start(bf16[3,48,1152]{2,1,0:T(8,128)(2,1)S(1)} %pad_maximum_fusion.refs_0_), channel_id=1, source_target_pairs={{2,0},{3,1},{4,2},{5,3},{6,4},{7,5},{0,6},{1,7},{10,8},{11,9},{12,... | collective-permute-start | bytes 995336 | tf_op jit(solution)/shard_map/ppermute | solution.py:277
  65.4 3.4 %correlate.1 = bf16[32,32,128]{2,1,0:T(8,128)(2,1)} custom-call(f32[32,80,128]{2,1,0:T(8,128)S(1)} %convert_element_type.7.x_ref, bf16[512,256]{1,0:T(8,128)(2,1)S(1)} %copy-done, f32[128,128]{1,0:T(8,128)S(1)} %copy-done.1), custom_call_target="tpu_custom_call" | custom-call | flops 1207959552 | bytes 1638400 | tf_op jit(solution)/shard_map/correlate/pallas_call | solution.py:239
  68.8 7.5 %all-to-all-start.1 = ((bf16[32,32,128]{2,1,0:T(8,128)(2,1)}), bf16[32,32,128]{2,1,0:T(8,128)(2,1)S(1)}, u32[]{:S(2)}, u32[]{:S(2)}) async-start(bf16[32,32,128]{2,1,0:T(8,128)(2,1)} %correlate.1), calls=%async_computation.1 | async-start | bytes 524288 | tf_op jit(solution)/shard_map/all_to_all | solution.py:294
  76.3 1.9 %collective-permute-start.3 = (bf16[3,48,1152]{2,1,0:T(8,128)(2,1)S(1)}, bf16[3,48,1152]{2,1,0:T(8,128)(2,1)S(1)}, u32[]{:S(2)}, u32[]{:S(2)}) collective-permute-start(bf16[3,48,1152]{2,1,0:T(8,128)(2,1)S(1)} %pad_maximum_fusion.refs_0_), channel_id=1, source_target_pairs={{6,0},{7,1},{0,2},{1,3},{2,4},{3,5},{4,6},{5,7},{14,8},{15,9},{8,1... | collective-permute-start | bytes 995336 | tf_op jit(solution)/shard_map/ppermute | solution.py:277
  78.2 0.0 collective-permute-done.2.refs_1_
  78.2 4.6 %collective-permute-start.4 = (bf16[3,48,1152]{2,1,0:T(8,128)(2,1)S(1)}, bf16[3,48,1152]{2,1,0:T(8,128)(2,1)S(1)}, u32[]{:S(2)}, u32[]{:S(2)}) collective-permute-start(bf16[3,48,1152]{2,1,0:T(8,128)(2,1)S(1)} %collective-permute-done.2.refs_1_), channel_id=1, source_target_pairs={{2,0},{3,1},{4,2},{5,3},{6,4},{7,5},{0,6},{1,7},{10,8},{11,9},{12,... | collective-permute-start | bytes 995336 | tf_op jit(solution)/shard_map/ppermute | solution.py:277
  82.8 5.8 %collective-permute-start.5 = (bf16[3,48,1152]{2,1,0:T(8,128)(2,1)S(1)}, bf16[3,48,1152]{2,1,0:T(8,128)(2,1)S(1)}, u32[]{:S(2)}, u32[]{:S(2)}) collective-permute-start(bf16[3,48,1152]{2,1,0:T(8,128)(2,1)S(1)} %pad_maximum_fusion.refs_0_), channel_id=1, source_target_pairs={{1,0},{0,1},{3,2},{2,3},{5,4},{4,5},{7,6},{6,7},{9,8},{8,9},{11,10... | collective-permute-start | bytes 995336 | tf_op jit(solution)/shard_map/ppermute | solution.py:277
  88.6 1.9 %collective-permute-start.6 = (bf16[3,48,1152]{2,1,0:T(8,128)(2,1)S(1)}, bf16[3,48,1152]{2,1,0:T(8,128)(2,1)S(1)}, u32[]{:S(2)}, u32[]{:S(2)}) collective-permute-start(bf16[3,48,1152]{2,1,0:T(8,128)(2,1)S(1)} %collective-permute-done.2.refs_1_), channel_id=1, source_target_pairs={{1,0},{0,1},{3,2},{2,3},{5,4},{4,5},{7,6},{6,7},{9,8},{8,9},{11,10... | collective-permute-start | bytes 995336 | tf_op jit(solution)/shard_map/ppermute | solution.py:277
  90.6 2.4 %collective-permute-start.7 = (bf16[3,48,1152]{2,1,0:T(8,128)(2,1)S(1)}, bf16[3,48,1152]{2,1,0:T(8,128)(2,1)S(1)}, u32[]{:S(2)}, u32[]{:S(2)}) collective-permute-start(bf16[3,48,1152]{2,1,0:T(8,128)(2,1)S(1)} %collective-permute-done.3.refs_2_), channel_id=1, source_target_pairs={{1,0},{0,1},{3,2},{2,3},{5,4},{4,5},{7,6},{6,7},{9,8},{8,9},{11,10... | collective-permute-start | bytes 995336 | tf_op jit(solution)/shard_map/ppermute | solution.py:277
  93.0 0.0 collective-permute-done.4.refs_3_
  93.0 1.9 %collective-permute-start.8 = (bf16[3,48,1152]{2,1,0:T(8,128)(2,1)S(1)}, bf16[3,48,1152]{2,1,0:T(8,128)(2,1)S(1)}, u32[]{:S(2)}, u32[]{:S(2)}) collective-permute-start(bf16[3,48,1152]{2,1,0:T(8,128)(2,1)S(1)} %collective-permute-done.4.refs_3_), channel_id=1, source_target_pairs={{1,0},{0,1},{3,2},{2,3},{5,4},{4,5},{7,6},{6,7},{9,8},{8,9},{11,10... | collective-permute-start | bytes 995336 | tf_op jit(solution)/shard_map/ppermute | solution.py:277
  94.9 0.1 pad_add_fusion.place_ref
  95.1 1.5 %collective-permute-done.8.refs_7_ = bf16[3,48,1152]{2,1,0:T(8,128)(2,1)S(1)} collective-permute-done((bf16[3,48,1152]{2,1,0:T(8,128)(2,1)S(1)}, bf16[3,48,1152]{2,1,0:T(8,128)(2,1)S(1)}, u32[]{:S(2)}, u32[]{:S(2)}) %collective-permute-start.8) | collective-permute-done | bytes 331808 | tf_op jit(solution)/shard_map/ppermute | solution.py:277
  96.5 2.4 %screen.1 = f32[864,128]{1,0:T(8,128)} custom-call(s32[3]{0:T(128)S(1)} %pad_add_fusion.place_ref, bf16[32,32,128]{2,1,0:T(8,128)(2,1)S(1)} %all-to-all-done.1.polar_ref, bf16[3,48,1152]{2,1,0:T(8,128)(2,1)S(1)} %pad_maximum_fusion.refs_0_, bf16[3,48,1152]{2,1,0:T(8,128)(2,1)S(1)} %collective-permute-done.2.refs_1_, ...), custom_call_target="tpu_custom_call" | custom-call | tf_op jit(solution)/shard_map/screen/pallas_call | solution.py:257
  (9 shorter events, 0.1 us)
Async XLA Ops:
  39.7 25.7 %copy-start = (bf16[512,256]{1,0:T(8,128)(2,1)S(1)}, bf16[512,256]{1,0:T(8,128)(2,1)}, u32[]{:S(2)}) copy-start(bf16[512,256]{1,0:T(8,128)(2,1)} %constant.21.clone.matrices_ref) | copy-start | bytes 786436
  39.7 25.6 %copy-start.1 = (f32[128,128]{1,0:T(8,128)S(1)}, f32[128,128]{1,0:T(8,128)}, u32[]{:S(2)}) copy-start(f32[128,128]{1,0:T(8,128)} %constant.22.clone.twiddle_ref) | copy-start | bytes 196612
  40.0 17.0 %collective-permute-start.1 = (bf16[48,1152]{1,0:T(8,128)(2,1)S(1)}, bf16[48,1152]{1,0:T(8,128)(2,1)S(1)}, u32[]{:S(2)}, u32[]{:S(2)}) collective-permute-start(bf16[48,1152]{1,0:T(8,128)(2,1)S(1)} %unpack.1), channel_id=1, source_target_pairs={{16,0},{17,1},{18,2},{19,3},{20,4},{21,5},{22,6},{23,7},{0,8},{1,9... | collective-permute-start | bytes 331784 | tf_op jit(solution)/shard_map/ppermute | solution.py:277
  55.0 5.9 %collective-permute-start = (bf16[48,1152]{1,0:T(8,128)(2,1)S(1)}, bf16[48,1152]{1,0:T(8,128)(2,1)S(1)}, u32[]{:S(2)}, u32[]{:S(2)}) collective-permute-start(bf16[48,1152]{1,0:T(8,128)(2,1)S(1)} %unpack.1), channel_id=1, source_target_pairs={{8,0},{9,1},{10,2},{11,3},{12,4},{13,5},{14,6},{15,7},{16,8},{17,9... | collective-permute-start | bytes 331784 | tf_op jit(solution)/shard_map/ppermute | solution.py:277
  61.0 17.2 %collective-permute-start.2 = (bf16[3,48,1152]{2,1,0:T(8,128)(2,1)S(1)}, bf16[3,48,1152]{2,1,0:T(8,128)(2,1)S(1)}, u32[]{:S(2)}, u32[]{:S(2)}) collective-permute-start(bf16[3,48,1152]{2,1,0:T(8,128)(2,1)S(1)} %pad_maximum_fusion.refs_0_), channel_id=1, source_target_pairs={{2,0},{3,1},{4,2},{5,3},{6,4},{7,5},{0,6},{1,7},{10,8},{11,9},{12,... | collective-permute-start | bytes 995336 | tf_op jit(solution)/shard_map/ppermute | solution.py:277
  68.8 26.2 %all-to-all-start.1 = ((bf16[32,32,128]{2,1,0:T(8,128)(2,1)}), bf16[32,32,128]{2,1,0:T(8,128)(2,1)S(1)}, u32[]{:S(2)}, u32[]{:S(2)}) async-start(bf16[32,32,128]{2,1,0:T(8,128)(2,1)} %correlate.1), calls=%async_computation.1 | async-start | bytes 524288 | tf_op jit(solution)/shard_map/all_to_all | solution.py:294
  76.3 14.3 %collective-permute-start.3 = (bf16[3,48,1152]{2,1,0:T(8,128)(2,1)S(1)}, bf16[3,48,1152]{2,1,0:T(8,128)(2,1)S(1)}, u32[]{:S(2)}, u32[]{:S(2)}) collective-permute-start(bf16[3,48,1152]{2,1,0:T(8,128)(2,1)S(1)} %pad_maximum_fusion.refs_0_), channel_id=1, source_target_pairs={{6,0},{7,1},{0,2},{1,3},{2,4},{3,5},{4,6},{5,7},{14,8},{15,9},{8,1... | collective-permute-start | bytes 995336 | tf_op jit(solution)/shard_map/ppermute | solution.py:277
  78.2 14.8 %collective-permute-start.4 = (bf16[3,48,1152]{2,1,0:T(8,128)(2,1)S(1)}, bf16[3,48,1152]{2,1,0:T(8,128)(2,1)S(1)}, u32[]{:S(2)}, u32[]{:S(2)}) collective-permute-start(bf16[3,48,1152]{2,1,0:T(8,128)(2,1)S(1)} %collective-permute-done.2.refs_1_), channel_id=1, source_target_pairs={{2,0},{3,1},{4,2},{5,3},{6,4},{7,5},{0,6},{1,7},{10,8},{11,9},{12,... | collective-permute-start | bytes 995336 | tf_op jit(solution)/shard_map/ppermute | solution.py:277
  82.8 12.2 %collective-permute-start.5 = (bf16[3,48,1152]{2,1,0:T(8,128)(2,1)S(1)}, bf16[3,48,1152]{2,1,0:T(8,128)(2,1)S(1)}, u32[]{:S(2)}, u32[]{:S(2)}) collective-permute-start(bf16[3,48,1152]{2,1,0:T(8,128)(2,1)S(1)} %pad_maximum_fusion.refs_0_), channel_id=1, source_target_pairs={{1,0},{0,1},{3,2},{2,3},{5,4},{4,5},{7,6},{6,7},{9,8},{8,9},{11,10... | collective-permute-start | bytes 995336 | tf_op jit(solution)/shard_map/ppermute | solution.py:277
  88.6 6.4 %collective-permute-start.6 = (bf16[3,48,1152]{2,1,0:T(8,128)(2,1)S(1)}, bf16[3,48,1152]{2,1,0:T(8,128)(2,1)S(1)}, u32[]{:S(2)}, u32[]{:S(2)}) collective-permute-start(bf16[3,48,1152]{2,1,0:T(8,128)(2,1)S(1)} %collective-permute-done.2.refs_1_), channel_id=1, source_target_pairs={{1,0},{0,1},{3,2},{2,3},{5,4},{4,5},{7,6},{6,7},{9,8},{8,9},{11,10... | collective-permute-start | bytes 995336 | tf_op jit(solution)/shard_map/ppermute | solution.py:277
  90.6 4.5 %collective-permute-start.7 = (bf16[3,48,1152]{2,1,0:T(8,128)(2,1)S(1)}, bf16[3,48,1152]{2,1,0:T(8,128)(2,1)S(1)}, u32[]{:S(2)}, u32[]{:S(2)}) collective-permute-start(bf16[3,48,1152]{2,1,0:T(8,128)(2,1)S(1)} %collective-permute-done.3.refs_2_), channel_id=1, source_target_pairs={{1,0},{0,1},{3,2},{2,3},{5,4},{4,5},{7,6},{6,7},{9,8},{8,9},{11,10... | collective-permute-start | bytes 995336 | tf_op jit(solution)/shard_map/ppermute | solution.py:277
  93.0 3.5 %collective-permute-start.8 = (bf16[3,48,1152]{2,1,0:T(8,128)(2,1)S(1)}, bf16[3,48,1152]{2,1,0:T(8,128)(2,1)S(1)}, u32[]{:S(2)}, u32[]{:S(2)}) collective-permute-start(bf16[3,48,1152]{2,1,0:T(8,128)(2,1)S(1)} %collective-permute-done.4.refs_3_), channel_id=1, source_target_pairs={{1,0},{0,1},{3,2},{2,3},{5,4},{4,5},{7,6},{6,7},{9,8},{8,9},{11,10... | collective-permute-start | bytes 995336 | tf_op jit(solution)/shard_map/ppermute | solution.py:277

commit v8 on v6

--- a/solution.py
+++ b/solution.py
@@ -290,7 +290,7 @@
     polar = correlate(got)
     run, polar = lax.optimization_barrier((run, polar))
     ahead, behind = moved(run, sharers, (0, 1, 0)), moved(run, sharers, (0, ACROSS - 1, 0))
-    runs = [run, ahead, behind, moved(ahead, sharers, (0, 1, 0))]
+    runs = [run, ahead, behind, moved(behind, sharers, (0, ACROSS - 1, 0))]
     runs += [moved(run, sharers, (0, 0, 1)) for run in runs]
     polar = lax.all_to_all(polar, "energy", split_axis=0, concat_axis=0, tiled=True)
     at = lax.axis_index("col")

time: 96.8 us -> 94.9 us (0.980)
  starting transfers between devices: 48.5 us -> 46.6 us
    ppermute x9, starting transfers between devices: 41 us -> 39.1 us  [moved(): return lax.ppermute(x, 'col', [(source(at), at) for at in range(sharers)])]
where the time goes in v8:
time: 94.9 us; the launch traced here: 94.4 us
  starting transfers between devices  46.6 us (49%)
  blocking collectives  38.1 us (40%)
  Pallas kernels  7.52 us (8%)
  waiting for transfers between devices  1.67 us (2%)
    ppermute x9, starting transfers between devices, moved(): return lax.ppermute(x, 'col', [(source(at), at) for at in range(sharers)])  39.1 us
    all_to_all x1, blocking collectives, per_device(): lax.all_to_all(packed.astype(jnp.float16), 'energy', split_axis=0, concat...  38.1 us
    all_to_all x1, starting transfers between devices, per_device(): lax.all_to_all(polar, 'energy', split_axis=0, concat_axis=0, tiled=True)  7.48 us
    pallas_call x1, Pallas kernels, correlate(): pl.pallas_call(correlate_kernel, out_shape=jax.ShapeDtypeStruct((owners,...  3.42 us
    pallas_call x1, Pallas kernels, screen(): pl.pallas_call(screen_kernel, out_shape=jax.ShapeDtypeStruct((energies *...  2.42 us
  transfers between devices with their start and end apart: 10, of which 2 were waited for; matrix products, arithmetic and copies ran while one was open for 0% of the time, Pallas kernels for 4%

profile of v8, /device:TPU:1, one launch (start us, length us, event | category | flops | bytes accessed | tf_op | source)
XLA Modules:
  0.0 94.4 jit_solution(1314812760299345589)
XLA Ops:
  0.0 1.4 %pack.1 = f32[32,80,128]{2,1,0:T(8,128)S(1)} custom-call(f32[864,128]{1,0:T(8,128)} %bitcast.24, f32[864,128]{1,0:T(8,128)} %bitcast.25, bf16[36,48]{1,0:T(8,128)(2,1)} %coulomb_hbm.1), custom_call_target="tpu_custom_call" | custom-call | tf_op jit(solution)/shard_map/pack/pallas_call | solution.py:213
  1.4 0.1 convert_element_type.6
  1.5 38.1 %all_to_all.10 = f16[32,80,128]{2,1,0:T(8,128)(2,1)S(1)} all-to-all(f16[32,80,128]{2,1,0:T(8,128)(2,1)S(1)} %convert_element_type.6), channel_id=1, replica_groups=mesh['energy'=32,'col'=24] {'energy'}, dimensions={0} | all-to-all | bytes 1310720 | tf_op jit(solution)/shard_map/all_to_all | solution.py:285
  39.6 0.1 convert_element_type.7.x_ref
  39.7 0.3 unpack.1
  40.0 15.0 %collective-permute-start.1 = (bf16[48,1152]{1,0:T(8,128)(2,1)S(1)}, bf16[48,1152]{1,0:T(8,128)(2,1)S(1)}, u32[]{:S(2)}, u32[]{:S(2)}) collective-permute-start(bf16[48,1152]{1,0:T(8,128)(2,1)S(1)} %unpack.1), channel_id=1, source_target_pairs={{16,0},{17,1},{18,2},{19,3},{20,4},{21,5},{22,6},{23,7},{0,8},{1,9... | collective-permute-start | bytes 331784 | tf_op jit(solution)/shard_map/ppermute | solution.py:277
  55.0 1.9 %collective-permute-start = (bf16[48,1152]{1,0:T(8,128)(2,1)S(1)}, bf16[48,1152]{1,0:T(8,128)(2,1)S(1)}, u32[]{:S(2)}, u32[]{:S(2)}) collective-permute-start(bf16[48,1152]{1,0:T(8,128)(2,1)S(1)} %unpack.1), channel_id=1, source_target_pairs={{8,0},{9,1},{10,2},{11,3},{12,4},{13,5},{14,6},{15,7},{16,8},{17,9... | collective-permute-start | bytes 331784 | tf_op jit(solution)/shard_map/ppermute | solution.py:277
  57.0 3.4 %correlate.1 = bf16[32,32,128]{2,1,0:T(8,128)(2,1)} custom-call(f32[32,80,128]{2,1,0:T(8,128)S(1)} %convert_element_type.7.x_ref, bf16[512,256]{1,0:T(8,128)(2,1)S(1)} %copy-done, f32[128,128]{1,0:T(8,128)S(1)} %copy-done.1), custom_call_target="tpu_custom_call" | custom-call | flops 1207959552 | bytes 1638400 | tf_op jit(solution)/shard_map/correlate/pallas_call | solution.py:239
  60.4 0.0 collective-permute-done.1
  60.4 0.5 collective-permute-done
  61.0 3.1 %collective-permute-start.3 = (bf16[3,48,1152]{2,1,0:T(8,128)(2,1)S(1)}, bf16[3,48,1152]{2,1,0:T(8,128)(2,1)S(1)}, u32[]{:S(2)}, u32[]{:S(2)}) collective-permute-start(bf16[3,48,1152]{2,1,0:T(8,128)(2,1)S(1)} %pad_maximum_fusion.refs_0_), channel_id=1, source_target_pairs={{6,0},{7,1},{0,2},{1,3},{2,4},{3,5},{4,6},{5,7},{14,8},{15,9},{8,1... | collective-permute-start | bytes 995336 | tf_op jit(solution)/shard_map/ppermute | solution.py:277
  64.1 7.5 %all-to-all-start.1 = ((bf16[32,32,128]{2,1,0:T(8,128)(2,1)}), bf16[32,32,128]{2,1,0:T(8,128)(2,1)S(1)}, u32[]{:S(2)}, u32[]{:S(2)}) async-start(bf16[32,32,128]{2,1,0:T(8,128)(2,1)} %correlate.1), calls=%async_computation.1 | async-start | bytes 524288 | tf_op jit(solution)/shard_map/all_to_all | solution.py:295
  71.6 3.4 %collective-permute-start.2 = (bf16[3,48,1152]{2,1,0:T(8,128)(2,1)S(1)}, bf16[3,48,1152]{2,1,0:T(8,128)(2,1)S(1)}, u32[]{:S(2)}, u32[]{:S(2)}) collective-permute-start(bf16[3,48,1152]{2,1,0:T(8,128)(2,1)S(1)} %pad_maximum_fusion.refs_0_), channel_id=1, source_target_pairs={{2,0},{3,1},{4,2},{5,3},{6,4},{7,5},{0,6},{1,7},{10,8},{11,9},{12,... | collective-permute-start | bytes 995336 | tf_op jit(solution)/shard_map/ppermute | solution.py:277
  75.0 0.0 collective-permute-done.3.refs_2_
  75.0 1.9 %collective-permute-start.4 = (bf16[3,48,1152]{2,1,0:T(8,128)(2,1)S(1)}, bf16[3,48,1152]{2,1,0:T(8,128)(2,1)S(1)}, u32[]{:S(2)}, u32[]{:S(2)}) collective-permute-start(bf16[3,48,1152]{2,1,0:T(8,128)(2,1)S(1)} %collective-permute-done.3.refs_2_), channel_id=1, source_target_pairs={{6,0},{7,1},{0,2},{1,3},{2,4},{3,5},{4,6},{5,7},{14,8},{15,9},{8,1... | collective-permute-start | bytes 995336 | tf_op jit(solution)/shard_map/ppermute | solution.py:277
  76.9 5.8 %collective-permute-start.5 = (bf16[3,48,1152]{2,1,0:T(8,128)(2,1)S(1)}, bf16[3,48,1152]{2,1,0:T(8,128)(2,1)S(1)}, u32[]{:S(2)}, u32[]{:S(2)}) collective-permute-start(bf16[3,48,1152]{2,1,0:T(8,128)(2,1)S(1)} %pad_maximum_fusion.refs_0_), channel_id=1, source_target_pairs={{1,0},{0,1},{3,2},{2,3},{5,4},{4,5},{7,6},{6,7},{9,8},{8,9},{11,10... | collective-permute-start | bytes 995336 | tf_op jit(solution)/shard_map/ppermute | solution.py:277
  82.7 1.9 %collective-permute-start.7 = (bf16[3,48,1152]{2,1,0:T(8,128)(2,1)S(1)}, bf16[3,48,1152]{2,1,0:T(8,128)(2,1)S(1)}, u32[]{:S(2)}, u32[]{:S(2)}) collective-permute-start(bf16[3,48,1152]{2,1,0:T(8,128)(2,1)S(1)} %collective-permute-done.3.refs_2_), channel_id=1, source_target_pairs={{1,0},{0,1},{3,2},{2,3},{5,4},{4,5},{7,6},{6,7},{9,8},{8,9},{11,10... | collective-permute-start | bytes 995336 | tf_op jit(solution)/shard_map/ppermute | solution.py:277
  84.6 2.4 %collective-permute-start.6 = (bf16[3,48,1152]{2,1,0:T(8,128)(2,1)S(1)}, bf16[3,48,1152]{2,1,0:T(8,128)(2,1)S(1)}, u32[]{:S(2)}, u32[]{:S(2)}) collective-permute-start(bf16[3,48,1152]{2,1,0:T(8,128)(2,1)S(1)} %collective-permute-done.2.refs_1_), channel_id=1, source_target_pairs={{1,0},{0,1},{3,2},{2,3},{5,4},{4,5},{7,6},{6,7},{9,8},{8,9},{11,10... | collective-permute-start | bytes 995336 | tf_op jit(solution)/shard_map/ppermute | solution.py:277
  87.1 3.6 %collective-permute-start.8 = (bf16[3,48,1152]{2,1,0:T(8,128)(2,1)S(1)}, bf16[3,48,1152]{2,1,0:T(8,128)(2,1)S(1)}, u32[]{:S(2)}, u32[]{:S(2)}) collective-permute-start(bf16[3,48,1152]{2,1,0:T(8,128)(2,1)S(1)} %collective-permute-done.4.refs_3_), channel_id=1, source_target_pairs={{1,0},{0,1},{3,2},{2,3},{5,4},{4,5},{7,6},{6,7},{9,8},{8,9},{11,10... | collective-permute-start | bytes 995336 | tf_op jit(solution)/shard_map/ppermute | solution.py:277
  90.7 0.1 pad_add_fusion.place_ref
  90.8 0.0 collective-permute-done.5.refs_4_
  90.8 0.0 collective-permute-done.7.refs_6_
  90.9 1.1 %collective-permute-done.8.refs_7_ = bf16[3,48,1152]{2,1,0:T(8,128)(2,1)S(1)} collective-permute-done((bf16[3,48,1152]{2,1,0:T(8,128)(2,1)S(1)}, bf16[3,48,1152]{2,1,0:T(8,128)(2,1)S(1)}, u32[]{:S(2)}, u32[]{:S(2)}) %collective-permute-start.8) | collective-permute-done | bytes 331808 | tf_op jit(solution)/shard_map/ppermute | solution.py:277
  92.0 2.4 %screen.1 = f32[864,128]{1,0:T(8,128)} custom-call(s32[3]{0:T(128)S(1)} %pad_add_fusion.place_ref, bf16[32,32,128]{2,1,0:T(8,128)(2,1)S(1)} %all-to-all-done.1.polar_ref, bf16[3,48,1152]{2,1,0:T(8,128)(2,1)S(1)} %pad_maximum_fusion.refs_0_, bf16[3,48,1152]{2,1,0:T(8,128)(2,1)S(1)} %collective-permute-done.2.refs_1_, ...), custom_call_target="tpu_custom_call" | custom-call | tf_op jit(solution)/shard_map/screen/pallas_call | solution.py:257
  (9 shorter events, 0.1 us)
Async XLA Ops:
  39.6 17.3 %copy-start = (bf16[512,256]{1,0:T(8,128)(2,1)S(1)}, bf16[512,256]{1,0:T(8,128)(2,1)}, u32[]{:S(2)}) copy-start(bf16[512,256]{1,0:T(8,128)(2,1)} %constant.21.clone.matrices_ref) | copy-start | bytes 786436
  39.6 17.3 %copy-start.1 = (f32[128,128]{1,0:T(8,128)S(1)}, f32[128,128]{1,0:T(8,128)}, u32[]{:S(2)}) copy-start(f32[128,128]{1,0:T(8,128)} %constant.22.clone.twiddle_ref) | copy-start | bytes 196612
  40.0 20.4 %collective-permute-start.1 = (bf16[48,1152]{1,0:T(8,128)(2,1)S(1)}, bf16[48,1152]{1,0:T(8,128)(2,1)S(1)}, u32[]{:S(2)}, u32[]{:S(2)}) collective-permute-start(bf16[48,1152]{1,0:T(8,128)(2,1)S(1)} %unpack.1), channel_id=1, source_target_pairs={{16,0},{17,1},{18,2},{19,3},{20,4},{21,5},{22,6},{23,7},{0,8},{1,9... | collective-permute-start | bytes 331784 | tf_op jit(solution)/shard_map/ppermute | solution.py:277
  55.0 5.9 %collective-permute-start = (bf16[48,1152]{1,0:T(8,128)(2,1)S(1)}, bf16[48,1152]{1,0:T(8,128)(2,1)S(1)}, u32[]{:S(2)}, u32[]{:S(2)}) collective-permute-start(bf16[48,1152]{1,0:T(8,128)(2,1)S(1)} %unpack.1), channel_id=1, source_target_pairs={{8,0},{9,1},{10,2},{11,3},{12,4},{13,5},{14,6},{15,7},{16,8},{17,9... | collective-permute-start | bytes 331784 | tf_op jit(solution)/shard_map/ppermute | solution.py:277
  61.0 14.0 %collective-permute-start.3 = (bf16[3,48,1152]{2,1,0:T(8,128)(2,1)S(1)}, bf16[3,48,1152]{2,1,0:T(8,128)(2,1)S(1)}, u32[]{:S(2)}, u32[]{:S(2)}) collective-permute-start(bf16[3,48,1152]{2,1,0:T(8,128)(2,1)S(1)} %pad_maximum_fusion.refs_0_), channel_id=1, source_target_pairs={{6,0},{7,1},{0,2},{1,3},{2,4},{3,5},{4,6},{5,7},{14,8},{15,9},{8,1... | collective-permute-start | bytes 995336 | tf_op jit(solution)/shard_map/ppermute | solution.py:277
  64.1 26.8 %all-to-all-start.1 = ((bf16[32,32,128]{2,1,0:T(8,128)(2,1)}), bf16[32,32,128]{2,1,0:T(8,128)(2,1)S(1)}, u32[]{:S(2)}, u32[]{:S(2)}) async-start(bf16[32,32,128]{2,1,0:T(8,128)(2,1)} %correlate.1), calls=%async_computation.1 | async-start | bytes 524288 | tf_op jit(solution)/shard_map/all_to_all | solution.py:295
  71.6 13.1 %collective-permute-start.2 = (bf16[3,48,1152]{2,1,0:T(8,128)(2,1)S(1)}, bf16[3,48,1152]{2,1,0:T(8,128)(2,1)S(1)}, u32[]{:S(2)}, u32[]{:S(2)}) collective-permute-start(bf16[3,48,1152]{2,1,0:T(8,128)(2,1)S(1)} %pad_maximum_fusion.refs_0_), channel_id=1, source_target_pairs={{2,0},{3,1},{4,2},{5,3},{6,4},{7,5},{0,6},{1,7},{10,8},{11,9},{12,... | collective-permute-start | bytes 995336 | tf_op jit(solution)/shard_map/ppermute | solution.py:277
  75.0 12.1 %collective-permute-start.4 = (bf16[3,48,1152]{2,1,0:T(8,128)(2,1)S(1)}, bf16[3,48,1152]{2,1,0:T(8,128)(2,1)S(1)}, u32[]{:S(2)}, u32[]{:S(2)}) collective-permute-start(bf16[3,48,1152]{2,1,0:T(8,128)(2,1)S(1)} %collective-permute-done.3.refs_2_), channel_id=1, source_target_pairs={{6,0},{7,1},{0,2},{1,3},{2,4},{3,5},{4,6},{5,7},{14,8},{15,9},{8,1... | collective-permute-start | bytes 995336 | tf_op jit(solution)/shard_map/ppermute | solution.py:277
  76.9 13.9 %collective-permute-start.5 = (bf16[3,48,1152]{2,1,0:T(8,128)(2,1)S(1)}, bf16[3,48,1152]{2,1,0:T(8,128)(2,1)S(1)}, u32[]{:S(2)}, u32[]{:S(2)}) collective-permute-start(bf16[3,48,1152]{2,1,0:T(8,128)(2,1)S(1)} %pad_maximum_fusion.refs_0_), channel_id=1, source_target_pairs={{1,0},{0,1},{3,2},{2,3},{5,4},{4,5},{7,6},{6,7},{9,8},{8,9},{11,10... | collective-permute-start | bytes 995336 | tf_op jit(solution)/shard_map/ppermute | solution.py:277
  82.7 8.1 %collective-permute-start.7 = (bf16[3,48,1152]{2,1,0:T(8,128)(2,1)S(1)}, bf16[3,48,1152]{2,1,0:T(8,128)(2,1)S(1)}, u32[]{:S(2)}, u32[]{:S(2)}) collective-permute-start(bf16[3,48,1152]{2,1,0:T(8,128)(2,1)S(1)} %collective-permute-done.3.refs_2_), channel_id=1, source_target_pairs={{1,0},{0,1},{3,2},{2,3},{5,4},{4,5},{7,6},{6,7},{9,8},{8,9},{11,10... | collective-permute-start | bytes 995336 | tf_op jit(solution)/shard_map/ppermute | solution.py:277
  84.6 6.2 %collective-permute-start.6 = (bf16[3,48,1152]{2,1,0:T(8,128)(2,1)S(1)}, bf16[3,48,1152]{2,1,0:T(8,128)(2,1)S(1)}, u32[]{:S(2)}, u32[]{:S(2)}) collective-permute-start(bf16[3,48,1152]{2,1,0:T(8,128)(2,1)S(1)} %collective-permute-done.2.refs_1_), channel_id=1, source_target_pairs={{1,0},{0,1},{3,2},{2,3},{5,4},{4,5},{7,6},{6,7},{9,8},{8,9},{11,10... | collective-permute-start | bytes 995336 | tf_op jit(solution)/shard_map/ppermute | solution.py:277
  87.1 4.9 %collective-permute-start.8 = (bf16[3,48,1152]{2,1,0:T(8,128)(2,1)S(1)}, bf16[3,48,1152]{2,1,0:T(8,128)(2,1)S(1)}, u32[]{:S(2)}, u32[]{:S(2)}) collective-permute-start(bf16[3,48,1152]{2,1,0:T(8,128)(2,1)S(1)} %collective-permute-done.4.refs_3_), channel_id=1, source_target_pairs={{1,0},{0,1},{3,2},{2,3},{5,4},{4,5},{7,6},{6,7},{9,8},{8,9},{11,10... | collective-permute-start | bytes 995336 | tf_op jit(solution)/shard_map/ppermute | solution.py:277
